TPU v7x, 32 devices: a whole 2x2x4 slice. The times are simulated.
32 devices in a mesh: tm: 4 (over y, x), dp: 8 (over z, core).
Axes of the slice: x: 2, y: 2, z: 4, core: 2. Of those that a mesh axis runs over, the one named last changes fastest.
Arguments:
- video_clips: bfloat16 [8, 8, 16, 16, 256], P('dp', 'tm'), may hold values from -6 to 6
- cotangent: bfloat16 [8, 8, 16, 16, 256], P('dp', 'tm'), may hold values from -6 to 6
- weight: bfloat16 [3, 3, 3, 256, 256], replicated, may hold values from -0.078125 to 0.078125
- lengths: int32 [8], P('dp'), may hold values from 1 to 8, as said below
Outputs:
- conv_out: bfloat16 [8, 8, 16, 16, 256], P('dp', 'tm')
- input_grad: bfloat16 [8, 8, 16, 16, 256], P('dp', 'tm')
- weight_grad: float32 [3, 3, 3, 256, 256], P(None, None, None, 'dp')
Inputs may be any that keep to these rules, and one draw needn't show every extreme that they name: `lengths`: some clip has 8 frames and some clip has one frame.
All inputs are finite; a program needn't handle non-finite values.
Results may differ from a plain program's by a relative error of at most 0.0048.
Values may be sent and summed in bfloat16 or wider, within the bound.
No kernel may reach another device: no remote copies, remote signals or barrier semaphores. Data moves between devices by JAX's collectives and lax.ppermute only.
A program may use at most 128 MiB of HBM per device.

v0:
```python
import functools

import jax
import jax.numpy as jnp
from jax import lax
from jax.experimental import pallas as pl
from jax.experimental.pallas import tpu as pltpu
from jax.sharding import PartitionSpec as P


F32 = jnp.float32
BF16 = jnp.bfloat16
LANES = 128
VMEM = pl.BlockSpec(memory_space=pltpu.VMEM)


def call(body, outs, args, *, after=(), resident=True, scratch=(), flops=0, aliases=None):
    moved = sum(a.size * a.dtype.itemsize for a in args)
    space = pltpu.VMEM if resident else pltpu.HBM
    held = [a if a.size == 1 else pltpu.with_memory_space_constraint(a, space) for a in args]
    count = len(args)

    def with_after(*refs):
        body(*refs[:count], *refs[count + len(after) :])

    return pl.pallas_call(
        with_after,
        out_shape=tuple(outs),
        in_specs=[pl.BlockSpec(memory_space=pltpu.SMEM if a.size == 1 else space) for a in args]
        + [pl.BlockSpec(memory_space=pl.ANY)] * len(after),
        out_specs=tuple(VMEM for _ in outs),
        scratch_shapes=list(scratch),
        input_output_aliases=aliases or {},
        compiler_params=pltpu.CompilerParams(vmem_limit_bytes=32 << 20),
        cost_estimate=pl.CostEstimate(flops=flops, bytes_accessed=moved, transcendentals=0),
    )(*held, *after)


def sds(shape, dtype):
    return jax.ShapeDtypeStruct(shape, dtype)


def swap(value, axis, mask):
    count = lax.axis_size(axis)
    return lax.ppermute(value, axis, [(s, s ^ mask) for s in range(count)])


def swaps(values, axis, step):
    got = []
    for m, value in enumerate(values):
        got.append(swap(value, axis, (m + 1) * step))
    return got


def low_half(shape):
    return lax.broadcasted_iota(jnp.int32, shape, len(shape) - 1) < LANES // 2


def half_turn(value):
    return pltpu.roll(value, LANES // 2, axis=1)


def column_shift(value, step, width):
    if step == 0:
        return value
    rows = value.shape[0]
    turned = pltpu.roll(value, (-step) % rows, axis=0)
    column = lax.broadcasted_iota(jnp.int32, value.shape, 0) % width
    edge = width - 1 if step > 0 else 0
    return jnp.where(column == edge, jnp.zeros_like(turned), turned)


def row_shift(value, step, width):
    if step == 0:
        return value
    blank = jnp.zeros((width, value.shape[1]), value.dtype)
    if step > 0:
        return jnp.concatenate([value[width:], blank], axis=0)
    return jnp.concatenate([blank, value[:-width]], axis=0)


def kept(length_ref, frame):
    return jnp.where(frame < length_ref[0], 1.0, 0.0).astype(F32)


def slice_body(peers, area, cot_hbm, clips_hbm, *refs):
    outs, own = refs[:peers], refs[peers]
    cot, picks, sems = refs[peers + 1 :]
    me = lax.axis_index("tm")
    copies = []
    for tile in range(cot.shape[0]):
        lanes = pl.ds(tile * LANES, LANES)
        copies.append(pltpu.make_async_copy(cot_hbm.at[:, lanes], cot.at[tile], sems.at[tile]))
    own_copy = pltpu.make_async_copy(clips_hbm, own, sems.at[len(copies)])
    for copy in (*copies, own_copy):
        copy.start()
    low = low_half((area, LANES))
    halves = peers // len(copies)
    for tile, copy in enumerate(copies):
        copy.wait()
        first = cot[tile, :area, :].astype(F32)
        second = cot[tile, area:, :].astype(F32)
        picks[tile * halves] = jnp.where(low, first, half_turn(second))
        picks[tile * halves + 1] = jnp.where(low, half_turn(first), second)
    for mask, out in enumerate(outs):
        out[...] = picks[me ^ mask].astype(BF16)
    own_copy.wait()


def place_grads_body(peers, area, width, length_ref, *refs):
    slices, grads = refs[:peers], refs[peers]
    me = lax.axis_index("tm")
    grads[2 * peers * area :, :] = jnp.zeros((2 * area, grads.shape[1]), BF16)
    low = low_half((area, LANES))
    for mask, ref in enumerate(slices):
        start = pl.multiple_of((me ^ mask) * 2 * area, 2 * area)
        first = 2 * (me ^ mask)
        keep = jnp.where(low, kept(length_ref, first), kept(length_ref, first + 1))
        both = ref[...].astype(F32) * keep
        taps = []
        for row_tap in range(3):
            for col_tap in range(3):
                moved = column_shift(both, 1 - col_tap, width)
                turned = half_turn(moved)
                taps.append([row_shift(v, 1 - row_tap, width) for v in (moved, turned)])
        taps.append([jnp.zeros_like(both)] * 2)
        for tile in range(5):
            (even, even_turned), (odd, odd_turned) = taps[2 * tile], taps[2 * tile + 1]
            for frame in range(2):
                left, right = (even, odd_turned) if frame == 0 else (even_turned, odd)
                grads[pl.ds(start + frame * area, area), tile * LANES : (tile + 1) * LANES] = (
                    jnp.where(low, left, right).astype(BF16)
                )


def cut_body(start, source, out_ref):
    out_ref[...] = source[start : start + out_ref.shape[0], :]


def turn_frame(act_t, block, frame, values):
    area = values.shape[0]
    at = pl.multiple_of((2 * block + frame) * area, area)
    act_t[:, pl.ds(at, area)] = jax.nn.silu(values.astype(F32)).astype(BF16).T


def turn_blocks_body(area, *refs):
    act_t = refs[-1]
    me = lax.axis_index("tm")
    for mask, ref in enumerate(refs[:-1]):
        for frame in range(2):
            turn_frame(act_t, me ^ mask, frame, ref[frame * area : (frame + 1) * area, :])
    at = pl.multiple_of(2 * (me ^ 3) * area, area)
    act_t[:, pl.ds(at, 2 * area)] = jnp.zeros((act_t.shape[0], 2 * area), BF16)


def products_body(peers, area, grads, act_t, *outs):
    for time_tap, out in enumerate(outs):
        used = (2 * peers - 2 + time_tap) * area
        first = (2 - time_tap) * area
        out[...] = jnp.dot(
            act_t[:, :used], grads[first : first + used, :], preferred_element_type=F32
        )


def kernel_grad_body(area, grads, first, second, *refs):
    held, (keep_ref, send_ref) = refs[:3], refs[3:]
    me = lax.axis_index("tm")
    core = lax.axis_index("dp") % 2
    values = jnp.concatenate([first[...], second[...]], axis=0).astype(F32)
    turned = jax.nn.silu(values).astype(BF16).T
    sums = []
    for time_tap, ref in enumerate(held):
        at = pl.multiple_of((2 * (me ^ 3) + 2 - time_tap) * area, area)
        sums.append(
            ref[...]
            + jnp.dot(turned, grads[pl.ds(at, 2 * area), :], preferred_element_type=F32)
        )
    tiles = [s[:, tile * LANES : (tile + 1) * LANES] for s in sums for tile in range(4)]
    last = [s[:, 4 * LANES :] for s in sums]
    low = low_half(last[0].shape)
    tiles.append(jnp.where(low, last[0], half_turn(last[1])))
    tiles.append(last[2])
    parts, count = keep_ref.shape[:2]
    groups = [
        [t[(2 * z + c) * count : (2 * z + c + 1) * count] for t in tiles]
        for z in range(parts)
        for c in range(2)
    ]
    for own in range(2):

        @pl.when(core == own)
        def _(own=own):
            for z in range(parts):
                for at in range(len(tiles)):
                    lanes = slice(at * LANES, (at + 1) * LANES)
                    keep_ref[z, :, lanes] = groups[2 * z + own][at]
                    send_ref[z, :, lanes] = groups[2 * z + 1 - own][at].astype(BF16)


def sum_body(arrived, radix, step, *refs):
    keep_ref, in_refs = refs[0], refs[1 : 1 + arrived]
    total = keep_ref[...]
    for ref in in_refs:
        total = total + ref[...].astype(F32)
    if radix == 1:
        refs[1 + arrived][...] = total[0].astype(BF16)
        return
    out_refs, held = refs[1 + arrived : -1], refs[-1]
    held[...] = total
    digit = (lax.axis_index("dp") // 2) // step % radix
    for mask, out in enumerate(out_refs):
        out[...] = held[pl.ds((digit ^ mask) * step, step)].astype(out.dtype)


def sum_over_clips(keep, send, after):
    arrived = [swap(send, "dp", 1)]
    while True:
        parts, count, lanes = keep.shape
        radix = 1 if parts == 1 else (4 if parts % 4 == 0 else 2)
        assert parts % radix == 0 and radix & (radix - 1) == 0, "dp size"
        step = parts // radix
        if radix == 1:
            return call(
                functools.partial(sum_body, len(arrived), 1, 1),
                [pltpu.VMEM((count, lanes), BF16)],
                (keep, *arrived),
                after=after,
            )[0]
        outs = [pltpu.VMEM((step, count, lanes), F32)]
        outs += [pltpu.VMEM((step, count, lanes), BF16)] * (radix - 1)
        keep, *sends = call(
            functools.partial(sum_body, len(arrived), radix, step),
            outs,
            (keep, *arrived),
            scratch=[pltpu.VMEM((parts, count, lanes), F32)],
        )
        arrived = swaps(sends, "dp", 2 * step)


def place_body(peers, scale, *refs):
    pieces, out_ref, held = refs[:peers], refs[peers], refs[peers + 1]
    me = lax.axis_index("tm")
    for mask, piece in enumerate(pieces):
        held[me ^ mask] = piece[...].astype(F32) * scale
    low = low_half((held.shape[1], LANES))
    for time_tap in range(3):
        for tap in range(9):
            tile = 4 * time_tap + tap // 2 if tap < 8 else 12 + time_tap // 2
            half = tap % 2 if tap < 8 else time_tap % 2
            for pair in range(peers // 2):
                left = held[2 * pair, :, tile * LANES : (tile + 1) * LANES]
                right = held[2 * pair + 1, :, tile * LANES : (tile + 1) * LANES]
                if half == 0:
                    value = jnp.where(low, left, half_turn(right))
                else:
                    value = jnp.where(low, half_turn(left), right)
                out_ref[9 * time_tap + tap, :, pair * LANES : (pair + 1) * LANES] = value


def fill_padded(out_ref, frame, value, width, height, direction):
    wide = value.shape[1]
    blank = jnp.zeros((width, 3 * wide), BF16)
    out_ref[frame, :width, :] = blank
    out_ref[frame, (height + 1) * width :, :] = blank
    for tap in range(3):
        out_ref[frame, width : (height + 1) * width, tap * wide : (tap + 1) * wide] = column_shift(
            value, direction * (tap - 1), width
        ).astype(BF16)


def ahead_body(area, width, length_ref, own, near, first, second, w_ref, out_ref, token_ref, acts):
    token_ref[...] = jnp.zeros_like(token_ref)
    me = lax.axis_index("tm")
    height = area // width
    far = jnp.concatenate([first[...], second[...]], axis=0)
    for frame in range(2):
        rows = slice(frame * area, (frame + 1) * area)
        value = jnp.where((me ^ 3) == me - 1, far[rows].astype(F32), near[rows, :].astype(F32))
        value = value * jnp.where(me > 0, 1.0, 0.0).astype(F32)
        fill_padded(acts, frame, jax.nn.silu(value), width, height, 1)
        value = own[rows, :].astype(F32)
        fill_padded(acts, 2 + frame, jax.nn.silu(value), width, height, 1)
    for frame in range(2):
        rows = slice(frame * area, (frame + 1) * area)
        total = jnp.zeros((area, out_ref.shape[1]), F32)
        for time_tap in range(3):
            for row_tap in range(3):
                window = acts[frame + time_tap, row_tap * width : row_tap * width + area, :]
                total = total + jnp.dot(
                    window, w_ref[3 * time_tap + row_tap], preferred_element_type=F32
                )
        out_ref[rows, :] = (total * kept(length_ref, 2 * me + frame)).astype(BF16)


def back_body(area, width, total_clips, length_ref, own, cot, later, wt_ref, gin_ref, grads):
    me = lax.axis_index("tm")
    height = area // width
    for frame in range(2):
        rows = slice(frame * area, (frame + 1) * area)
        for at, ref in ((frame, cot), (2 + frame, later)):
            value = ref[rows, :].astype(F32) * kept(length_ref, 2 * me + at)
            fill_padded(grads, at, value, width, height, -1)
    for frame in range(2):
        rows = slice(frame * area, (frame + 1) * area)
        total = jnp.zeros((area, gin_ref.shape[1]), F32)
        for time_tap in range(3):
            for row_tap in range(3):
                first = (2 - row_tap) * width
                window = grads[frame + 2 - time_tap, first : first + area, :]
                total = total + jnp.dot(
                    window, wt_ref[3 * time_tap + row_tap], preferred_element_type=F32
                )
        values = own[rows, :].astype(F32)
        sig = jax.nn.sigmoid(values)
        slope = sig * (1.0 + values * (1.0 - sig))
        keep = kept(length_ref, 2 * me + frame)
        gin_ref[rows, :] = (total * slope * (keep / total_clips)).astype(BF16)


def turn_body(w_ref, out_ref):
    wide = w_ref.shape[2]
    for tap in range(27):
        rows = slice(tap % 3 * wide, (tap % 3 + 1) * wide)
        out_ref[tap // 3, rows, :] = w_ref[tap // 3, rows, :].T


def local(video_clips, cotangent, weight, lengths):
    clip_count, frame_count, height, width, channels = video_clips.shape
    peers, shards = lax.axis_size("tm"), lax.axis_size("dp")
    total_clips = clip_count * shards
    area = height * width
    assert clip_count == 1 and frame_count == 2, "block shape"
    assert 2 * channels == peers * LANES and peers == 4, "tm size"
    clips = video_clips.reshape(2 * area, channels)
    cot = cotangent.reshape(2 * area, channels)

    block = (2 * area, channels)
    near_x, near_y = swaps([clips] * 2, "tm", 1)
    *slices, own = call(
        functools.partial(slice_body, peers, area),
        [pltpu.VMEM((area, LANES), BF16)] * peers + [pltpu.VMEM(block, BF16)],
        (cot, clips),
        resident=False,
        scratch=[
            pltpu.VMEM((channels // LANES, 2 * area, LANES), BF16),
            pltpu.VMEM((peers, area, LANES), F32),
            pltpu.SemaphoreType.DMA((channels // LANES + 1,)),
        ],
    )
    slices = [slices[0]] + swaps(slices[1:], "tm", 1)
    split = area + area // 4
    relayed = [
        call(functools.partial(cut_body, start), [pltpu.VMEM((size, channels), BF16)], (near,))[0]
        for start, size, near in ((0, split, near_x), (split, 2 * area - split, near_y))
    ]
    first = swap(relayed[0], "tm", 2)
    second = swap(relayed[1], "tm", 1)
    later = lax.ppermute(cot, "tm", [(s, s - 1) for s in range(1, peers)])
    (act_t,) = call(
        functools.partial(turn_blocks_body, area),
        [pltpu.VMEM((channels, 2 * peers * area), BF16)],
        (own, near_x, near_y),
    )
    (grads,) = call(
        functools.partial(place_grads_body, peers, area, width),
        [pltpu.VMEM((2 * (peers + 1) * area, 5 * LANES), BF16)],
        (lengths, *slices),
    )

    parts = shards // 2
    count = channels // shards
    lanes = 14 * LANES
    products = call(
        functools.partial(products_body, peers, area),
        [pltpu.VMEM((channels, 5 * LANES), F32)] * 3,
        (grads, act_t),
        flops=2 * 27 * 2 * peers * area * channels * LANES // 2,
    )
    keep, send = call(
        functools.partial(kernel_grad_body, area),
        [pltpu.VMEM((parts, count, lanes), F32), pltpu.VMEM((parts, count, lanes), BF16)],
        (grads, first, second, *products),
        flops=2 * 27 * 2 * area * channels * LANES // 2,
    )
    flat = weight.reshape(9, 3 * channels, channels)
    token = pltpu.VMEM((8, LANES), F32)
    padded = pltpu.VMEM((4, area + 2 * width, 3 * channels), BF16)
    flops = 2 * 27 * 2 * area * channels * channels
    conv_out, token_a = call(
        functools.partial(ahead_body, area, width),
        [sds(block, BF16), token],
        (lengths, own, near_x, first, second, flat),
        after=(keep,),
        scratch=[padded],
        flops=flops,
    )
    (turned,) = call(turn_body, [pltpu.VMEM(flat.shape, BF16)], (flat,), after=(token_a,))
    piece = sum_over_clips(keep, send, (token_a,))
    (input_grad,) = call(
        functools.partial(back_body, area, width, total_clips),
        [sds(block, BF16)],
        (lengths, own, cot, later, turned),
        after=(piece,),
        scratch=[padded],
        flops=flops,
    )
    pieces = [piece] + swaps([piece] * (peers - 1), "tm", 1)
    (placed,) = call(
        functools.partial(place_body, peers, 1.0 / total_clips),
        [sds((27, count, channels), F32)],
        pieces,
        scratch=[pltpu.VMEM((peers, count, lanes), F32)],
    )
    shape = video_clips.shape
    weight_grad = placed.reshape(3, 3, 3, count, channels)
    return conv_out.reshape(shape), input_grad.reshape(shape), weight_grad


def cuts(parts):
    found = []
    while parts > 1:
        if parts % 4 == 0:
            found.append(parts)
        parts //= 4 if parts % 4 == 0 else 2
    return found


def solution(mesh):
    in_specs = (P("dp", "tm", None, None, None), P("dp", "tm", None, None, None), P(), P("dp"))
    out_specs = (
        P("dp", "tm", None, None, None),
        P("dp", "tm", None, None, None),
        P(None, None, None, "dp", None),
    )

    program = jax.shard_map(local, mesh=mesh, in_specs=in_specs, out_specs=out_specs, check_vma=False)
    sizes = cuts(mesh.shape["dp"] // 2)
    assert sizes, "dp size"
    return program
```

profile of v0, /device:TPU:0, one launch (start us, length us, event | category | flops | bytes accessed | tf_op | source)
XLA Modules:
  0.0 46.9 jit_solution(15173858764738885843)
XLA Ops:
  0.6 3.0 %collective-permute-start = (bf16[512,256]{1,0:T(8,128)(2,1)}, bf16[512,256]{1,0:T(8,128)(2,1)S(1)}, u32[]{:S(2)}, u32[]{:S(2)}) collective-permute-start(bf16[512,256]{1,0:T(8,128)(2,1)} %bitcast.12), channel_id=1, source_target_pairs={{0,8},{8,0},{16,24},{24,16},{1,9},{9,1},{17,25},{25,17},{2,10},{10... | collective-permute-start | bytes 786440 | tf_op jit(solution)/shard_map/ppermute | solution.py:45
  3.7 1.5 %collective-permute-start.2 = (bf16[512,256]{1,0:T(8,128)(2,1)}, bf16[512,256]{1,0:T(8,128)(2,1)S(1)}, u32[]{:S(2)}, u32[]{:S(2)}) collective-permute-start(bf16[512,256]{1,0:T(8,128)(2,1)} %bitcast.13), channel_id=1, source_target_pairs={{0,16},{8,24},{16,0},{24,8},{1,17},{9,25},{17,1},{25,9},{2,18},{10... | collective-permute-start | bytes 786440 | tf_op jit(solution)/shard_map/ppermute | solution.py:45
  5.2 1.2 %shard_map.67 = (bf16[256,128]{1,0:T(8,128)(2,1)S(1)}, bf16[256,128]{1,0:T(8,128)(2,1)S(1)}, bf16[256,128]{1,0:T(8,128)(2,1)S(1)}, bf16[256,128]{1,0:T(8,128)(2,1)S(1)}, bf16[512,256]{1,0:T(8,128)(2,1)S(1)}) custom-call(bf16[512,256]{1,0:T(8,128)(2,1)} %bitcast.8, bf16[512,256]{1,0:T(8,128)(2,1)} %bitcast.14), custom_call_target="tpu_custom_call" | custom-call | bytes 524288 | tf_op jit(solution)/shard_map/pallas_call | solution.py:26
  6.4 0.6 %collective-permute-start.4 = (bf16[256,128]{1,0:T(8,128)(2,1)S(1)}, bf16[256,128]{1,0:T(8,128)(2,1)S(1)}, u32[]{:S(2)}, u32[]{:S(2)}) collective-permute-start(bf16[256,128]{1,0:T(8,128)(2,1)S(1)} %get-tuple-element.21), channel_id=1, source_target_pairs={{0,8},{8,0},{16,24},{24,16},{1,9},{9,1},{17,25},{25,17},{2,10},{10... | collective-permute-start | bytes 196616 | tf_op jit(solution)/shard_map/ppermute | solution.py:45
  7.0 2.9 %collective-permute-start.6 = (bf16[256,128]{1,0:T(8,128)(2,1)S(1)}, bf16[256,128]{1,0:T(8,128)(2,1)S(1)}, u32[]{:S(2)}, u32[]{:S(2)}) collective-permute-start(bf16[256,128]{1,0:T(8,128)(2,1)S(1)} %get-tuple-element.23), channel_id=1, source_target_pairs={{0,24},{8,16},{16,8},{24,0},{1,25},{9,17},{17,9},{25,1},{2,26},{10... | collective-permute-start | bytes 196616 | tf_op jit(solution)/shard_map/ppermute | solution.py:45
  10.6 1.7 %collective-permute-done.4.refs_2_ = bf16[256,128]{1,0:T(8,128)(2,1)S(1)} collective-permute-done((bf16[256,128]{1,0:T(8,128)(2,1)S(1)}, bf16[256,128]{1,0:T(8,128)(2,1)S(1)}, u32[]{:S(2)}, u32[]{:S(2)}) %collective-permute-start.4) | collective-permute-done | bytes 65568 | tf_op jit(solution)/shard_map/ppermute | solution.py:45
  12.3 2.2 %collective-permute-done.5.refs_3_ = bf16[256,128]{1,0:T(8,128)(2,1)S(1)} collective-permute-done((bf16[256,128]{1,0:T(8,128)(2,1)S(1)}, bf16[256,128]{1,0:T(8,128)(2,1)S(1)}, u32[]{:S(2)}, u32[]{:S(2)}) %collective-permute-start.5) | collective-permute-done | bytes 65568 | tf_op jit(solution)/shard_map/ppermute | solution.py:45
  14.5 0.7 %shard_map.70.refs_0_ = bf16[2560,640]{1,0:T(8,128)(2,1)S(1)} custom-call(s32[1]{0:T(128)S(6)} %copy.7.refs_0_, bf16[256,128]{1,0:T(8,128)(2,1)S(1)} %get-tuple-element.20.refs_1_, bf16[256,128]{1,0:T(8,128)(2,1)S(1)} %collective-permute-done.4.refs_2_, bf16[256,128]{1,0:T(8,128)(2,1)S(1)} %collective-permute-done.5.refs_3_, ...), custom_call_target="tpu_custom_call" | custom-call | bytes 262148 | tf_op jit(solution)/shard_map/pallas_call | solution.py:26
  15.2 1.6 %collective-permute-start.1 = (bf16[320,256]{1,0:T(8,128)(2,1)S(1)}, bf16[320,256]{1,0:T(8,128)(2,1)S(1)}, u32[]{:S(2)}, u32[]{:S(2)}) collective-permute-start(bf16[320,256]{1,0:T(8,128)(2,1)S(1)} %shard_map.68), channel_id=1, source_target_pairs={{0,16},{8,24},{16,0},{24,8},{1,17},{9,25},{17,1},{25,9},{2,18},{10... | collective-permute-start | bytes 491528 | tf_op jit(solution)/shard_map/ppermute | solution.py:45
  16.8 0.6 %collective-permute-start.3 = (bf16[192,256]{1,0:T(8,128)(2,1)S(1)}, bf16[192,256]{1,0:T(8,128)(2,1)S(1)}, u32[]{:S(2)}, u32[]{:S(2)}) collective-permute-start(bf16[192,256]{1,0:T(8,128)(2,1)S(1)} %shard_map.69), channel_id=1, source_target_pairs={{0,8},{8,0},{16,24},{24,16},{1,9},{9,1},{17,25},{25,17},{2,10},{10... | collective-permute-start | bytes 294920 | tf_op jit(solution)/shard_map/ppermute | solution.py:45
  17.4 0.3 shard_map.71.refs_1_
  17.8 2.3 %shard_map.72 = (f32[256,640]{1,0:T(8,128)S(1)}, f32[256,640]{1,0:T(8,128)S(1)}, f32[256,640]{1,0:T(8,128)S(1)}) custom-call(bf16[2560,640]{1,0:T(8,128)(2,1)S(1)} %shard_map.70.refs_0_, bf16[256,2048]{1,0:T(8,128)(2,1)S(1)} %shard_map.71.refs_1_), custom_call_target="tpu_custom_call" | custom-call | flops 1811939328 | bytes 4325376 | tf_op jit(solution)/shard_map/pallas_call | solution.py:26
  20.1 1.4 %collective-permute-done.3.refs_2_.refs_4_ = bf16[192,256]{1,0:T(8,128)(2,1)S(1)} collective-permute-done((bf16[192,256]{1,0:T(8,128)(2,1)S(1)}, bf16[192,256]{1,0:T(8,128)(2,1)S(1)}, u32[]{:S(2)}, u32[]{:S(2)}) %collective-permute-start.3) | collective-permute-done | bytes 98336 | tf_op jit(solution)/shard_map/ppermute | solution.py:45
  21.5 0.9 %shard_map.73 = (f32[4,32,1792]{2,1,0:T(8,128)S(1)}, bf16[4,32,1792]{2,1,0:T(8,128)(2,1)S(1)}) custom-call(bf16[2560,640]{1,0:T(8,128)(2,1)S(1)} %shard_map.70.refs_0_, bf16[320,256]{1,0:T(8,128)(2,1)S(1)} %collective-permute-done.1.refs_1_.refs_3_, bf16[192,256]{1,0:T(8,128)(2,1)S(1)} %collective-permute-done.3.refs_2_.refs_4_, ...), custom_call_target="tpu_custom_call" | custom-call | flops 452984832 | bytes 5505024 | tf_op jit(solution)/shard_map/pallas_call | solution.py:26
  22.4 0.1 collective-permute-start.8
  22.5 1.3 %collective-permute-start.7 = (bf16[512,256]{1,0:T(8,128)(2,1)S(1)}, bf16[512,256]{1,0:T(8,128)(2,1)S(1)}, u32[]{:S(2)}, u32[]{:S(2)}) collective-permute-start(bf16[512,256]{1,0:T(8,128)(2,1)S(1)} %bitcast.9), channel_id=1, source_target_pairs={{8,0},{16,8},{24,16},{9,1},{17,9},{25,17},{10,2},{18,10},{26,18},{... | collective-permute-start | bytes 786440 | tf_op jit(solution)/shard_map/ppermute | solution.py:358
  23.8 0.5 %collective-permute-done.8.refs_1_ = bf16[4,32,1792]{2,1,0:T(8,128)(2,1)S(1)} collective-permute-done((bf16[4,32,1792]{2,1,0:T(8,128)(2,1)S(1)}, bf16[4,32,1792]{2,1,0:T(8,128)(2,1)S(1)}, u32[]{:S(2)}, u32[]{:S(2)}) %collective-permute-start.8) | collective-permute-done | bytes 458784 | tf_op jit(solution)/shard_map/ppermute | solution.py:45
  24.3 0.1 shard_map.76
  24.5 2.7 %collective-permute-start.10 = (bf16[1,32,1792]{2,1,0:T(8,128)(2,1)S(1)}, bf16[1,32,1792]{2,1,0:T(8,128)(2,1)S(1)}, u32[]{:S(2)}, u32[]{:S(2)}) collective-permute-start(bf16[1,32,1792]{2,1,0:T(8,128)(2,1)S(1)} %get-tuple-element.33), channel_id=1, source_target_pairs={{0,4},{1,5},{2,6},{3,7},{4,0},{5,1},{6,2},{7,3},{8,12},{9,13},{10,... | collective-permute-start | bytes 344072 | tf_op jit(solution)/shard_map/ppermute | solution.py:45
  27.1 1.3 %collective-permute-start.11 = (bf16[1,32,1792]{2,1,0:T(8,128)(2,1)S(1)}, bf16[1,32,1792]{2,1,0:T(8,128)(2,1)S(1)}, u32[]{:S(2)}, u32[]{:S(2)}) collective-permute-start(bf16[1,32,1792]{2,1,0:T(8,128)(2,1)S(1)} %get-tuple-element.34), channel_id=1, source_target_pairs={{0,6},{1,7},{2,4},{3,5},{4,2},{5,3},{6,0},{7,1},{8,14},{9,15},{10,... | collective-permute-start | bytes 344072 | tf_op jit(solution)/shard_map/ppermute | solution.py:45
  28.5 0.2 collective-permute-start.9
  28.7 2.8 %shard_map.74 = (bf16[512,256]{1,0:T(8,128)(2,1)}, f32[8,128]{1,0:T(8,128)S(1)}) custom-call(s32[1]{0:T(128)S(6)} %copy.7.refs_0_, bf16[512,256]{1,0:T(8,128)(2,1)S(1)} %get-tuple-element.19.refs_0_.refs_1_, bf16[512,256]{1,0:T(8,128)(2,1)S(1)} %collective-permute-done.refs_0_.refs_1_.refs_2_, bf16[320,256]{1,0:T(8,128)(2,1)S(1)} %collective-permute-done.1.refs_1_.refs_3_, ...), custom_call_target="tpu_custom_call" | custom-call | flops 1811939328 | bytes 4325380 | tf_op jit(solution)/shard_map/pallas_call | solution.py:26
  31.5 1.0 %shard_map.75.refs_4_ = bf16[9,768,256]{2,1,0:T(8,128)(2,1)S(1)} custom-call(bf16[9,768,256]{2,1,0:T(8,128)(2,1)S(1)} %bitcast.7, f32[8,128]{1,0:T(8,128)S(1)} %get-tuple-element.29.refs_1_.refs_4_), custom_call_target="tpu_custom_call" | custom-call | bytes 3538944 | tf_op jit(solution)/shard_map/pallas_call | solution.py:26
  32.5 3.9 %collective-permute-done.10.refs_2_ = bf16[1,32,1792]{2,1,0:T(8,128)(2,1)S(1)} collective-permute-done((bf16[1,32,1792]{2,1,0:T(8,128)(2,1)S(1)}, bf16[1,32,1792]{2,1,0:T(8,128)(2,1)S(1)}, u32[]{:S(2)}, u32[]{:S(2)}) %collective-permute-start.10) | collective-permute-done | bytes 114720 | tf_op jit(solution)/shard_map/ppermute | solution.py:45
  36.4 0.5 %collective-permute-done.9.refs_1_ = bf16[1,32,1792]{2,1,0:T(8,128)(2,1)S(1)} collective-permute-done((bf16[1,32,1792]{2,1,0:T(8,128)(2,1)S(1)}, bf16[1,32,1792]{2,1,0:T(8,128)(2,1)S(1)}, u32[]{:S(2)}, u32[]{:S(2)}) %collective-permute-start.9) | collective-permute-done | bytes 114720 | tf_op jit(solution)/shard_map/ppermute | solution.py:45
  37.0 2.3 %collective-permute-start.12 = (bf16[32,1792]{1,0:T(8,128)(2,1)S(1)}, bf16[32,1792]{1,0:T(8,128)(2,1)S(1)}, u32[]{:S(2)}, u32[]{:S(2)}) collective-permute-start(bf16[32,1792]{1,0:T(8,128)(2,1)S(1)} %shard_map.77.refs_5_.refs_0_), channel_id=1, source_target_pairs={{0,8},{8,0},{16,24},{24,16},{1,9},{9,1},{17,25},{25,17},{2,10},{10... | collective-permute-start | bytes 344072 | tf_op jit(solution)/shard_map/ppermute | solution.py:45
  39.3 0.6 %collective-permute-start.13 = (bf16[32,1792]{1,0:T(8,128)(2,1)S(1)}, bf16[32,1792]{1,0:T(8,128)(2,1)S(1)}, u32[]{:S(2)}, u32[]{:S(2)}) collective-permute-start(bf16[32,1792]{1,0:T(8,128)(2,1)S(1)} %shard_map.77.refs_5_.refs_0_), channel_id=1, source_target_pairs={{0,16},{8,24},{16,0},{24,8},{1,17},{9,25},{17,1},{25,9},{2,18},{10... | collective-permute-start | bytes 344072 | tf_op jit(solution)/shard_map/ppermute | solution.py:45
  39.9 0.9 %collective-permute-start.14 = (bf16[32,1792]{1,0:T(8,128)(2,1)S(1)}, bf16[32,1792]{1,0:T(8,128)(2,1)S(1)}, u32[]{:S(2)}, u32[]{:S(2)}) collective-permute-start(bf16[32,1792]{1,0:T(8,128)(2,1)S(1)} %shard_map.77.refs_5_.refs_0_), channel_id=1, source_target_pairs={{0,24},{8,16},{16,8},{24,0},{1,25},{9,17},{17,9},{25,1},{2,26},{10... | collective-permute-start | bytes 344072 | tf_op jit(solution)/shard_map/ppermute | solution.py:45
  40.8 2.8 %shard_map.78 = bf16[512,256]{1,0:T(8,128)(2,1)} custom-call(s32[1]{0:T(128)S(6)} %copy.7.refs_0_, bf16[512,256]{1,0:T(8,128)(2,1)S(1)} %get-tuple-element.19.refs_0_.refs_1_, bf16[512,256]{1,0:T(8,128)(2,1)S(1)} %bitcast.10, bf16[512,256]{1,0:T(8,128)(2,1)S(1)} %collective-permute-done.7.refs_3_, bf16[9,768,256]{2,1,0:T(8,128)(2,1)S(1)} %shard_map.75.refs_4_, ...), custom_call_target="tpu_custom_call" | custom-call | flops 1811939328 | bytes 4325380 | tf_op jit(solution)/shard_map/pallas_call | solution.py:26
  43.6 0.6 %collective-permute-done.13.refs_2_ = bf16[32,1792]{1,0:T(8,128)(2,1)S(1)} collective-permute-done((bf16[32,1792]{1,0:T(8,128)(2,1)S(1)}, bf16[32,1792]{1,0:T(8,128)(2,1)S(1)}, u32[]{:S(2)}, u32[]{:S(2)}) %collective-permute-start.13) | collective-permute-done | bytes 114720 | tf_op jit(solution)/shard_map/ppermute | solution.py:45
  44.2 1.4 %collective-permute-done.14.refs_3_ = bf16[32,1792]{1,0:T(8,128)(2,1)S(1)} collective-permute-done((bf16[32,1792]{1,0:T(8,128)(2,1)S(1)}, bf16[32,1792]{1,0:T(8,128)(2,1)S(1)}, u32[]{:S(2)}, u32[]{:S(2)}) %collective-permute-start.14) | collective-permute-done | bytes 114720 | tf_op jit(solution)/shard_map/ppermute | solution.py:45
  45.6 1.3 %shard_map.79 = f32[27,32,256]{2,1,0:T(8,128)} custom-call(bf16[32,1792]{1,0:T(8,128)(2,1)S(1)} %shard_map.77.refs_5_.refs_0_, bf16[32,1792]{1,0:T(8,128)(2,1)S(1)} %collective-permute-done.12.refs_1_, bf16[32,1792]{1,0:T(8,128)(2,1)S(1)} %collective-permute-done.13.refs_2_, bf16[32,1792]{1,0:T(8,128)(2,1)S(1)} %collective-permute-done.14.refs_3_), custom_call_target="tpu_custom_call" | custom-call | bytes 458752 | tf_op jit(solution)/shard_map/pallas_call | solution.py:26
  (15 shorter events, 0.2 us)
Async XLA Ops:
  0.6 14.6 %collective-permute-start = (bf16[512,256]{1,0:T(8,128)(2,1)}, bf16[512,256]{1,0:T(8,128)(2,1)S(1)}, u32[]{:S(2)}, u32[]{:S(2)}) collective-permute-start(bf16[512,256]{1,0:T(8,128)(2,1)} %bitcast.12), channel_id=1, source_target_pairs={{0,8},{8,0},{16,24},{24,16},{1,9},{9,1},{17,25},{25,17},{2,10},{10... | collective-permute-start | bytes 786440 | tf_op jit(solution)/shard_map/ppermute | solution.py:45
  3.7 13.1 %collective-permute-start.2 = (bf16[512,256]{1,0:T(8,128)(2,1)}, bf16[512,256]{1,0:T(8,128)(2,1)S(1)}, u32[]{:S(2)}, u32[]{:S(2)}) collective-permute-start(bf16[512,256]{1,0:T(8,128)(2,1)} %bitcast.13), channel_id=1, source_target_pairs={{0,16},{8,24},{16,0},{24,8},{1,17},{9,25},{17,1},{25,9},{2,18},{10... | collective-permute-start | bytes 786440 | tf_op jit(solution)/shard_map/ppermute | solution.py:45
  6.4 5.9 %collective-permute-start.4 = (bf16[256,128]{1,0:T(8,128)(2,1)S(1)}, bf16[256,128]{1,0:T(8,128)(2,1)S(1)}, u32[]{:S(2)}, u32[]{:S(2)}) collective-permute-start(bf16[256,128]{1,0:T(8,128)(2,1)S(1)} %get-tuple-element.21), channel_id=1, source_target_pairs={{0,8},{8,0},{16,24},{24,16},{1,9},{9,1},{17,25},{25,17},{2,10},{10... | collective-permute-start | bytes 196616 | tf_op jit(solution)/shard_map/ppermute | solution.py:45
  7.0 7.5 %collective-permute-start.5 = (bf16[256,128]{1,0:T(8,128)(2,1)S(1)}, bf16[256,128]{1,0:T(8,128)(2,1)S(1)}, u32[]{:S(2)}, u32[]{:S(2)}) collective-permute-start(bf16[256,128]{1,0:T(8,128)(2,1)S(1)} %get-tuple-element.22), channel_id=1, source_target_pairs={{0,16},{8,24},{16,0},{24,8},{1,17},{9,25},{17,1},{25,9},{2,18},{10... | collective-permute-start | bytes 196616 | tf_op jit(solution)/shard_map/ppermute | solution.py:45
  7.0 7.4 %collective-permute-start.6 = (bf16[256,128]{1,0:T(8,128)(2,1)S(1)}, bf16[256,128]{1,0:T(8,128)(2,1)S(1)}, u32[]{:S(2)}, u32[]{:S(2)}) collective-permute-start(bf16[256,128]{1,0:T(8,128)(2,1)S(1)} %get-tuple-element.23), channel_id=1, source_target_pairs={{0,24},{8,16},{16,8},{24,0},{1,25},{9,17},{17,9},{25,1},{2,26},{10... | collective-permute-start | bytes 196616 | tf_op jit(solution)/shard_map/ppermute | solution.py:45
  15.2 6.3 %collective-permute-start.1 = (bf16[320,256]{1,0:T(8,128)(2,1)S(1)}, bf16[320,256]{1,0:T(8,128)(2,1)S(1)}, u32[]{:S(2)}, u32[]{:S(2)}) collective-permute-start(bf16[320,256]{1,0:T(8,128)(2,1)S(1)} %shard_map.68), channel_id=1, source_target_pairs={{0,16},{8,24},{16,0},{24,8},{1,17},{9,25},{17,1},{25,9},{2,18},{10... | collective-permute-start | bytes 491528 | tf_op jit(solution)/shard_map/ppermute | solution.py:45
  16.8 4.7 %collective-permute-start.3 = (bf16[192,256]{1,0:T(8,128)(2,1)S(1)}, bf16[192,256]{1,0:T(8,128)(2,1)S(1)}, u32[]{:S(2)}, u32[]{:S(2)}) collective-permute-start(bf16[192,256]{1,0:T(8,128)(2,1)S(1)} %shard_map.69), channel_id=1, source_target_pairs={{0,8},{8,0},{16,24},{24,16},{1,9},{9,1},{17,25},{25,17},{2,10},{10... | collective-permute-start | bytes 294920 | tf_op jit(solution)/shard_map/ppermute | solution.py:45
  20.1 2.4 %copy-start.1 = (bf16[1,2,16,16,256]{4,3,2,1,0:T(8,128)(2,1)S(1)}, bf16[1,2,16,16,256]{4,3,2,1,0:T(8,128)(2,1)}, u32[]{:S(2)}) copy-start(bf16[1,2,16,16,256]{4,3,2,1,0:T(8,128)(2,1)} %param.5) | copy-start | bytes 786436
  20.1 8.6 %copy-start = (bf16[3,3,3,256,256]{4,3,2,1,0:T(8,128)(2,1)S(1)}, bf16[3,3,3,256,256]{4,3,2,1,0:T(8,128)(2,1)}, u32[]{:S(2)}) copy-start(bf16[3,3,3,256,256]{4,3,2,1,0:T(8,128)(2,1)} %param.6) | copy-start | bytes 10616836
  22.4 1.9 %collective-permute-start.8 = (bf16[4,32,1792]{2,1,0:T(8,128)(2,1)S(1)}, bf16[4,32,1792]{2,1,0:T(8,128)(2,1)S(1)}, u32[]{:S(2)}, u32[]{:S(2)}) collective-permute-start(bf16[4,32,1792]{2,1,0:T(8,128)(2,1)S(1)} %get-tuple-element.30), channel_id=1, source_target_pairs={{0,1},{1,0},{2,3},{3,2},{4,5},{5,4},{6,7},{7,6},{8,9},{9,8},{10,11... | collective-permute-start | bytes 1376264 | tf_op jit(solution)/shard_map/ppermute | solution.py:45
  22.5 18.3 %collective-permute-start.7 = (bf16[512,256]{1,0:T(8,128)(2,1)S(1)}, bf16[512,256]{1,0:T(8,128)(2,1)S(1)}, u32[]{:S(2)}, u32[]{:S(2)}) collective-permute-start(bf16[512,256]{1,0:T(8,128)(2,1)S(1)} %bitcast.9), channel_id=1, source_target_pairs={{8,0},{16,8},{24,16},{9,1},{17,9},{25,17},{10,2},{18,10},{26,18},{... | collective-permute-start | bytes 786440 | tf_op jit(solution)/shard_map/ppermute | solution.py:358
  24.5 11.9 %collective-permute-start.10 = (bf16[1,32,1792]{2,1,0:T(8,128)(2,1)S(1)}, bf16[1,32,1792]{2,1,0:T(8,128)(2,1)S(1)}, u32[]{:S(2)}, u32[]{:S(2)}) collective-permute-start(bf16[1,32,1792]{2,1,0:T(8,128)(2,1)S(1)} %get-tuple-element.33), channel_id=1, source_target_pairs={{0,4},{1,5},{2,6},{3,7},{4,0},{5,1},{6,2},{7,3},{8,12},{9,13},{10,... | collective-permute-start | bytes 344072 | tf_op jit(solution)/shard_map/ppermute | solution.py:45
  27.1 9.3 %collective-permute-start.11 = (bf16[1,32,1792]{2,1,0:T(8,128)(2,1)S(1)}, bf16[1,32,1792]{2,1,0:T(8,128)(2,1)S(1)}, u32[]{:S(2)}, u32[]{:S(2)}) collective-permute-start(bf16[1,32,1792]{2,1,0:T(8,128)(2,1)S(1)} %get-tuple-element.34), channel_id=1, source_target_pairs={{0,6},{1,7},{2,4},{3,5},{4,2},{5,3},{6,0},{7,1},{8,14},{9,15},{10,... | collective-permute-start | bytes 344072 | tf_op jit(solution)/shard_map/ppermute | solution.py:45
  28.5 8.5 %collective-permute-start.9 = (bf16[1,32,1792]{2,1,0:T(8,128)(2,1)S(1)}, bf16[1,32,1792]{2,1,0:T(8,128)(2,1)S(1)}, u32[]{:S(2)}, u32[]{:S(2)}) collective-permute-start(bf16[1,32,1792]{2,1,0:T(8,128)(2,1)S(1)} %get-tuple-element.32), channel_id=1, source_target_pairs={{0,2},{1,3},{2,0},{3,1},{4,6},{5,7},{6,4},{7,5},{8,10},{9,11},{10,... | collective-permute-start | bytes 344072 | tf_op jit(solution)/shard_map/ppermute | solution.py:45
  37.0 6.6 %collective-permute-start.12 = (bf16[32,1792]{1,0:T(8,128)(2,1)S(1)}, bf16[32,1792]{1,0:T(8,128)(2,1)S(1)}, u32[]{:S(2)}, u32[]{:S(2)}) collective-permute-start(bf16[32,1792]{1,0:T(8,128)(2,1)S(1)} %shard_map.77.refs_5_.refs_0_), channel_id=1, source_target_pairs={{0,8},{8,0},{16,24},{24,16},{1,9},{9,1},{17,25},{25,17},{2,10},{10... | collective-permute-start | bytes 344072 | tf_op jit(solution)/shard_map/ppermute | solution.py:45
  39.3 4.9 %collective-permute-start.13 = (bf16[32,1792]{1,0:T(8,128)(2,1)S(1)}, bf16[32,1792]{1,0:T(8,128)(2,1)S(1)}, u32[]{:S(2)}, u32[]{:S(2)}) collective-permute-start(bf16[32,1792]{1,0:T(8,128)(2,1)S(1)} %shard_map.77.refs_5_.refs_0_), channel_id=1, source_target_pairs={{0,16},{8,24},{16,0},{24,8},{1,17},{9,25},{17,1},{25,9},{2,18},{10... | collective-permute-start | bytes 344072 | tf_op jit(solution)/shard_map/ppermute | solution.py:45
  39.9 5.7 %collective-permute-start.14 = (bf16[32,1792]{1,0:T(8,128)(2,1)S(1)}, bf16[32,1792]{1,0:T(8,128)(2,1)S(1)}, u32[]{:S(2)}, u32[]{:S(2)}) collective-permute-start(bf16[32,1792]{1,0:T(8,128)(2,1)S(1)} %shard_map.77.refs_5_.refs_0_), channel_id=1, source_target_pairs={{0,24},{8,16},{16,8},{24,0},{1,25},{9,17},{17,9},{25,1},{2,26},{10... | collective-permute-start | bytes 344072 | tf_op jit(solution)/shard_map/ppermute | solution.py:45
where the time goes:
time: 47.7 us; the launch traced here: 46.9 us
  starting transfers between devices  19.7 us (41%)
  Pallas kernels  13.5 us (28%)
  waiting for transfers between devices  12.3 us (26%)
  between operations  1.4 us (3%)
    ppermute x14, starting transfers between devices, swap(): return lax.ppermute(value, axis, [(s, s ^ mask) for s in range(count)])  18.4 us
    pallas_call x13, Pallas kernels, call(): pl.pallas_call(with_after, out_shape=tuple(outs), in_specs=[pl.BlockSpec(...  13.5 us
    ppermute x14, waiting for transfers between devices, swap(): return lax.ppermute(value, axis, [(s, s ^ mask) for s in range(count)])  12.3 us
    ppermute x1, starting transfers between devices, local(): later = lax.ppermute(cot, 'tm', [(s, s - 1) for s in range(1, peers)])  1.29 us
  transfers between devices with their start and end apart: 15, of which 8 were waited for; matrix products, arithmetic and copies ran while one was open for 0% of the time, Pallas kernels for 24%

commit v1 on v0

--- a/solution.py
+++ b/solution.py
@@ -45,6 +45,28 @@
     return lax.ppermute(value, axis, [(s, s ^ mask) for s in range(count)])
 
 
+def first_mask(core):
+    return 1 + core
+
+
+def cross(value, first):
+    peers, shards = lax.axis_size("tm"), lax.axis_size("dp")
+    pairs = []
+    for t in range(peers):
+        for d in range(shards):
+            mask = first_mask(d % 2) if first else 3 - first_mask(d % 2)
+            pairs.append((t * shards + d, (t ^ mask) * shards + d))
+    return lax.ppermute(value, ("tm", "dp"), pairs)
+
+
+def peer_block(turn):
+    me = lax.axis_index("tm")
+    if turn in (0, 3):
+        return me ^ turn
+    mask = first_mask(lax.axis_index("dp") % 2)
+    return me ^ (mask if turn == 1 else 3 - mask)
+
+
 def swaps(values, axis, step):
     got = []
     for m, value in enumerate(values):
@@ -86,7 +108,6 @@
 def slice_body(peers, area, cot_hbm, clips_hbm, *refs):
     outs, own = refs[:peers], refs[peers]
     cot, picks, sems = refs[peers + 1 :]
-    me = lax.axis_index("tm")
     copies = []
     for tile in range(cot.shape[0]):
         lanes = pl.ds(tile * LANES, LANES)
@@ -102,35 +123,37 @@
         second = cot[tile, area:, :].astype(F32)
         picks[tile * halves] = jnp.where(low, first, half_turn(second))
         picks[tile * halves + 1] = jnp.where(low, half_turn(first), second)
-    for mask, out in enumerate(outs):
-        out[...] = picks[me ^ mask].astype(BF16)
+    for turn, out in enumerate(outs):
+        out[...] = picks[peer_block(turn)].astype(BF16)
     own_copy.wait()
 
 
-def place_grads_body(peers, area, width, length_ref, *refs):
-    slices, grads = refs[:peers], refs[peers]
-    me = lax.axis_index("tm")
-    grads[2 * peers * area :, :] = jnp.zeros((2 * area, grads.shape[1]), BF16)
+def place_slice(area, width, length_ref, block, slice_ref, grads):
     low = low_half((area, LANES))
-    for mask, ref in enumerate(slices):
-        start = pl.multiple_of((me ^ mask) * 2 * area, 2 * area)
-        first = 2 * (me ^ mask)
-        keep = jnp.where(low, kept(length_ref, first), kept(length_ref, first + 1))
-        both = ref[...].astype(F32) * keep
-        taps = []
-        for row_tap in range(3):
-            for col_tap in range(3):
-                moved = column_shift(both, 1 - col_tap, width)
-                turned = half_turn(moved)
-                taps.append([row_shift(v, 1 - row_tap, width) for v in (moved, turned)])
-        taps.append([jnp.zeros_like(both)] * 2)
-        for tile in range(5):
-            (even, even_turned), (odd, odd_turned) = taps[2 * tile], taps[2 * tile + 1]
-            for frame in range(2):
-                left, right = (even, odd_turned) if frame == 0 else (even_turned, odd)
-                grads[pl.ds(start + frame * area, area), tile * LANES : (tile + 1) * LANES] = (
-                    jnp.where(low, left, right).astype(BF16)
-                )
+    start = pl.multiple_of(block * 2 * area, 2 * area)
+    keep = jnp.where(low, kept(length_ref, 2 * block), kept(length_ref, 2 * block + 1))
+    both = slice_ref[...].astype(F32) * keep
+    taps = []
+    for row_tap in range(3):
+        for col_tap in range(3):
+            moved = column_shift(both, 1 - col_tap, width)
+            turned = half_turn(moved)
+            taps.append([row_shift(v, 1 - row_tap, width) for v in (moved, turned)])
+    taps.append([jnp.zeros_like(both)] * 2)
+    for tile in range(5):
+        (even, even_turned), (odd, odd_turned) = taps[2 * tile], taps[2 * tile + 1]
+        for frame in range(2):
+            left, right = (even, odd_turned) if frame == 0 else (even_turned, odd)
+            grads[pl.ds(start + frame * area, area), tile * LANES : (tile + 1) * LANES] = (
+                jnp.where(low, left, right).astype(BF16)
+            )
+
+
+def place_grads_body(masks, area, width, length_ref, *refs):
+    slices, grads = refs[: len(masks)], refs[-1]
+    grads[grads.shape[0] - 2 * area :, :] = jnp.zeros((2 * area, grads.shape[1]), BF16)
+    for mask, ref in zip(masks, slices):
+        place_slice(area, width, length_ref, peer_block(mask), ref, grads)
 
 
 def cut_body(start, source, out_ref):
@@ -148,12 +171,19 @@
     me = lax.axis_index("tm")
     for mask, ref in enumerate(refs[:-1]):
         for frame in range(2):
-            turn_frame(act_t, me ^ mask, frame, ref[frame * area : (frame + 1) * area, :])
+            turn_frame(act_t, peer_block(mask), frame, ref[frame * area : (frame + 1) * area, :])
     at = pl.multiple_of(2 * (me ^ 3) * area, area)
     act_t[:, pl.ds(at, 2 * area)] = jnp.zeros((act_t.shape[0], 2 * area), BF16)
 
 
-def products_body(peers, area, grads, act_t, *outs):
+def products_body(peers, masks, area, width, length_ref, *refs):
+    slices, near_b = refs[: len(masks)], refs[len(masks)]
+    grads, act_t, *outs = refs[len(masks) + 3 :]
+    block = peer_block(2)
+    for mask, ref in zip(masks, slices):
+        place_slice(area, width, length_ref, peer_block(mask), ref, grads)
+    for frame in range(2):
+        turn_frame(act_t, block, frame, near_b[frame * area : (frame + 1) * area, :])
     for time_tap, out in enumerate(outs):
         used = (2 * peers - 2 + time_tap) * area
         first = (2 - time_tap) * area
@@ -268,15 +298,17 @@
         ).astype(BF16)
 
 
-def ahead_body(area, width, length_ref, own, near, first, second, w_ref, out_ref, token_ref, acts):
+def ahead_body(area, width, length_ref, own, near_a, near_b, first, second, w_ref, *refs):
+    out_ref, token_ref, acts = refs
     token_ref[...] = jnp.zeros_like(token_ref)
     me = lax.axis_index("tm")
     height = area // width
     far = jnp.concatenate([first[...], second[...]], axis=0)
     for frame in range(2):
         rows = slice(frame * area, (frame + 1) * area)
-        value = jnp.where((me ^ 3) == me - 1, far[rows].astype(F32), near[rows, :].astype(F32))
-        value = value * jnp.where(me > 0, 1.0, 0.0).astype(F32)
+        value = jnp.zeros((area, far.shape[1]), F32)
+        for turn, block in ((1, near_a[rows, :]), (2, near_b[rows, :]), (3, far[rows])):
+            value = jnp.where(peer_block(turn) == me - 1, block.astype(F32), value)
         fill_padded(acts, frame, jax.nn.silu(value), width, height, 1)
         value = own[rows, :].astype(F32)
         fill_padded(acts, 2 + frame, jax.nn.silu(value), width, height, 1)
@@ -335,7 +367,8 @@
     cot = cotangent.reshape(2 * area, channels)
 
     block = (2 * area, channels)
-    near_x, near_y = swaps([clips] * 2, "tm", 1)
+    near_a = cross(clips, True)
+    near_b = cross(clips, False)
     *slices, own = call(
         functools.partial(slice_body, peers, area),
         [pltpu.VMEM((area, LANES), BF16)] * peers + [pltpu.VMEM(block, BF16)],
@@ -347,33 +380,37 @@
             pltpu.SemaphoreType.DMA((channels // LANES + 1,)),
         ],
     )
-    slices = [slices[0]] + swaps(slices[1:], "tm", 1)
+    slices[1] = cross(slices[1], True)
+    slices[2] = cross(slices[2], False)
+    slices[3] = swap(slices[3], "tm", 3)
     split = area + area // 4
     relayed = [
         call(functools.partial(cut_body, start), [pltpu.VMEM((size, channels), BF16)], (near,))[0]
-        for start, size, near in ((0, split, near_x), (split, 2 * area - split, near_y))
+        for start, size, near in ((0, split, near_a), (split, 2 * area - split, near_b))
     ]
-    first = swap(relayed[0], "tm", 2)
-    second = swap(relayed[1], "tm", 1)
+    first = cross(relayed[0], False)
+    second = cross(relayed[1], True)
     later = lax.ppermute(cot, "tm", [(s, s - 1) for s in range(1, peers)])
     (act_t,) = call(
         functools.partial(turn_blocks_body, area),
         [pltpu.VMEM((channels, 2 * peers * area), BF16)],
-        (own, near_x, near_y),
+        (own, near_a),
     )
     (grads,) = call(
-        functools.partial(place_grads_body, peers, area, width),
+        functools.partial(place_grads_body, (0, 1,), area, width),
         [pltpu.VMEM((2 * (peers + 1) * area, 5 * LANES), BF16)],
-        (lengths, *slices),
+        (lengths, slices[0], slices[1]),
     )
 
     parts = shards // 2
     count = channels // shards
     lanes = 14 * LANES
-    products = call(
-        functools.partial(products_body, peers, area),
-        [pltpu.VMEM((channels, 5 * LANES), F32)] * 3,
-        (grads, act_t),
+    grads, _, *products = call(
+        functools.partial(products_body, peers, (3, 2,), area, width),
+        [pltpu.VMEM(grads.shape, BF16), pltpu.VMEM(act_t.shape, BF16)]
+        + [pltpu.VMEM((channels, 5 * LANES), F32)] * 3,
+        (lengths, slices[3], slices[2], near_b, grads, act_t),
+        aliases={4: 0, 5: 1},
         flops=2 * 27 * 2 * peers * area * channels * LANES // 2,
     )
     keep, send = call(
@@ -389,7 +426,7 @@
     conv_out, token_a = call(
         functools.partial(ahead_body, area, width),
         [sds(block, BF16), token],
-        (lengths, own, near_x, first, second, flat),
+        (lengths, own, near_a, near_b, first, second, flat),
         after=(keep,),
         scratch=[padded],
         flops=flops,

time: 47.7 us -> 46.2 us (0.969)
  the two profiles are of different devices: /device:TPU:0 before, /device:TPU:16 now
where the time goes in v1:
time: 46.2 us; the launch traced here: 46.1 us
  starting transfers between devices  20.3 us (44%)
  Pallas kernels  13.6 us (29%)
  waiting for transfers between devices  10.7 us (23%)
  between operations  1.43 us (3%)
    pallas_call x13, Pallas kernels, call(): pl.pallas_call(with_after, out_shape=tuple(outs), in_specs=[pl.BlockSpec(...  13.6 us
    ppermute x8, starting transfers between devices, swap(): return lax.ppermute(value, axis, [(s, s ^ mask) for s in range(count)])  10.6 us
    ppermute x8, waiting for transfers between devices, swap(): return lax.ppermute(value, axis, [(s, s ^ mask) for s in range(count)])  8.44 us
    ppermute x6, starting transfers between devices, cross(): return lax.ppermute(value, ('tm', 'dp'), pairs)  8.24 us
    ppermute x6, waiting for transfers between devices, cross(): return lax.ppermute(value, ('tm', 'dp'), pairs)  2.3 us
    ppermute x1, starting transfers between devices, local(): later = lax.ppermute(cot, 'tm', [(s, s - 1) for s in range(1, peers)])  1.42 us
  transfers between devices with their start and end apart: 15, of which 6 were waited for; matrix products, arithmetic and copies ran while one was open for 0% of the time, Pallas kernels for 25%

profile of v1, /device:TPU:16, one launch (start us, length us, event | category | flops | bytes accessed | tf_op | source)
XLA Modules:
  0.0 46.1 jit_solution(11928082126787189904)
XLA Ops:
  0.6 1.6 %collective-permute-start = (bf16[512,256]{1,0:T(8,128)(2,1)}, bf16[512,256]{1,0:T(8,128)(2,1)S(1)}, u32[]{:S(2)}, u32[]{:S(2)}) collective-permute-start(bf16[512,256]{1,0:T(8,128)(2,1)} %bitcast.12), channel_id=1, source_target_pairs={{0,8},{1,17},{2,10},{3,19},{4,12},{5,21},{6,14},{7,23},{8,0},{9,25... | collective-permute-start | bytes 786440 | tf_op jit(solution)/shard_map/ppermute | solution.py:59
  2.2 1.5 %collective-permute-start.1 = (bf16[512,256]{1,0:T(8,128)(2,1)}, bf16[512,256]{1,0:T(8,128)(2,1)S(1)}, u32[]{:S(2)}, u32[]{:S(2)}) collective-permute-start(bf16[512,256]{1,0:T(8,128)(2,1)} %bitcast.13), channel_id=1, source_target_pairs={{0,16},{1,9},{2,18},{3,11},{4,20},{5,13},{6,22},{7,15},{8,24},{9,1... | collective-permute-start | bytes 786440 | tf_op jit(solution)/shard_map/ppermute | solution.py:59
  3.7 1.2 %shard_map.67 = (bf16[256,128]{1,0:T(8,128)(2,1)S(1)}, bf16[256,128]{1,0:T(8,128)(2,1)S(1)}, bf16[256,128]{1,0:T(8,128)(2,1)S(1)}, bf16[256,128]{1,0:T(8,128)(2,1)S(1)}, bf16[512,256]{1,0:T(8,128)(2,1)S(1)}) custom-call(bf16[512,256]{1,0:T(8,128)(2,1)} %bitcast.8, bf16[512,256]{1,0:T(8,128)(2,1)} %bitcast.14), custom_call_target="tpu_custom_call" | custom-call | bytes 524288 | tf_op jit(solution)/shard_map/pallas_call | solution.py:26
  4.9 0.6 %collective-permute-start.6 = (bf16[256,128]{1,0:T(8,128)(2,1)S(1)}, bf16[256,128]{1,0:T(8,128)(2,1)S(1)}, u32[]{:S(2)}, u32[]{:S(2)}) collective-permute-start(bf16[256,128]{1,0:T(8,128)(2,1)S(1)} %get-tuple-element.24), channel_id=1, source_target_pairs={{0,8},{1,17},{2,10},{3,19},{4,12},{5,21},{6,14},{7,23},{8,0},{9,25... | collective-permute-start | bytes 196616 | tf_op jit(solution)/shard_map/ppermute | solution.py:59
  5.5 1.4 %collective-permute-start.4 = (bf16[256,128]{1,0:T(8,128)(2,1)S(1)}, bf16[256,128]{1,0:T(8,128)(2,1)S(1)}, u32[]{:S(2)}, u32[]{:S(2)}) collective-permute-start(bf16[256,128]{1,0:T(8,128)(2,1)S(1)} %get-tuple-element.21), channel_id=1, source_target_pairs={{0,24},{8,16},{16,8},{24,0},{1,25},{9,17},{17,9},{25,1},{2,26},{10... | collective-permute-start | bytes 196616 | tf_op jit(solution)/shard_map/ppermute | solution.py:45
  6.9 1.5 %collective-permute-start.5 = (bf16[256,128]{1,0:T(8,128)(2,1)S(1)}, bf16[256,128]{1,0:T(8,128)(2,1)S(1)}, u32[]{:S(2)}, u32[]{:S(2)}) collective-permute-start(bf16[256,128]{1,0:T(8,128)(2,1)S(1)} %get-tuple-element.22), channel_id=1, source_target_pairs={{0,16},{1,9},{2,18},{3,11},{4,20},{5,13},{6,22},{7,15},{8,24},{9,1... | collective-permute-start | bytes 196616 | tf_op jit(solution)/shard_map/ppermute | solution.py:59
  9.1 2.3 %collective-permute-done.6.refs_2_ = bf16[256,128]{1,0:T(8,128)(2,1)S(1)} collective-permute-done((bf16[256,128]{1,0:T(8,128)(2,1)S(1)}, bf16[256,128]{1,0:T(8,128)(2,1)S(1)}, u32[]{:S(2)}, u32[]{:S(2)}) %collective-permute-start.6) | collective-permute-done | bytes 65568 | tf_op jit(solution)/shard_map/ppermute | solution.py:59
  11.4 0.4 shard_map.70.refs_4_
  11.8 1.5 %collective-permute-start.2 = (bf16[320,256]{1,0:T(8,128)(2,1)S(1)}, bf16[320,256]{1,0:T(8,128)(2,1)S(1)}, u32[]{:S(2)}, u32[]{:S(2)}) collective-permute-start(bf16[320,256]{1,0:T(8,128)(2,1)S(1)} %shard_map.68), channel_id=1, source_target_pairs={{0,16},{1,9},{2,18},{3,11},{4,20},{5,13},{6,22},{7,15},{8,24},{9,1... | collective-permute-start | bytes 491528 | tf_op jit(solution)/shard_map/ppermute | solution.py:59
  13.3 1.6 %collective-permute-start.3 = (bf16[192,256]{1,0:T(8,128)(2,1)S(1)}, bf16[192,256]{1,0:T(8,128)(2,1)S(1)}, u32[]{:S(2)}, u32[]{:S(2)}) collective-permute-start(bf16[192,256]{1,0:T(8,128)(2,1)S(1)} %shard_map.69), channel_id=1, source_target_pairs={{0,8},{1,17},{2,10},{3,19},{4,12},{5,21},{6,14},{7,23},{8,0},{9,25... | collective-permute-start | bytes 294920 | tf_op jit(solution)/shard_map/ppermute | solution.py:59
  14.9 0.2 shard_map.71.refs_5_
  15.1 2.8 %shard_map.72 = (bf16[2560,640]{1,0:T(8,128)(2,1)S(1)}, bf16[256,2048]{1,0:T(8,128)(2,1)S(1)}, f32[256,640]{1,0:T(8,128)S(1)}, f32[256,640]{1,0:T(8,128)S(1)}, f32[256,640]{1,0:T(8,128)S(1)}) custom-call(s32[1]{0:T(128)S(6)} %copy.11.refs_0_, bf16[256,128]{1,0:T(8,128)(2,1)S(1)} %collective-permute-done.4.refs_1_, ...), custom_call_target="tpu_custom_call", output_to_operand_aliasing={{0}: (4, {}), {1}: (5, {})} | custom-call | flops 1811939328 | bytes 4718596 | tf_op jit(solution)/shard_map/pallas_call | solution.py:26
  18.0 0.9 %shard_map.73 = (f32[4,32,1792]{2,1,0:T(8,128)S(1)}, bf16[4,32,1792]{2,1,0:T(8,128)(2,1)S(1)}) custom-call(bf16[2560,640]{1,0:T(8,128)(2,1)S(1)} %get-tuple-element.25.refs_0_, bf16[320,256]{1,0:T(8,128)(2,1)S(1)} %collective-permute-done.2.refs_1_.refs_4_, bf16[192,256]{1,0:T(8,128)(2,1)S(1)} %collective-permute-done.3.refs_2_.refs_5_, ...), custom_call_target="tpu_custom_call" | custom-call | flops 452984832 | bytes 5505024 | tf_op jit(solution)/shard_map/pallas_call | solution.py:26
  18.9 0.1 collective-permute-start.8
  19.0 1.4 %collective-permute-start.7 = (bf16[512,256]{1,0:T(8,128)(2,1)S(1)}, bf16[512,256]{1,0:T(8,128)(2,1)S(1)}, u32[]{:S(2)}, u32[]{:S(2)}) collective-permute-start(bf16[512,256]{1,0:T(8,128)(2,1)S(1)} %bitcast.9), channel_id=1, source_target_pairs={{8,0},{16,8},{24,16},{9,1},{17,9},{25,17},{10,2},{18,10},{26,18},{... | collective-permute-start | bytes 786440 | tf_op jit(solution)/shard_map/ppermute | solution.py:393
  20.5 0.4 collective-permute-done.8.refs_1_
  20.8 0.1 shard_map.76
  21.0 0.4 collective-permute-start.10
  21.4 2.7 %collective-permute-start.11 = (bf16[1,32,1792]{2,1,0:T(8,128)(2,1)S(1)}, bf16[1,32,1792]{2,1,0:T(8,128)(2,1)S(1)}, u32[]{:S(2)}, u32[]{:S(2)}) collective-permute-start(bf16[1,32,1792]{2,1,0:T(8,128)(2,1)S(1)} %get-tuple-element.36), channel_id=1, source_target_pairs={{0,6},{1,7},{2,4},{3,5},{4,2},{5,3},{6,0},{7,1},{8,14},{9,15},{10,... | collective-permute-start | bytes 344072 | tf_op jit(solution)/shard_map/ppermute | solution.py:45
  24.1 1.3 %collective-permute-start.9 = (bf16[1,32,1792]{2,1,0:T(8,128)(2,1)S(1)}, bf16[1,32,1792]{2,1,0:T(8,128)(2,1)S(1)}, u32[]{:S(2)}, u32[]{:S(2)}) collective-permute-start(bf16[1,32,1792]{2,1,0:T(8,128)(2,1)S(1)} %get-tuple-element.34), channel_id=1, source_target_pairs={{0,2},{1,3},{2,0},{3,1},{4,6},{5,7},{6,4},{7,5},{8,10},{9,11},{10,... | collective-permute-start | bytes 344072 | tf_op jit(solution)/shard_map/ppermute | solution.py:45
  25.4 2.8 %shard_map.74 = (bf16[512,256]{1,0:T(8,128)(2,1)}, f32[8,128]{1,0:T(8,128)S(1)}) custom-call(s32[1]{0:T(128)S(6)} %copy.11.refs_0_, bf16[512,256]{1,0:T(8,128)(2,1)S(1)} %get-tuple-element.20.refs_0_.refs_1_, bf16[512,256]{1,0:T(8,128)(2,1)S(1)} %collective-permute-done.refs_0_.refs_1_.refs_2_, bf16[512,256]{1,0:T(8,128)(2,1)S(1)} %collective-permute-done.1.refs_0_.refs_3_, ...), custom_call_target="tpu_custom_call" | custom-call | flops 1811939328 | bytes 4587524 | tf_op jit(solution)/shard_map/pallas_call | solution.py:26
  28.2 1.0 %shard_map.75.refs_4_ = bf16[9,768,256]{2,1,0:T(8,128)(2,1)S(1)} custom-call(bf16[9,768,256]{2,1,0:T(8,128)(2,1)S(1)} %bitcast.7, f32[8,128]{1,0:T(8,128)S(1)} %get-tuple-element.31.refs_1_.refs_4_), custom_call_target="tpu_custom_call" | custom-call | bytes 3538944 | tf_op jit(solution)/shard_map/pallas_call | solution.py:26
  29.2 0.7 %collective-permute-done.10.refs_2_ = bf16[1,32,1792]{2,1,0:T(8,128)(2,1)S(1)} collective-permute-done((bf16[1,32,1792]{2,1,0:T(8,128)(2,1)S(1)}, bf16[1,32,1792]{2,1,0:T(8,128)(2,1)S(1)}, u32[]{:S(2)}, u32[]{:S(2)}) %collective-permute-start.10) | collective-permute-done | bytes 114720 | tf_op jit(solution)/shard_map/ppermute | solution.py:45
  29.9 4.7 %collective-permute-done.11.refs_3_ = bf16[1,32,1792]{2,1,0:T(8,128)(2,1)S(1)} collective-permute-done((bf16[1,32,1792]{2,1,0:T(8,128)(2,1)S(1)}, bf16[1,32,1792]{2,1,0:T(8,128)(2,1)S(1)}, u32[]{:S(2)}, u32[]{:S(2)}) %collective-permute-start.11) | collective-permute-done | bytes 114720 | tf_op jit(solution)/shard_map/ppermute | solution.py:45
  34.5 0.1 shard_map.77.refs_5_.refs_0_
  34.6 2.3 %collective-permute-start.12 = (bf16[32,1792]{1,0:T(8,128)(2,1)S(1)}, bf16[32,1792]{1,0:T(8,128)(2,1)S(1)}, u32[]{:S(2)}, u32[]{:S(2)}) collective-permute-start(bf16[32,1792]{1,0:T(8,128)(2,1)S(1)} %shard_map.77.refs_5_.refs_0_), channel_id=1, source_target_pairs={{0,8},{8,0},{16,24},{24,16},{1,9},{9,1},{17,25},{25,17},{2,10},{10... | collective-permute-start | bytes 344072 | tf_op jit(solution)/shard_map/ppermute | solution.py:45
  36.9 1.0 %collective-permute-start.13 = (bf16[32,1792]{1,0:T(8,128)(2,1)S(1)}, bf16[32,1792]{1,0:T(8,128)(2,1)S(1)}, u32[]{:S(2)}, u32[]{:S(2)}) collective-permute-start(bf16[32,1792]{1,0:T(8,128)(2,1)S(1)} %shard_map.77.refs_5_.refs_0_), channel_id=1, source_target_pairs={{0,16},{8,24},{16,0},{24,8},{1,17},{9,25},{17,1},{25,9},{2,18},{10... | collective-permute-start | bytes 344072 | tf_op jit(solution)/shard_map/ppermute | solution.py:45
  37.9 1.4 %collective-permute-start.14 = (bf16[32,1792]{1,0:T(8,128)(2,1)S(1)}, bf16[32,1792]{1,0:T(8,128)(2,1)S(1)}, u32[]{:S(2)}, u32[]{:S(2)}) collective-permute-start(bf16[32,1792]{1,0:T(8,128)(2,1)S(1)} %shard_map.77.refs_5_.refs_0_), channel_id=1, source_target_pairs={{0,24},{8,16},{16,8},{24,0},{1,25},{9,17},{17,9},{25,1},{2,26},{10... | collective-permute-start | bytes 344072 | tf_op jit(solution)/shard_map/ppermute | solution.py:45
  39.3 2.8 %shard_map.78 = bf16[512,256]{1,0:T(8,128)(2,1)} custom-call(s32[1]{0:T(128)S(6)} %copy.11.refs_0_, bf16[512,256]{1,0:T(8,128)(2,1)S(1)} %get-tuple-element.20.refs_0_.refs_1_, bf16[512,256]{1,0:T(8,128)(2,1)S(1)} %bitcast.10, bf16[512,256]{1,0:T(8,128)(2,1)S(1)} %collective-permute-done.7.refs_3_, bf16[9,768,256]{2,1,0:T(8,128)(2,1)S(1)} %shard_map.75.refs_4_, ...), custom_call_target="tpu_custom_call" | custom-call | flops 1811939328 | bytes 4325380 | tf_op jit(solution)/shard_map/pallas_call | solution.py:26
  42.0 0.9 %collective-permute-done.13.refs_2_ = bf16[32,1792]{1,0:T(8,128)(2,1)S(1)} collective-permute-done((bf16[32,1792]{1,0:T(8,128)(2,1)S(1)}, bf16[32,1792]{1,0:T(8,128)(2,1)S(1)}, u32[]{:S(2)}, u32[]{:S(2)}) %collective-permute-start.13) | collective-permute-done | bytes 114720 | tf_op jit(solution)/shard_map/ppermute | solution.py:45
  42.9 1.8 %collective-permute-done.14.refs_3_ = bf16[32,1792]{1,0:T(8,128)(2,1)S(1)} collective-permute-done((bf16[32,1792]{1,0:T(8,128)(2,1)S(1)}, bf16[32,1792]{1,0:T(8,128)(2,1)S(1)}, u32[]{:S(2)}, u32[]{:S(2)}) %collective-permute-start.14) | collective-permute-done | bytes 114720 | tf_op jit(solution)/shard_map/ppermute | solution.py:45
  44.8 1.3 %shard_map.79 = f32[27,32,256]{2,1,0:T(8,128)} custom-call(bf16[32,1792]{1,0:T(8,128)(2,1)S(1)} %shard_map.77.refs_5_.refs_0_, bf16[32,1792]{1,0:T(8,128)(2,1)S(1)} %collective-permute-done.12.refs_1_, bf16[32,1792]{1,0:T(8,128)(2,1)S(1)} %collective-permute-done.13.refs_2_, bf16[32,1792]{1,0:T(8,128)(2,1)S(1)} %collective-permute-done.14.refs_3_), custom_call_target="tpu_custom_call" | custom-call | bytes 458752 | tf_op jit(solution)/shard_map/pallas_call | solution.py:26
  (15 shorter events, 0.1 us)
Async XLA Ops:
  0.6 11.1 %collective-permute-start = (bf16[512,256]{1,0:T(8,128)(2,1)}, bf16[512,256]{1,0:T(8,128)(2,1)S(1)}, u32[]{:S(2)}, u32[]{:S(2)}) collective-permute-start(bf16[512,256]{1,0:T(8,128)(2,1)} %bitcast.12), channel_id=1, source_target_pairs={{0,8},{1,17},{2,10},{3,19},{4,12},{5,21},{6,14},{7,23},{8,0},{9,25... | collective-permute-start | bytes 786440 | tf_op jit(solution)/shard_map/ppermute | solution.py:59
  2.2 11.1 %collective-permute-start.1 = (bf16[512,256]{1,0:T(8,128)(2,1)}, bf16[512,256]{1,0:T(8,128)(2,1)S(1)}, u32[]{:S(2)}, u32[]{:S(2)}) collective-permute-start(bf16[512,256]{1,0:T(8,128)(2,1)} %bitcast.13), channel_id=1, source_target_pairs={{0,16},{1,9},{2,18},{3,11},{4,20},{5,13},{6,22},{7,15},{8,24},{9,1... | collective-permute-start | bytes 786440 | tf_op jit(solution)/shard_map/ppermute | solution.py:59
  4.9 6.5 %collective-permute-start.6 = (bf16[256,128]{1,0:T(8,128)(2,1)S(1)}, bf16[256,128]{1,0:T(8,128)(2,1)S(1)}, u32[]{:S(2)}, u32[]{:S(2)}) collective-permute-start(bf16[256,128]{1,0:T(8,128)(2,1)S(1)} %get-tuple-element.24), channel_id=1, source_target_pairs={{0,8},{1,17},{2,10},{3,19},{4,12},{5,21},{6,14},{7,23},{8,0},{9,25... | collective-permute-start | bytes 196616 | tf_op jit(solution)/shard_map/ppermute | solution.py:59
  5.5 9.6 %collective-permute-start.4 = (bf16[256,128]{1,0:T(8,128)(2,1)S(1)}, bf16[256,128]{1,0:T(8,128)(2,1)S(1)}, u32[]{:S(2)}, u32[]{:S(2)}) collective-permute-start(bf16[256,128]{1,0:T(8,128)(2,1)S(1)} %get-tuple-element.21), channel_id=1, source_target_pairs={{0,24},{8,16},{16,8},{24,0},{1,25},{9,17},{17,9},{25,1},{2,26},{10... | collective-permute-start | bytes 196616 | tf_op jit(solution)/shard_map/ppermute | solution.py:45
  6.9 8.2 %collective-permute-start.5 = (bf16[256,128]{1,0:T(8,128)(2,1)S(1)}, bf16[256,128]{1,0:T(8,128)(2,1)S(1)}, u32[]{:S(2)}, u32[]{:S(2)}) collective-permute-start(bf16[256,128]{1,0:T(8,128)(2,1)S(1)} %get-tuple-element.22), channel_id=1, source_target_pairs={{0,16},{1,9},{2,18},{3,11},{4,20},{5,13},{6,22},{7,15},{8,24},{9,1... | collective-permute-start | bytes 196616 | tf_op jit(solution)/shard_map/ppermute | solution.py:59
  11.8 6.2 %collective-permute-start.2 = (bf16[320,256]{1,0:T(8,128)(2,1)S(1)}, bf16[320,256]{1,0:T(8,128)(2,1)S(1)}, u32[]{:S(2)}, u32[]{:S(2)}) collective-permute-start(bf16[320,256]{1,0:T(8,128)(2,1)S(1)} %shard_map.68), channel_id=1, source_target_pairs={{0,16},{1,9},{2,18},{3,11},{4,20},{5,13},{6,22},{7,15},{8,24},{9,1... | collective-permute-start | bytes 491528 | tf_op jit(solution)/shard_map/ppermute | solution.py:59
  13.3 4.7 %collective-permute-start.3 = (bf16[192,256]{1,0:T(8,128)(2,1)S(1)}, bf16[192,256]{1,0:T(8,128)(2,1)S(1)}, u32[]{:S(2)}, u32[]{:S(2)}) collective-permute-start(bf16[192,256]{1,0:T(8,128)(2,1)S(1)} %shard_map.69), channel_id=1, source_target_pairs={{0,8},{1,17},{2,10},{3,19},{4,12},{5,21},{6,14},{7,23},{8,0},{9,25... | collective-permute-start | bytes 294920 | tf_op jit(solution)/shard_map/ppermute | solution.py:59
  18.0 1.1 %copy-start.1 = (bf16[1,2,16,16,256]{4,3,2,1,0:T(8,128)(2,1)S(1)}, bf16[1,2,16,16,256]{4,3,2,1,0:T(8,128)(2,1)}, u32[]{:S(2)}) copy-start(bf16[1,2,16,16,256]{4,3,2,1,0:T(8,128)(2,1)} %param.5) | copy-start | bytes 786436
  18.0 7.5 %copy-start = (bf16[3,3,3,256,256]{4,3,2,1,0:T(8,128)(2,1)S(1)}, bf16[3,3,3,256,256]{4,3,2,1,0:T(8,128)(2,1)}, u32[]{:S(2)}) copy-start(bf16[3,3,3,256,256]{4,3,2,1,0:T(8,128)(2,1)} %param.6) | copy-start | bytes 10616836
  18.9 1.9 %collective-permute-start.8 = (bf16[4,32,1792]{2,1,0:T(8,128)(2,1)S(1)}, bf16[4,32,1792]{2,1,0:T(8,128)(2,1)S(1)}, u32[]{:S(2)}, u32[]{:S(2)}) collective-permute-start(bf16[4,32,1792]{2,1,0:T(8,128)(2,1)S(1)} %get-tuple-element.32), channel_id=1, source_target_pairs={{0,1},{1,0},{2,3},{3,2},{4,5},{5,4},{6,7},{7,6},{8,9},{9,8},{10,11... | collective-permute-start | bytes 1376264 | tf_op jit(solution)/shard_map/ppermute | solution.py:45
  19.0 20.2 %collective-permute-start.7 = (bf16[512,256]{1,0:T(8,128)(2,1)S(1)}, bf16[512,256]{1,0:T(8,128)(2,1)S(1)}, u32[]{:S(2)}, u32[]{:S(2)}) collective-permute-start(bf16[512,256]{1,0:T(8,128)(2,1)S(1)} %bitcast.9), channel_id=1, source_target_pairs={{8,0},{16,8},{24,16},{9,1},{17,9},{25,17},{10,2},{18,10},{26,18},{... | collective-permute-start | bytes 786440 | tf_op jit(solution)/shard_map/ppermute | solution.py:393
  21.0 8.9 %collective-permute-start.10 = (bf16[1,32,1792]{2,1,0:T(8,128)(2,1)S(1)}, bf16[1,32,1792]{2,1,0:T(8,128)(2,1)S(1)}, u32[]{:S(2)}, u32[]{:S(2)}) collective-permute-start(bf16[1,32,1792]{2,1,0:T(8,128)(2,1)S(1)} %get-tuple-element.35), channel_id=1, source_target_pairs={{0,4},{1,5},{2,6},{3,7},{4,0},{5,1},{6,2},{7,3},{8,12},{9,13},{10,... | collective-permute-start | bytes 344072 | tf_op jit(solution)/shard_map/ppermute | solution.py:45
  21.4 13.2 %collective-permute-start.11 = (bf16[1,32,1792]{2,1,0:T(8,128)(2,1)S(1)}, bf16[1,32,1792]{2,1,0:T(8,128)(2,1)S(1)}, u32[]{:S(2)}, u32[]{:S(2)}) collective-permute-start(bf16[1,32,1792]{2,1,0:T(8,128)(2,1)S(1)} %get-tuple-element.36), channel_id=1, source_target_pairs={{0,6},{1,7},{2,4},{3,5},{4,2},{5,3},{6,0},{7,1},{8,14},{9,15},{10,... | collective-permute-start | bytes 344072 | tf_op jit(solution)/shard_map/ppermute | solution.py:45
  24.1 10.5 %collective-permute-start.9 = (bf16[1,32,1792]{2,1,0:T(8,128)(2,1)S(1)}, bf16[1,32,1792]{2,1,0:T(8,128)(2,1)S(1)}, u32[]{:S(2)}, u32[]{:S(2)}) collective-permute-start(bf16[1,32,1792]{2,1,0:T(8,128)(2,1)S(1)} %get-tuple-element.34), channel_id=1, source_target_pairs={{0,2},{1,3},{2,0},{3,1},{4,6},{5,7},{6,4},{7,5},{8,10},{9,11},{10,... | collective-permute-start | bytes 344072 | tf_op jit(solution)/shard_map/ppermute | solution.py:45
  34.6 7.4 %collective-permute-start.12 = (bf16[32,1792]{1,0:T(8,128)(2,1)S(1)}, bf16[32,1792]{1,0:T(8,128)(2,1)S(1)}, u32[]{:S(2)}, u32[]{:S(2)}) collective-permute-start(bf16[32,1792]{1,0:T(8,128)(2,1)S(1)} %shard_map.77.refs_5_.refs_0_), channel_id=1, source_target_pairs={{0,8},{8,0},{16,24},{24,16},{1,9},{9,1},{17,25},{25,17},{2,10},{10... | collective-permute-start | bytes 344072 | tf_op jit(solution)/shard_map/ppermute | solution.py:45
  36.9 6.0 %collective-permute-start.13 = (bf16[32,1792]{1,0:T(8,128)(2,1)S(1)}, bf16[32,1792]{1,0:T(8,128)(2,1)S(1)}, u32[]{:S(2)}, u32[]{:S(2)}) collective-permute-start(bf16[32,1792]{1,0:T(8,128)(2,1)S(1)} %shard_map.77.refs_5_.refs_0_), channel_id=1, source_target_pairs={{0,16},{8,24},{16,0},{24,8},{1,17},{9,25},{17,1},{25,9},{2,18},{10... | collective-permute-start | bytes 344072 | tf_op jit(solution)/shard_map/ppermute | solution.py:45
  37.9 6.9 %collective-permute-start.14 = (bf16[32,1792]{1,0:T(8,128)(2,1)S(1)}, bf16[32,1792]{1,0:T(8,128)(2,1)S(1)}, u32[]{:S(2)}, u32[]{:S(2)}) collective-permute-start(bf16[32,1792]{1,0:T(8,128)(2,1)S(1)} %shard_map.77.refs_5_.refs_0_), channel_id=1, source_target_pairs={{0,24},{8,16},{16,8},{24,0},{1,25},{9,17},{17,9},{25,1},{2,26},{10... | collective-permute-start | bytes 344072 | tf_op jit(solution)/shard_map/ppermute | solution.py:45

commit v2 on v1

--- a/solution.py
+++ b/solution.py
@@ -11,10 +11,12 @@
 F32 = jnp.float32
 BF16 = jnp.bfloat16
 LANES = 128
-VMEM = pl.BlockSpec(memory_space=pltpu.VMEM)
-
-
-def call(body, outs, args, *, after=(), resident=True, scratch=(), flops=0, aliases=None):
+
+
+def call(
+    body, outs, args, *, after=(), resident=True, scratch=(), flops=0, aliases=None,
+    out_space=pltpu.VMEM,
+):
     moved = sum(a.size * a.dtype.itemsize for a in args)
     space = pltpu.VMEM if resident else pltpu.HBM
     held = [a if a.size == 1 else pltpu.with_memory_space_constraint(a, space) for a in args]
@@ -28,7 +30,7 @@
         out_shape=tuple(outs),
         in_specs=[pl.BlockSpec(memory_space=pltpu.SMEM if a.size == 1 else space) for a in args]
         + [pl.BlockSpec(memory_space=pl.ANY)] * len(after),
-        out_specs=tuple(VMEM for _ in outs),
+        out_specs=tuple(pl.BlockSpec(memory_space=out_space) for _ in outs),
         scratch_shapes=list(scratch),
         input_output_aliases=aliases or {},
         compiler_params=pltpu.CompilerParams(vmem_limit_bytes=32 << 20),
@@ -149,68 +151,92 @@
             )
 
 
-def place_grads_body(masks, area, width, length_ref, *refs):
-    slices, grads = refs[: len(masks)], refs[-1]
-    grads[grads.shape[0] - 2 * area :, :] = jnp.zeros((2 * area, grads.shape[1]), BF16)
-    for mask, ref in zip(masks, slices):
-        place_slice(area, width, length_ref, peer_block(mask), ref, grads)
-
-
 def cut_body(start, source, out_ref):
     out_ref[...] = source[start : start + out_ref.shape[0], :]
 
 
-def turn_frame(act_t, block, frame, values):
+def turn_frame(act_t, turn, frame, values):
     area = values.shape[0]
-    at = pl.multiple_of((2 * block + frame) * area, area)
-    act_t[:, pl.ds(at, area)] = jax.nn.silu(values.astype(F32)).astype(BF16).T
-
-
-def turn_blocks_body(area, *refs):
-    act_t = refs[-1]
-    me = lax.axis_index("tm")
-    for mask, ref in enumerate(refs[:-1]):
-        for frame in range(2):
-            turn_frame(act_t, peer_block(mask), frame, ref[frame * area : (frame + 1) * area, :])
-    at = pl.multiple_of(2 * (me ^ 3) * area, area)
-    act_t[:, pl.ds(at, 2 * area)] = jnp.zeros((act_t.shape[0], 2 * area), BF16)
-
-
-def products_body(peers, masks, area, width, length_ref, *refs):
-    slices, near_b = refs[: len(masks)], refs[len(masks)]
-    grads, act_t, *outs = refs[len(masks) + 3 :]
-    block = peer_block(2)
-    for mask, ref in zip(masks, slices):
-        place_slice(area, width, length_ref, peer_block(mask), ref, grads)
+    at = (2 * turn + frame) * area
+    act_t[:, at : at + area] = jax.nn.silu(values.astype(F32)).astype(BF16).T
+
+
+def turn_block(area, act_t, turn, ref):
     for frame in range(2):
-        turn_frame(act_t, block, frame, near_b[frame * area : (frame + 1) * area, :])
+        turn_frame(act_t, turn, frame, ref[frame * area : (frame + 1) * area, :])
+
+
+def own_body(area, width, length_ref, own, slice_ref, act_t, grads):
+    turn_block(area, act_t, 0, own)
+    grads[grads.shape[0] - 2 * area :, :] = jnp.zeros((2 * area, grads.shape[1]), BF16)
+    place_slice(area, width, length_ref, lax.axis_index("tm"), slice_ref, grads)
+
+
+def windows(area, grads, turn, time_tap):
+    at = pl.multiple_of((2 * peer_block(turn) + 2 - time_tap) * area, area)
+    return grads[pl.ds(at, 2 * area), :]
+
+
+def near_body(area, width, length_ref, slice_a, near_a, near_b, *refs):
+    grads, act_t = refs[2:]
+    place_slice(area, width, length_ref, peer_block(1), slice_a, grads)
+    turn_block(area, act_t, 1, near_a)
+    turn_block(area, act_t, 2, near_b)
+
+
+def products_body(area, width, length_ref, slice_b, slice_3, act_t, _, grads, *outs):
+    for turn, ref in ((2, slice_b), (3, slice_3)):
+        place_slice(area, width, length_ref, peer_block(turn), ref, grads)
     for time_tap, out in enumerate(outs):
-        used = (2 * peers - 2 + time_tap) * area
-        first = (2 - time_tap) * area
+        used = [windows(area, grads, turn, time_tap) for turn in range(3)]
         out[...] = jnp.dot(
-            act_t[:, :used], grads[first : first + used, :], preferred_element_type=F32
+            act_t[...], jnp.concatenate(used, axis=0), preferred_element_type=F32
         )
 
 
-def kernel_grad_body(area, grads, first, second, *refs):
+def sums_shape(parts, count):
+    if count % 32 == 0:
+        return (parts, 13 * count + count // 2, LANES)
+    return (parts, count, 14 * LANES)
+
+
+def put_tile(ref, part, tile, value):
+    count = value.shape[0]
+    if ref.shape[2] != LANES:
+        ref[part, :, tile * LANES : (tile + 1) * LANES] = value
+        return
+    if tile == 13:
+        low = low_half((count // 2, LANES))
+        value = jnp.where(low, value[: count // 2], half_turn(value[count // 2 :]))
+    ref[part, tile * count : tile * count + value.shape[0], :] = value
+
+
+def get_tile(ref, part, tile, count):
+    if ref.shape[2] != LANES:
+        return ref[part, :, tile * LANES : (tile + 1) * LANES]
+    if tile < 13:
+        return ref[part, tile * count : (tile + 1) * count, :]
+    value = ref[part, tile * count :, :]
+    return jnp.concatenate([value, half_turn(value)], axis=0)
+
+
+def kernel_grad_body(count, area, grads, first, second, *refs):
     held, (keep_ref, send_ref) = refs[:3], refs[3:]
-    me = lax.axis_index("tm")
     core = lax.axis_index("dp") % 2
     values = jnp.concatenate([first[...], second[...]], axis=0).astype(F32)
     turned = jax.nn.silu(values).astype(BF16).T
     sums = []
     for time_tap, ref in enumerate(held):
-        at = pl.multiple_of((2 * (me ^ 3) + 2 - time_tap) * area, area)
         sums.append(
             ref[...]
-            + jnp.dot(turned, grads[pl.ds(at, 2 * area), :], preferred_element_type=F32)
+            + jnp.dot(turned, windows(area, grads, 3, time_tap), preferred_element_type=F32)
         )
     tiles = [s[:, tile * LANES : (tile + 1) * LANES] for s in sums for tile in range(4)]
     last = [s[:, 4 * LANES :] for s in sums]
     low = low_half(last[0].shape)
     tiles.append(jnp.where(low, last[0], half_turn(last[1])))
     tiles.append(last[2])
-    parts, count = keep_ref.shape[:2]
+    parts = keep_ref.shape[0]
     groups = [
         [t[(2 * z + c) * count : (2 * z + c + 1) * count] for t in tiles]
         for z in range(parts)
@@ -222,9 +248,8 @@
         def _(own=own):
             for z in range(parts):
                 for at in range(len(tiles)):
-                    lanes = slice(at * LANES, (at + 1) * LANES)
-                    keep_ref[z, :, lanes] = groups[2 * z + own][at]
-                    send_ref[z, :, lanes] = groups[2 * z + 1 - own][at].astype(BF16)
+                    put_tile(keep_ref, z, at, groups[2 * z + own][at])
+                    put_tile(send_ref, z, at, groups[2 * z + 1 - own][at].astype(BF16))
 
 
 def sum_body(arrived, radix, step, *refs):
@@ -268,23 +293,29 @@
 
 
 def place_body(peers, scale, *refs):
-    pieces, out_ref, held = refs[:peers], refs[peers], refs[peers + 1]
-    me = lax.axis_index("tm")
-    for mask, piece in enumerate(pieces):
-        held[me ^ mask] = piece[...].astype(F32) * scale
-    low = low_half((held.shape[1], LANES))
+    pieces, out_hbm, held, placed, sems = refs[:peers], *refs[peers:]
+    for turn, piece in enumerate(pieces):
+        held[lax.axis_index("tm") ^ turn] = piece[...].astype(F32) * scale
+    count = placed.shape[1]
+    low = low_half((count, LANES))
+    copies = []
     for time_tap in range(3):
         for tap in range(9):
             tile = 4 * time_tap + tap // 2 if tap < 8 else 12 + time_tap // 2
             half = tap % 2 if tap < 8 else time_tap % 2
             for pair in range(peers // 2):
-                left = held[2 * pair, :, tile * LANES : (tile + 1) * LANES]
-                right = held[2 * pair + 1, :, tile * LANES : (tile + 1) * LANES]
+                left = get_tile(held, 2 * pair, tile, count)
+                right = get_tile(held, 2 * pair + 1, tile, count)
                 if half == 0:
                     value = jnp.where(low, left, half_turn(right))
                 else:
                     value = jnp.where(low, half_turn(left), right)
-                out_ref[9 * time_tap + tap, :, pair * LANES : (pair + 1) * LANES] = value
+                placed[9 * time_tap + tap, :, pair * LANES : (pair + 1) * LANES] = value
+        taps = pl.ds(9 * time_tap, 9)
+        copies.append(pltpu.make_async_copy(placed.at[taps], out_hbm.at[taps], sems.at[time_tap]))
+        copies[-1].start()
+    for copy in copies:
+        copy.wait()
 
 
 def fill_padded(out_ref, frame, value, width, height, direction):
@@ -298,8 +329,15 @@
         ).astype(BF16)
 
 
+def turn_taps(w_ref, out_ref, at):
+    wide = w_ref.shape[2]
+    for tap in range(3):
+        rows = slice(tap * wide, (tap + 1) * wide)
+        out_ref[at, rows, :] = w_ref[at, rows, :].T
+
+
 def ahead_body(area, width, length_ref, own, near_a, near_b, first, second, w_ref, *refs):
-    out_ref, token_ref, acts = refs
+    out_ref, token_ref, turned_ref, acts = refs
     token_ref[...] = jnp.zeros_like(token_ref)
     me = lax.axis_index("tm")
     height = area // width
@@ -318,9 +356,10 @@
         for time_tap in range(3):
             for row_tap in range(3):
                 window = acts[frame + time_tap, row_tap * width : row_tap * width + area, :]
-                total = total + jnp.dot(
-                    window, w_ref[3 * time_tap + row_tap], preferred_element_type=F32
-                )
+                at = 3 * time_tap + row_tap
+                total = total + jnp.dot(window, w_ref[at], preferred_element_type=F32)
+                if frame == 0:
+                    turn_taps(w_ref, turned_ref, at)
         out_ref[rows, :] = (total * kept(length_ref, 2 * me + frame)).astype(BF16)
 
 
@@ -349,13 +388,6 @@
         gin_ref[rows, :] = (total * slope * (keep / total_clips)).astype(BF16)
 
 
-def turn_body(w_ref, out_ref):
-    wide = w_ref.shape[2]
-    for tap in range(27):
-        rows = slice(tap % 3 * wide, (tap % 3 + 1) * wide)
-        out_ref[tap // 3, rows, :] = w_ref[tap // 3, rows, :].T
-
-
 def local(video_clips, cotangent, weight, lengths):
     clip_count, frame_count, height, width, channels = video_clips.shape
     peers, shards = lax.axis_size("tm"), lax.axis_size("dp")
@@ -383,7 +415,7 @@
     slices[1] = cross(slices[1], True)
     slices[2] = cross(slices[2], False)
     slices[3] = swap(slices[3], "tm", 3)
-    split = area + area // 4
+    split = area
     relayed = [
         call(functools.partial(cut_body, start), [pltpu.VMEM((size, channels), BF16)], (near,))[0]
         for start, size, near in ((0, split, near_a), (split, 2 * area - split, near_b))
@@ -391,31 +423,29 @@
     first = cross(relayed[0], False)
     second = cross(relayed[1], True)
     later = lax.ppermute(cot, "tm", [(s, s - 1) for s in range(1, peers)])
-    (act_t,) = call(
-        functools.partial(turn_blocks_body, area),
-        [pltpu.VMEM((channels, 2 * peers * area), BF16)],
-        (own, near_a),
-    )
-    (grads,) = call(
-        functools.partial(place_grads_body, (0, 1,), area, width),
-        [pltpu.VMEM((2 * (peers + 1) * area, 5 * LANES), BF16)],
-        (lengths, slices[0], slices[1]),
-    )
-
+    moved = pltpu.VMEM((2 * (peers + 1) * area, 5 * LANES), BF16)
+    turned_acts = pltpu.VMEM((channels, 6 * area), BF16)
+    act_t, grads = call(
+        functools.partial(own_body, area, width), [turned_acts, moved], (lengths, own, slices[0])
+    )
     parts = shards // 2
     count = channels // shards
-    lanes = 14 * LANES
-    grads, _, *products = call(
-        functools.partial(products_body, peers, (3, 2,), area, width),
-        [pltpu.VMEM(grads.shape, BF16), pltpu.VMEM(act_t.shape, BF16)]
-        + [pltpu.VMEM((channels, 5 * LANES), F32)] * 3,
-        (lengths, slices[3], slices[2], near_b, grads, act_t),
+    grads, act_t = call(
+        functools.partial(near_body, area, width),
+        [moved, turned_acts],
+        (lengths, slices[1], near_a, near_b, grads, act_t),
         aliases={4: 0, 5: 1},
+    )
+    grads, *products = call(
+        functools.partial(products_body, area, width),
+        [moved] + [pltpu.VMEM((channels, 5 * LANES), F32)] * 3,
+        (lengths, slices[2], slices[3], act_t, grads),
+        aliases={4: 0},
         flops=2 * 27 * 2 * peers * area * channels * LANES // 2,
     )
     keep, send = call(
-        functools.partial(kernel_grad_body, area),
-        [pltpu.VMEM((parts, count, lanes), F32), pltpu.VMEM((parts, count, lanes), BF16)],
+        functools.partial(kernel_grad_body, count, area),
+        [pltpu.VMEM(sums_shape(parts, count), kind) for kind in (F32, BF16)],
         (grads, first, second, *products),
         flops=2 * 27 * 2 * area * channels * LANES // 2,
     )
@@ -423,15 +453,14 @@
     token = pltpu.VMEM((8, LANES), F32)
     padded = pltpu.VMEM((4, area + 2 * width, 3 * channels), BF16)
     flops = 2 * 27 * 2 * area * channels * channels
-    conv_out, token_a = call(
+    conv_out, token_a, turned = call(
         functools.partial(ahead_body, area, width),
-        [sds(block, BF16), token],
+        [sds(block, BF16), token, pltpu.VMEM(flat.shape, BF16)],
         (lengths, own, near_a, near_b, first, second, flat),
         after=(keep,),
         scratch=[padded],
         flops=flops,
     )
-    (turned,) = call(turn_body, [pltpu.VMEM(flat.shape, BF16)], (flat,), after=(token_a,))
     piece = sum_over_clips(keep, send, (token_a,))
     (input_grad,) = call(
         functools.partial(back_body, area, width, total_clips),
@@ -446,7 +475,12 @@
         functools.partial(place_body, peers, 1.0 / total_clips),
         [sds((27, count, channels), F32)],
         pieces,
-        scratch=[pltpu.VMEM((peers, count, lanes), F32)],
+        scratch=[
+            pltpu.VMEM((peers, *piece.shape), F32),
+            pltpu.VMEM((27, count, channels), F32),
+            pltpu.SemaphoreType.DMA((3,)),
+        ],
+        out_space=pl.ANY,
     )
     shape = video_clips.shape
     weight_grad = placed.reshape(3, 3, 3, count, channels)

time: 46.2 us -> 44.3 us (0.959)
  the two profiles are of different devices: /device:TPU:16 before, /device:TPU:0 now
where the time goes in v2:
time: 44.3 us; the launch traced here: 43.5 us
  starting transfers between devices  22.3 us (50%)
  Pallas kernels  12.2 us (28%)
  waiting for transfers between devices  7.53 us (17%)
  between operations  1.41 us (3%)
    pallas_call x12, Pallas kernels, call(): pl.pallas_call(with_after, out_shape=tuple(outs), in_specs=[pl.BlockSpec(...  12.2 us
    ppermute x8, starting transfers between devices, swap(): return lax.ppermute(value, axis, [(s, s ^ mask) for s in range(count)])  11.9 us
    ppermute x6, starting transfers between devices, cross(): return lax.ppermute(value, ('tm', 'dp'), pairs)  9 us
    ppermute x8, waiting for transfers between devices, swap(): return lax.ppermute(value, axis, [(s, s ^ mask) for s in range(count)])  7.05 us
    ppermute x1, starting transfers between devices, local(): later = lax.ppermute(cot, 'tm', [(s, s - 1) for s in range(1, peers)])  1.42 us
  transfers between devices with their start and end apart: 15, of which 6 were waited for; matrix products, arithmetic and copies ran while one was open for 0% of the time, Pallas kernels for 23%

profile of v2, /device:TPU:0, one launch (start us, length us, event | category | flops | bytes accessed | tf_op | source)
XLA Modules:
  0.0 43.5 jit_solution(4320594606865904738)
XLA Ops:
  0.6 3.0 %collective-permute-start = (bf16[512,256]{1,0:T(8,128)(2,1)}, bf16[512,256]{1,0:T(8,128)(2,1)S(1)}, u32[]{:S(2)}, u32[]{:S(2)}) collective-permute-start(bf16[512,256]{1,0:T(8,128)(2,1)} %bitcast.11), channel_id=1, source_target_pairs={{0,8},{1,17},{2,10},{3,19},{4,12},{5,21},{6,14},{7,23},{8,0},{9,25... | collective-permute-start | bytes 786440 | tf_op jit(solution)/shard_map/ppermute | solution.py:61
  3.7 1.5 %collective-permute-start.1 = (bf16[512,256]{1,0:T(8,128)(2,1)}, bf16[512,256]{1,0:T(8,128)(2,1)S(1)}, u32[]{:S(2)}, u32[]{:S(2)}) collective-permute-start(bf16[512,256]{1,0:T(8,128)(2,1)} %bitcast.12), channel_id=1, source_target_pairs={{0,16},{1,9},{2,18},{3,11},{4,20},{5,13},{6,22},{7,15},{8,24},{9,1... | collective-permute-start | bytes 786440 | tf_op jit(solution)/shard_map/ppermute | solution.py:61
  5.2 1.2 %shard_map.67 = (bf16[256,128]{1,0:T(8,128)(2,1)S(1)}, bf16[256,128]{1,0:T(8,128)(2,1)S(1)}, bf16[256,128]{1,0:T(8,128)(2,1)S(1)}, bf16[256,128]{1,0:T(8,128)(2,1)S(1)}, bf16[512,256]{1,0:T(8,128)(2,1)S(1)}) custom-call(bf16[512,256]{1,0:T(8,128)(2,1)} %bitcast.6, bf16[512,256]{1,0:T(8,128)(2,1)} %bitcast.13), custom_call_target="tpu_custom_call" | custom-call | bytes 524288 | tf_op jit(solution)/shard_map/pallas_call | solution.py:28
  6.4 0.6 %collective-permute-start.6 = (bf16[256,128]{1,0:T(8,128)(2,1)S(1)}, bf16[256,128]{1,0:T(8,128)(2,1)S(1)}, u32[]{:S(2)}, u32[]{:S(2)}) collective-permute-start(bf16[256,128]{1,0:T(8,128)(2,1)S(1)} %get-tuple-element.28), channel_id=1, source_target_pairs={{0,8},{1,17},{2,10},{3,19},{4,12},{5,21},{6,14},{7,23},{8,0},{9,25... | collective-permute-start | bytes 196616 | tf_op jit(solution)/shard_map/ppermute | solution.py:61
  7.0 0.1 collective-permute-start.4
  7.0 2.9 %collective-permute-start.5 = (bf16[256,128]{1,0:T(8,128)(2,1)S(1)}, bf16[256,128]{1,0:T(8,128)(2,1)S(1)}, u32[]{:S(2)}, u32[]{:S(2)}) collective-permute-start(bf16[256,128]{1,0:T(8,128)(2,1)S(1)} %get-tuple-element.27), channel_id=1, source_target_pairs={{0,24},{8,16},{16,8},{24,0},{1,25},{9,17},{17,9},{25,1},{2,26},{10... | collective-permute-start | bytes 196616 | tf_op jit(solution)/shard_map/ppermute | solution.py:47
  10.6 0.3 shard_map.70
  10.9 2.2 %collective-permute-start.2 = (bf16[256,256]{1,0:T(8,128)(2,1)S(1)}, bf16[256,256]{1,0:T(8,128)(2,1)S(1)}, u32[]{:S(2)}, u32[]{:S(2)}) collective-permute-start(bf16[256,256]{1,0:T(8,128)(2,1)S(1)} %shard_map.68), channel_id=1, source_target_pairs={{0,16},{1,9},{2,18},{3,11},{4,20},{5,13},{6,22},{7,15},{8,24},{9,1... | collective-permute-start | bytes 393224 | tf_op jit(solution)/shard_map/ppermute | solution.py:61
  13.2 1.6 %collective-permute-start.3 = (bf16[256,256]{1,0:T(8,128)(2,1)S(1)}, bf16[256,256]{1,0:T(8,128)(2,1)S(1)}, u32[]{:S(2)}, u32[]{:S(2)}) collective-permute-start(bf16[256,256]{1,0:T(8,128)(2,1)S(1)} %shard_map.69), channel_id=1, source_target_pairs={{0,8},{1,17},{2,10},{3,19},{4,12},{5,21},{6,14},{7,23},{8,0},{9,25... | collective-permute-start | bytes 393224 | tf_op jit(solution)/shard_map/ppermute | solution.py:61
  14.7 0.4 shard_map.71
  15.2 0.2 collective-permute-done.5.refs_2_
  15.3 2.4 %shard_map.72 = (bf16[2560,640]{1,0:T(8,128)(2,1)S(1)}, f32[256,640]{1,0:T(8,128)S(1)}, f32[256,640]{1,0:T(8,128)S(1)}, f32[256,640]{1,0:T(8,128)S(1)}) custom-call(s32[1]{0:T(128)S(6)} %copy.13.refs_0_, bf16[256,128]{1,0:T(8,128)(2,1)S(1)} %collective-permute-done.4.refs_1_, ...), custom_call_target="tpu_custom_call", output_to_operand_aliasing={{0}: (4, {})} | custom-call | flops 1811939328 | bytes 4194308 | tf_op jit(solution)/shard_map/pallas_call | solution.py:28
  17.7 0.0 copy-start
  17.7 0.5 %collective-permute-done.3.refs_2_.refs_5_ = bf16[256,256]{1,0:T(8,128)(2,1)S(1)} collective-permute-done((bf16[256,256]{1,0:T(8,128)(2,1)S(1)}, bf16[256,256]{1,0:T(8,128)(2,1)S(1)}, u32[]{:S(2)}, u32[]{:S(2)}) %collective-permute-start.3) | collective-permute-done | bytes 131104 | tf_op jit(solution)/shard_map/ppermute | solution.py:61
  18.2 0.9 %shard_map.73 = (f32[4,432,128]{2,1,0:T(8,128)S(1)}, bf16[4,432,128]{2,1,0:T(8,128)(2,1)S(1)}) custom-call(bf16[2560,640]{1,0:T(8,128)(2,1)S(1)} %get-tuple-element.34.refs_0_, bf16[256,256]{1,0:T(8,128)(2,1)S(1)} %collective-permute-done.2.refs_1_.refs_4_, bf16[256,256]{1,0:T(8,128)(2,1)S(1)} %collective-permute-done.3.refs_2_.refs_5_, ...), custom_call_target="tpu_custom_call" | custom-call | flops 452984832 | bytes 5505024 | tf_op jit(solution)/shard_map/pallas_call | solution.py:28
  19.2 0.1 collective-permute-start.8
  19.2 1.4 %collective-permute-start.7 = (bf16[512,256]{1,0:T(8,128)(2,1)S(1)}, bf16[512,256]{1,0:T(8,128)(2,1)S(1)}, u32[]{:S(2)}, u32[]{:S(2)}) collective-permute-start(bf16[512,256]{1,0:T(8,128)(2,1)S(1)} %bitcast.7), channel_id=1, source_target_pairs={{8,0},{16,8},{24,16},{9,1},{17,9},{25,17},{10,2},{18,10},{26,18},{... | collective-permute-start | bytes 786440 | tf_op jit(solution)/shard_map/ppermute | solution.py:425
  20.7 0.3 collective-permute-done.8.refs_1_
  21.0 0.1 shard_map.75
  21.2 2.7 %collective-permute-start.10 = (bf16[1,432,128]{2,1,0:T(8,128)(2,1)S(1)}, bf16[1,432,128]{2,1,0:T(8,128)(2,1)S(1)}, u32[]{:S(2)}, u32[]{:S(2)}) collective-permute-start(bf16[1,432,128]{2,1,0:T(8,128)(2,1)S(1)} %get-tuple-element.44), channel_id=1, source_target_pairs={{0,4},{1,5},{2,6},{3,7},{4,0},{5,1},{6,2},{7,3},{8,12},{9,13},{10,... | collective-permute-start | bytes 331784 | tf_op jit(solution)/shard_map/ppermute | solution.py:47
  23.8 1.3 %collective-permute-start.11 = (bf16[1,432,128]{2,1,0:T(8,128)(2,1)S(1)}, bf16[1,432,128]{2,1,0:T(8,128)(2,1)S(1)}, u32[]{:S(2)}, u32[]{:S(2)}) collective-permute-start(bf16[1,432,128]{2,1,0:T(8,128)(2,1)S(1)} %get-tuple-element.45), channel_id=1, source_target_pairs={{0,6},{1,7},{2,4},{3,5},{4,2},{5,3},{6,0},{7,1},{8,14},{9,15},{10,... | collective-permute-start | bytes 331784 | tf_op jit(solution)/shard_map/ppermute | solution.py:47
  25.2 0.2 collective-permute-start.9
  25.4 2.8 %shard_map.74 = (bf16[512,256]{1,0:T(8,128)(2,1)}, f32[8,128]{1,0:T(8,128)S(1)}, bf16[9,768,256]{2,1,0:T(8,128)(2,1)S(1)}) custom-call(s32[1]{0:T(128)S(6)} %copy.13.refs_0_, bf16[512,256]{1,0:T(8,128)(2,1)S(1)} %get-tuple-element.25.refs_1_, bf16[512,256]{1,0:T(8,128)(2,1)S(1)} %collective-permute-done.refs_0_.refs_2_, ...), custom_call_target="tpu_custom_call" | custom-call | flops 1811939328 | bytes 4587524 | tf_op jit(solution)/shard_map/pallas_call | solution.py:28
  28.2 4.6 %collective-permute-done.10.refs_2_ = bf16[1,432,128]{2,1,0:T(8,128)(2,1)S(1)} collective-permute-done((bf16[1,432,128]{2,1,0:T(8,128)(2,1)S(1)}, bf16[1,432,128]{2,1,0:T(8,128)(2,1)S(1)}, u32[]{:S(2)}, u32[]{:S(2)}) %collective-permute-start.10) | collective-permute-done | bytes 110624 | tf_op jit(solution)/shard_map/ppermute | solution.py:47
  32.8 0.5 %collective-permute-done.9.refs_1_ = bf16[1,432,128]{2,1,0:T(8,128)(2,1)S(1)} collective-permute-done((bf16[1,432,128]{2,1,0:T(8,128)(2,1)S(1)}, bf16[1,432,128]{2,1,0:T(8,128)(2,1)S(1)}, u32[]{:S(2)}, u32[]{:S(2)}) %collective-permute-start.9) | collective-permute-done | bytes 110624 | tf_op jit(solution)/shard_map/ppermute | solution.py:47
  33.4 0.1 shard_map.76.refs_5_.refs_0_
  33.4 2.3 %collective-permute-start.12 = (bf16[432,128]{1,0:T(8,128)(2,1)S(1)}, bf16[432,128]{1,0:T(8,128)(2,1)S(1)}, u32[]{:S(2)}, u32[]{:S(2)}) collective-permute-start(bf16[432,128]{1,0:T(8,128)(2,1)S(1)} %shard_map.76.refs_5_.refs_0_), channel_id=1, source_target_pairs={{0,8},{8,0},{16,24},{24,16},{1,9},{9,1},{17,25},{25,17},{2,10},{10... | collective-permute-start | bytes 331784 | tf_op jit(solution)/shard_map/ppermute | solution.py:47
  35.7 1.0 %collective-permute-start.13 = (bf16[432,128]{1,0:T(8,128)(2,1)S(1)}, bf16[432,128]{1,0:T(8,128)(2,1)S(1)}, u32[]{:S(2)}, u32[]{:S(2)}) collective-permute-start(bf16[432,128]{1,0:T(8,128)(2,1)S(1)} %shard_map.76.refs_5_.refs_0_), channel_id=1, source_target_pairs={{0,16},{8,24},{16,0},{24,8},{1,17},{9,25},{17,1},{25,9},{2,18},{10... | collective-permute-start | bytes 331784 | tf_op jit(solution)/shard_map/ppermute | solution.py:47
  36.7 1.4 %collective-permute-start.14 = (bf16[432,128]{1,0:T(8,128)(2,1)S(1)}, bf16[432,128]{1,0:T(8,128)(2,1)S(1)}, u32[]{:S(2)}, u32[]{:S(2)}) collective-permute-start(bf16[432,128]{1,0:T(8,128)(2,1)S(1)} %shard_map.76.refs_5_.refs_0_), channel_id=1, source_target_pairs={{0,24},{8,16},{16,8},{24,0},{1,25},{9,17},{17,9},{25,1},{2,26},{10... | collective-permute-start | bytes 331784 | tf_op jit(solution)/shard_map/ppermute | solution.py:47
  38.1 2.8 %shard_map.77 = bf16[512,256]{1,0:T(8,128)(2,1)} custom-call(s32[1]{0:T(128)S(6)} %copy.13.refs_0_, bf16[512,256]{1,0:T(8,128)(2,1)S(1)} %get-tuple-element.25.refs_1_, bf16[512,256]{1,0:T(8,128)(2,1)S(1)} %bitcast.8, bf16[512,256]{1,0:T(8,128)(2,1)S(1)} %collective-permute-done.7.refs_3_, bf16[9,768,256]{2,1,0:T(8,128)(2,1)S(1)} %get-tuple-element.40.refs_4_, ...), custom_call_target="tpu_custom_call" | custom-call | flops 1811939328 | bytes 4325380 | tf_op jit(solution)/shard_map/pallas_call | solution.py:28
  41.0 1.4 %collective-permute-done.14.refs_3_ = bf16[432,128]{1,0:T(8,128)(2,1)S(1)} collective-permute-done((bf16[432,128]{1,0:T(8,128)(2,1)S(1)}, bf16[432,128]{1,0:T(8,128)(2,1)S(1)}, u32[]{:S(2)}, u32[]{:S(2)}) %collective-permute-start.14) | collective-permute-done | bytes 110624 | tf_op jit(solution)/shard_map/ppermute | solution.py:47
  42.4 1.1 %shard_map.78 = f32[27,32,256]{2,1,0:T(8,128)} custom-call(bf16[432,128]{1,0:T(8,128)(2,1)S(1)} %shard_map.76.refs_5_.refs_0_, bf16[432,128]{1,0:T(8,128)(2,1)S(1)} %collective-permute-done.12.refs_1_, bf16[432,128]{1,0:T(8,128)(2,1)S(1)} %collective-permute-done.13.refs_2_, bf16[432,128]{1,0:T(8,128)(2,1)S(1)} %collective-permute-done.14.refs_3_), custom_call_target="tpu_custom_call" | custom-call | bytes 442368 | tf_op jit(solution)/shard_map/pallas_call | solution.py:28
  (14 shorter events, 0.0 us)
Async XLA Ops:
  0.6 10.3 %collective-permute-start = (bf16[512,256]{1,0:T(8,128)(2,1)}, bf16[512,256]{1,0:T(8,128)(2,1)S(1)}, u32[]{:S(2)}, u32[]{:S(2)}) collective-permute-start(bf16[512,256]{1,0:T(8,128)(2,1)} %bitcast.11), channel_id=1, source_target_pairs={{0,8},{1,17},{2,10},{3,19},{4,12},{5,21},{6,14},{7,23},{8,0},{9,25... | collective-permute-start | bytes 786440 | tf_op jit(solution)/shard_map/ppermute | solution.py:61
  3.7 9.5 %collective-permute-start.1 = (bf16[512,256]{1,0:T(8,128)(2,1)}, bf16[512,256]{1,0:T(8,128)(2,1)S(1)}, u32[]{:S(2)}, u32[]{:S(2)}) collective-permute-start(bf16[512,256]{1,0:T(8,128)(2,1)} %bitcast.12), channel_id=1, source_target_pairs={{0,16},{1,9},{2,18},{3,11},{4,20},{5,13},{6,22},{7,15},{8,24},{9,1... | collective-permute-start | bytes 786440 | tf_op jit(solution)/shard_map/ppermute | solution.py:61
  6.4 8.4 %collective-permute-start.6 = (bf16[256,128]{1,0:T(8,128)(2,1)S(1)}, bf16[256,128]{1,0:T(8,128)(2,1)S(1)}, u32[]{:S(2)}, u32[]{:S(2)}) collective-permute-start(bf16[256,128]{1,0:T(8,128)(2,1)S(1)} %get-tuple-element.28), channel_id=1, source_target_pairs={{0,8},{1,17},{2,10},{3,19},{4,12},{5,21},{6,14},{7,23},{8,0},{9,25... | collective-permute-start | bytes 196616 | tf_op jit(solution)/shard_map/ppermute | solution.py:61
  7.0 8.2 %collective-permute-start.4 = (bf16[256,128]{1,0:T(8,128)(2,1)S(1)}, bf16[256,128]{1,0:T(8,128)(2,1)S(1)}, u32[]{:S(2)}, u32[]{:S(2)}) collective-permute-start(bf16[256,128]{1,0:T(8,128)(2,1)S(1)} %get-tuple-element.26), channel_id=1, source_target_pairs={{0,16},{1,9},{2,18},{3,11},{4,20},{5,13},{6,22},{7,15},{8,24},{9,1... | collective-permute-start | bytes 196616 | tf_op jit(solution)/shard_map/ppermute | solution.py:61
  7.0 8.3 %collective-permute-start.5 = (bf16[256,128]{1,0:T(8,128)(2,1)S(1)}, bf16[256,128]{1,0:T(8,128)(2,1)S(1)}, u32[]{:S(2)}, u32[]{:S(2)}) collective-permute-start(bf16[256,128]{1,0:T(8,128)(2,1)S(1)} %get-tuple-element.27), channel_id=1, source_target_pairs={{0,24},{8,16},{16,8},{24,0},{1,25},{9,17},{17,9},{25,1},{2,26},{10... | collective-permute-start | bytes 196616 | tf_op jit(solution)/shard_map/ppermute | solution.py:47
  10.9 6.8 %collective-permute-start.2 = (bf16[256,256]{1,0:T(8,128)(2,1)S(1)}, bf16[256,256]{1,0:T(8,128)(2,1)S(1)}, u32[]{:S(2)}, u32[]{:S(2)}) collective-permute-start(bf16[256,256]{1,0:T(8,128)(2,1)S(1)} %shard_map.68), channel_id=1, source_target_pairs={{0,16},{1,9},{2,18},{3,11},{4,20},{5,13},{6,22},{7,15},{8,24},{9,1... | collective-permute-start | bytes 393224 | tf_op jit(solution)/shard_map/ppermute | solution.py:61
  13.2 5.0 %collective-permute-start.3 = (bf16[256,256]{1,0:T(8,128)(2,1)S(1)}, bf16[256,256]{1,0:T(8,128)(2,1)S(1)}, u32[]{:S(2)}, u32[]{:S(2)}) collective-permute-start(bf16[256,256]{1,0:T(8,128)(2,1)S(1)} %shard_map.69), channel_id=1, source_target_pairs={{0,8},{1,17},{2,10},{3,19},{4,12},{5,21},{6,14},{7,23},{8,0},{9,25... | collective-permute-start | bytes 393224 | tf_op jit(solution)/shard_map/ppermute | solution.py:61
  17.7 1.5 %copy-start = (bf16[1,2,16,16,256]{4,3,2,1,0:T(8,128)(2,1)S(1)}, bf16[1,2,16,16,256]{4,3,2,1,0:T(8,128)(2,1)}, u32[]{:S(2)}) copy-start(bf16[1,2,16,16,256]{4,3,2,1,0:T(8,128)(2,1)} %param.5) | copy-start | bytes 786436
  18.2 7.2 %copy-start.1 = (bf16[3,3,3,256,256]{4,3,2,1,0:T(8,128)(2,1)S(1)}, bf16[3,3,3,256,256]{4,3,2,1,0:T(8,128)(2,1)}, u32[]{:S(2)}) copy-start(bf16[3,3,3,256,256]{4,3,2,1,0:T(8,128)(2,1)} %param.6) | copy-start | bytes 10616836
  19.2 1.9 %collective-permute-start.8 = (bf16[4,432,128]{2,1,0:T(8,128)(2,1)S(1)}, bf16[4,432,128]{2,1,0:T(8,128)(2,1)S(1)}, u32[]{:S(2)}, u32[]{:S(2)}) collective-permute-start(bf16[4,432,128]{2,1,0:T(8,128)(2,1)S(1)} %get-tuple-element.41), channel_id=1, source_target_pairs={{0,1},{1,0},{2,3},{3,2},{4,5},{5,4},{6,7},{7,6},{8,9},{9,8},{10,11... | collective-permute-start | bytes 1327112 | tf_op jit(solution)/shard_map/ppermute | solution.py:47
  19.2 18.9 %collective-permute-start.7 = (bf16[512,256]{1,0:T(8,128)(2,1)S(1)}, bf16[512,256]{1,0:T(8,128)(2,1)S(1)}, u32[]{:S(2)}, u32[]{:S(2)}) collective-permute-start(bf16[512,256]{1,0:T(8,128)(2,1)S(1)} %bitcast.7), channel_id=1, source_target_pairs={{8,0},{16,8},{24,16},{9,1},{17,9},{25,17},{10,2},{18,10},{26,18},{... | collective-permute-start | bytes 786440 | tf_op jit(solution)/shard_map/ppermute | solution.py:425
  21.2 11.7 %collective-permute-start.10 = (bf16[1,432,128]{2,1,0:T(8,128)(2,1)S(1)}, bf16[1,432,128]{2,1,0:T(8,128)(2,1)S(1)}, u32[]{:S(2)}, u32[]{:S(2)}) collective-permute-start(bf16[1,432,128]{2,1,0:T(8,128)(2,1)S(1)} %get-tuple-element.44), channel_id=1, source_target_pairs={{0,4},{1,5},{2,6},{3,7},{4,0},{5,1},{6,2},{7,3},{8,12},{9,13},{10,... | collective-permute-start | bytes 331784 | tf_op jit(solution)/shard_map/ppermute | solution.py:47
  23.8 9.0 %collective-permute-start.11 = (bf16[1,432,128]{2,1,0:T(8,128)(2,1)S(1)}, bf16[1,432,128]{2,1,0:T(8,128)(2,1)S(1)}, u32[]{:S(2)}, u32[]{:S(2)}) collective-permute-start(bf16[1,432,128]{2,1,0:T(8,128)(2,1)S(1)} %get-tuple-element.45), channel_id=1, source_target_pairs={{0,6},{1,7},{2,4},{3,5},{4,2},{5,3},{6,0},{7,1},{8,14},{9,15},{10,... | collective-permute-start | bytes 331784 | tf_op jit(solution)/shard_map/ppermute | solution.py:47
  25.2 8.2 %collective-permute-start.9 = (bf16[1,432,128]{2,1,0:T(8,128)(2,1)S(1)}, bf16[1,432,128]{2,1,0:T(8,128)(2,1)S(1)}, u32[]{:S(2)}, u32[]{:S(2)}) collective-permute-start(bf16[1,432,128]{2,1,0:T(8,128)(2,1)S(1)} %get-tuple-element.43), channel_id=1, source_target_pairs={{0,2},{1,3},{2,0},{3,1},{4,6},{5,7},{6,4},{7,5},{8,10},{9,11},{10,... | collective-permute-start | bytes 331784 | tf_op jit(solution)/shard_map/ppermute | solution.py:47
  33.4 7.5 %collective-permute-start.12 = (bf16[432,128]{1,0:T(8,128)(2,1)S(1)}, bf16[432,128]{1,0:T(8,128)(2,1)S(1)}, u32[]{:S(2)}, u32[]{:S(2)}) collective-permute-start(bf16[432,128]{1,0:T(8,128)(2,1)S(1)} %shard_map.76.refs_5_.refs_0_), channel_id=1, source_target_pairs={{0,8},{8,0},{16,24},{24,16},{1,9},{9,1},{17,25},{25,17},{2,10},{10... | collective-permute-start | bytes 331784 | tf_op jit(solution)/shard_map/ppermute | solution.py:47
  35.7 5.2 %collective-permute-start.13 = (bf16[432,128]{1,0:T(8,128)(2,1)S(1)}, bf16[432,128]{1,0:T(8,128)(2,1)S(1)}, u32[]{:S(2)}, u32[]{:S(2)}) collective-permute-start(bf16[432,128]{1,0:T(8,128)(2,1)S(1)} %shard_map.76.refs_5_.refs_0_), channel_id=1, source_target_pairs={{0,16},{8,24},{16,0},{24,8},{1,17},{9,25},{17,1},{25,9},{2,18},{10... | collective-permute-start | bytes 331784 | tf_op jit(solution)/shard_map/ppermute | solution.py:47
  36.7 5.6 %collective-permute-start.14 = (bf16[432,128]{1,0:T(8,128)(2,1)S(1)}, bf16[432,128]{1,0:T(8,128)(2,1)S(1)}, u32[]{:S(2)}, u32[]{:S(2)}) collective-permute-start(bf16[432,128]{1,0:T(8,128)(2,1)S(1)} %shard_map.76.refs_5_.refs_0_), channel_id=1, source_target_pairs={{0,24},{8,16},{16,8},{24,0},{1,25},{9,17},{17,9},{25,1},{2,26},{10... | collective-permute-start | bytes 331784 | tf_op jit(solution)/shard_map/ppermute | solution.py:47

commit v3 on v2

--- a/solution.py
+++ b/solution.py
@@ -220,36 +220,49 @@
     return jnp.concatenate([value, half_turn(value)], axis=0)
 
 
-def kernel_grad_body(count, area, grads, first, second, *refs):
-    held, (keep_ref, send_ref) = refs[:3], refs[3:]
-    core = lax.axis_index("dp") % 2
-    values = jnp.concatenate([first[...], second[...]], axis=0).astype(F32)
-    turned = jax.nn.silu(values).astype(BF16).T
+def rows_for(ref, parts, count, core):
+    if count % 32 == 0:
+        found = [
+            ref[pl.ds(pl.multiple_of((2 * z + core) * count, count), count), :]
+            for z in range(parts)
+        ]
+        return jnp.concatenate(found, axis=0)
+    full = ref[...].astype(F32)
+    groups = [full[at * count : (at + 1) * count] for at in range(2 * parts)]
+    found = [jnp.where(core == 0, groups[2 * z], groups[2 * z + 1]) for z in range(parts)]
+    return jnp.concatenate(found, axis=0).astype(ref.dtype)
+
+
+def core_sums(count, area, core, grads, turned, products, out_ref):
+    parts = out_ref.shape[0]
+    acts = rows_for(turned, parts, count, core)
     sums = []
-    for time_tap, ref in enumerate(held):
+    for time_tap, ref in enumerate(products):
         sums.append(
-            ref[...]
-            + jnp.dot(turned, windows(area, grads, 3, time_tap), preferred_element_type=F32)
+            rows_for(ref, parts, count, core)
+            + jnp.dot(acts, windows(area, grads, 3, time_tap), preferred_element_type=F32)
         )
     tiles = [s[:, tile * LANES : (tile + 1) * LANES] for s in sums for tile in range(4)]
     last = [s[:, 4 * LANES :] for s in sums]
     low = low_half(last[0].shape)
     tiles.append(jnp.where(low, last[0], half_turn(last[1])))
     tiles.append(last[2])
-    parts = keep_ref.shape[0]
-    groups = [
-        [t[(2 * z + c) * count : (2 * z + c + 1) * count] for t in tiles]
-        for z in range(parts)
-        for c in range(2)
-    ]
-    for own in range(2):
-
-        @pl.when(core == own)
-        def _(own=own):
-            for z in range(parts):
-                for at in range(len(tiles)):
-                    put_tile(keep_ref, z, at, groups[2 * z + own][at])
-                    put_tile(send_ref, z, at, groups[2 * z + 1 - own][at].astype(BF16))
+    for part in range(parts):
+        for at, tile in enumerate(tiles):
+            value = tile[part * count : (part + 1) * count]
+            put_tile(out_ref, part, at, value.astype(out_ref.dtype))
+
+
+def send_body(count, area, grads, first, second, *refs):
+    products, (send_ref, turned) = refs[:3], refs[3:]
+    values = jnp.concatenate([first[...], second[...]], axis=0).astype(F32)
+    turned[...] = jax.nn.silu(values).astype(BF16).T
+    other = 1 - lax.axis_index("dp") % 2
+    core_sums(count, area, other, grads, turned, products, send_ref)
+
+
+def keep_body(count, area, grads, turned, *refs):
+    core_sums(count, area, lax.axis_index("dp") % 2, grads, turned, refs[:3], refs[3])
 
 
 def sum_body(arrived, radix, step, *refs):
@@ -443,11 +456,19 @@
         aliases={4: 0},
         flops=2 * 27 * 2 * peers * area * channels * LANES // 2,
     )
-    keep, send = call(
-        functools.partial(kernel_grad_body, count, area),
-        [pltpu.VMEM(sums_shape(parts, count), kind) for kind in (F32, BF16)],
+    half = 27 * 2 * area * channels * LANES // 2
+    send, last_turned = call(
+        functools.partial(send_body, count, area),
+        [pltpu.VMEM(sums_shape(parts, count), BF16), pltpu.VMEM((channels, 2 * area), BF16)],
         (grads, first, second, *products),
-        flops=2 * 27 * 2 * area * channels * LANES // 2,
+        flops=half,
+    )
+    (keep,) = call(
+        functools.partial(keep_body, count, area),
+        [pltpu.VMEM(sums_shape(parts, count), F32)],
+        (grads, last_turned, *products),
+        after=(send,),
+        flops=half,
     )
     flat = weight.reshape(9, 3 * channels, channels)
     token = pltpu.VMEM((8, LANES), F32)

time: 44.3 us -> 44.5 us (level)
    pallas_call x12 -> x13, Pallas kernels: 12.2 us -> 12.5 us  [call(): pl.pallas_call(with_after, out_shape=tuple(outs), in_specs=[pl.BlockSpec(...]
  transfers between devices with their start and end apart: 15 -> 15, of which waited for: 6 -> 5; matrix products, arithmetic and copies ran while one was open for 0% -> 0% of each run, Pallas kernels for 23% -> 25%
where the time goes in v3:
time: 44.5 us; the launch traced here: 43.7 us
  starting transfers between devices  22.3 us (50%)
  Pallas kernels  12.5 us (28%)
  waiting for transfers between devices  7.54 us (17%)
  between operations  1.41 us (3%)
    pallas_call x13, Pallas kernels, call(): pl.pallas_call(with_after, out_shape=tuple(outs), in_specs=[pl.BlockSpec(...  12.5 us
    ppermute x8, starting transfers between devices, swap(): return lax.ppermute(value, axis, [(s, s ^ mask) for s in range(count)])  12 us
    ppermute x6, starting transfers between devices, cross(): return lax.ppermute(value, ('tm', 'dp'), pairs)  9 us
    ppermute x8, waiting for transfers between devices, swap(): return lax.ppermute(value, axis, [(s, s ^ mask) for s in range(count)])  7.06 us
    ppermute x1, starting transfers between devices, local(): later = lax.ppermute(cot, 'tm', [(s, s - 1) for s in range(1, peers)])  1.29 us
  transfers between devices with their start and end apart: 15, of which 5 were waited for; matrix products, arithmetic and copies ran while one was open for 0% of the time, Pallas kernels for 25%

profile of v3, /device:TPU:0, one launch (start us, length us, event | category | flops | bytes accessed | tf_op | source)
XLA Modules:
  0.0 43.7 jit_solution(5023647783509859685)
XLA Ops:
  0.6 3.0 %collective-permute-start = (bf16[512,256]{1,0:T(8,128)(2,1)}, bf16[512,256]{1,0:T(8,128)(2,1)S(1)}, u32[]{:S(2)}, u32[]{:S(2)}) collective-permute-start(bf16[512,256]{1,0:T(8,128)(2,1)} %bitcast.11), channel_id=1, source_target_pairs={{0,8},{1,17},{2,10},{3,19},{4,12},{5,21},{6,14},{7,23},{8,0},{9,25... | collective-permute-start | bytes 786440 | tf_op jit(solution)/shard_map/ppermute | solution.py:61
  3.7 1.5 %collective-permute-start.1 = (bf16[512,256]{1,0:T(8,128)(2,1)}, bf16[512,256]{1,0:T(8,128)(2,1)S(1)}, u32[]{:S(2)}, u32[]{:S(2)}) collective-permute-start(bf16[512,256]{1,0:T(8,128)(2,1)} %bitcast.12), channel_id=1, source_target_pairs={{0,16},{1,9},{2,18},{3,11},{4,20},{5,13},{6,22},{7,15},{8,24},{9,1... | collective-permute-start | bytes 786440 | tf_op jit(solution)/shard_map/ppermute | solution.py:61
  5.2 1.2 %shard_map.67 = (bf16[256,128]{1,0:T(8,128)(2,1)S(1)}, bf16[256,128]{1,0:T(8,128)(2,1)S(1)}, bf16[256,128]{1,0:T(8,128)(2,1)S(1)}, bf16[256,128]{1,0:T(8,128)(2,1)S(1)}, bf16[512,256]{1,0:T(8,128)(2,1)S(1)}) custom-call(bf16[512,256]{1,0:T(8,128)(2,1)} %bitcast.6, bf16[512,256]{1,0:T(8,128)(2,1)} %bitcast.13), custom_call_target="tpu_custom_call" | custom-call | bytes 524288 | tf_op jit(solution)/shard_map/pallas_call | solution.py:28
  6.4 0.6 %collective-permute-start.6 = (bf16[256,128]{1,0:T(8,128)(2,1)S(1)}, bf16[256,128]{1,0:T(8,128)(2,1)S(1)}, u32[]{:S(2)}, u32[]{:S(2)}) collective-permute-start(bf16[256,128]{1,0:T(8,128)(2,1)S(1)} %get-tuple-element.28), channel_id=1, source_target_pairs={{0,8},{1,17},{2,10},{3,19},{4,12},{5,21},{6,14},{7,23},{8,0},{9,25... | collective-permute-start | bytes 196616 | tf_op jit(solution)/shard_map/ppermute | solution.py:61
  7.0 0.1 collective-permute-start.4
  7.0 2.9 %collective-permute-start.5 = (bf16[256,128]{1,0:T(8,128)(2,1)S(1)}, bf16[256,128]{1,0:T(8,128)(2,1)S(1)}, u32[]{:S(2)}, u32[]{:S(2)}) collective-permute-start(bf16[256,128]{1,0:T(8,128)(2,1)S(1)} %get-tuple-element.27), channel_id=1, source_target_pairs={{0,24},{8,16},{16,8},{24,0},{1,25},{9,17},{17,9},{25,1},{2,26},{10... | collective-permute-start | bytes 196616 | tf_op jit(solution)/shard_map/ppermute | solution.py:47
  10.6 0.3 shard_map.70
  10.9 2.2 %collective-permute-start.2 = (bf16[256,256]{1,0:T(8,128)(2,1)S(1)}, bf16[256,256]{1,0:T(8,128)(2,1)S(1)}, u32[]{:S(2)}, u32[]{:S(2)}) collective-permute-start(bf16[256,256]{1,0:T(8,128)(2,1)S(1)} %shard_map.68), channel_id=1, source_target_pairs={{0,16},{1,9},{2,18},{3,11},{4,20},{5,13},{6,22},{7,15},{8,24},{9,1... | collective-permute-start | bytes 393224 | tf_op jit(solution)/shard_map/ppermute | solution.py:61
  13.2 1.6 %collective-permute-start.3 = (bf16[256,256]{1,0:T(8,128)(2,1)S(1)}, bf16[256,256]{1,0:T(8,128)(2,1)S(1)}, u32[]{:S(2)}, u32[]{:S(2)}) collective-permute-start(bf16[256,256]{1,0:T(8,128)(2,1)S(1)} %shard_map.69), channel_id=1, source_target_pairs={{0,8},{1,17},{2,10},{3,19},{4,12},{5,21},{6,14},{7,23},{8,0},{9,25... | collective-permute-start | bytes 393224 | tf_op jit(solution)/shard_map/ppermute | solution.py:61
  14.7 0.4 shard_map.71
  15.2 0.2 collective-permute-done.5.refs_2_
  15.3 2.4 %shard_map.72 = (bf16[2560,640]{1,0:T(8,128)(2,1)S(1)}, f32[256,640]{1,0:T(8,128)S(1)}, f32[256,640]{1,0:T(8,128)S(1)}, f32[256,640]{1,0:T(8,128)S(1)}) custom-call(s32[1]{0:T(128)S(6)} %copy.13.refs_0_, bf16[256,128]{1,0:T(8,128)(2,1)S(1)} %collective-permute-done.4.refs_1_, ...), custom_call_target="tpu_custom_call", output_to_operand_aliasing={{0}: (4, {})} | custom-call | flops 1811939328 | bytes 4194308 | tf_op jit(solution)/shard_map/pallas_call | solution.py:28
  17.7 0.0 copy-start
  17.7 0.5 %collective-permute-done.3.refs_2_.refs_5_ = bf16[256,256]{1,0:T(8,128)(2,1)S(1)} collective-permute-done((bf16[256,256]{1,0:T(8,128)(2,1)S(1)}, bf16[256,256]{1,0:T(8,128)(2,1)S(1)}, u32[]{:S(2)}, u32[]{:S(2)}) %collective-permute-start.3) | collective-permute-done | bytes 131104 | tf_op jit(solution)/shard_map/ppermute | solution.py:61
  18.2 0.6 %shard_map.73 = (bf16[4,432,128]{2,1,0:T(8,128)(2,1)S(1)}, bf16[256,512]{1,0:T(8,128)(2,1)S(1)}) custom-call(bf16[2560,640]{1,0:T(8,128)(2,1)S(1)} %get-tuple-element.34.refs_0_, bf16[256,256]{1,0:T(8,128)(2,1)S(1)} %collective-permute-done.2.refs_1_.refs_4_, bf16[256,256]{1,0:T(8,128)(2,1)S(1)} %collective-permute-done.3.refs_2_.refs_5_, ...), custom_call_target="tpu_custom_call" | custom-call | flops 226492416 | bytes 5505024 | tf_op jit(solution)/shard_map/pallas_call | solution.py:28
  18.8 0.0 collective-permute-start.8
  18.9 1.3 %collective-permute-start.7 = (bf16[512,256]{1,0:T(8,128)(2,1)S(1)}, bf16[512,256]{1,0:T(8,128)(2,1)S(1)}, u32[]{:S(2)}, u32[]{:S(2)}) collective-permute-start(bf16[512,256]{1,0:T(8,128)(2,1)S(1)} %bitcast.7), channel_id=1, source_target_pairs={{8,0},{16,8},{24,16},{9,1},{17,9},{25,17},{10,2},{18,10},{26,18},{... | collective-permute-start | bytes 786440 | tf_op jit(solution)/shard_map/ppermute | solution.py:438
  20.2 0.6 %shard_map.74.refs_7_.refs_0_ = f32[4,432,128]{2,1,0:T(8,128)S(1)} custom-call(bf16[2560,640]{1,0:T(8,128)(2,1)S(1)} %get-tuple-element.34.refs_0_, bf16[256,512]{1,0:T(8,128)(2,1)S(1)} %get-tuple-element.38.refs_1_, f32[256,640]{1,0:T(8,128)S(1)} %get-tuple-element.35.refs_3_.refs_2_, f32[256,640]{1,0:T(8,128)S(1)} %get-tuple-element.36.refs_4_.refs_3_, ...), custom_call_target="tpu_custom_call" | custom-call | flops 226492416 | bytes 5505024 | tf_op jit(solution)/shard_map/pallas_call | solution.py:28
  20.7 0.1 shard_map.76
  20.9 2.7 %collective-permute-start.10 = (bf16[1,432,128]{2,1,0:T(8,128)(2,1)S(1)}, bf16[1,432,128]{2,1,0:T(8,128)(2,1)S(1)}, u32[]{:S(2)}, u32[]{:S(2)}) collective-permute-start(bf16[1,432,128]{2,1,0:T(8,128)(2,1)S(1)} %get-tuple-element.44), channel_id=1, source_target_pairs={{0,4},{1,5},{2,6},{3,7},{4,0},{5,1},{6,2},{7,3},{8,12},{9,13},{10,... | collective-permute-start | bytes 331784 | tf_op jit(solution)/shard_map/ppermute | solution.py:47
  23.6 1.3 %collective-permute-start.11 = (bf16[1,432,128]{2,1,0:T(8,128)(2,1)S(1)}, bf16[1,432,128]{2,1,0:T(8,128)(2,1)S(1)}, u32[]{:S(2)}, u32[]{:S(2)}) collective-permute-start(bf16[1,432,128]{2,1,0:T(8,128)(2,1)S(1)} %get-tuple-element.45), channel_id=1, source_target_pairs={{0,6},{1,7},{2,4},{3,5},{4,2},{5,3},{6,0},{7,1},{8,14},{9,15},{10,... | collective-permute-start | bytes 331784 | tf_op jit(solution)/shard_map/ppermute | solution.py:47
  24.9 0.2 collective-permute-start.9
  25.1 2.8 %shard_map.75 = (bf16[512,256]{1,0:T(8,128)(2,1)}, f32[8,128]{1,0:T(8,128)S(1)}, bf16[9,768,256]{2,1,0:T(8,128)(2,1)S(1)}) custom-call(s32[1]{0:T(128)S(6)} %copy.13.refs_0_, bf16[512,256]{1,0:T(8,128)(2,1)S(1)} %get-tuple-element.25.refs_1_, bf16[512,256]{1,0:T(8,128)(2,1)S(1)} %collective-permute-done.refs_0_.refs_2_, ...), custom_call_target="tpu_custom_call" | custom-call | flops 1811939328 | bytes 4587524 | tf_op jit(solution)/shard_map/pallas_call | solution.py:28
  28.0 4.6 %collective-permute-done.10.refs_2_ = bf16[1,432,128]{2,1,0:T(8,128)(2,1)S(1)} collective-permute-done((bf16[1,432,128]{2,1,0:T(8,128)(2,1)S(1)}, bf16[1,432,128]{2,1,0:T(8,128)(2,1)S(1)}, u32[]{:S(2)}, u32[]{:S(2)}) %collective-permute-start.10) | collective-permute-done | bytes 110624 | tf_op jit(solution)/shard_map/ppermute | solution.py:47
  32.6 0.9 %collective-permute-done.9.refs_1_ = bf16[1,432,128]{2,1,0:T(8,128)(2,1)S(1)} collective-permute-done((bf16[1,432,128]{2,1,0:T(8,128)(2,1)S(1)}, bf16[1,432,128]{2,1,0:T(8,128)(2,1)S(1)}, u32[]{:S(2)}, u32[]{:S(2)}) %collective-permute-start.9) | collective-permute-done | bytes 110624 | tf_op jit(solution)/shard_map/ppermute | solution.py:47
  33.4 0.1 shard_map.77.refs_5_.refs_0_
  33.5 2.4 %collective-permute-start.12 = (bf16[432,128]{1,0:T(8,128)(2,1)S(1)}, bf16[432,128]{1,0:T(8,128)(2,1)S(1)}, u32[]{:S(2)}, u32[]{:S(2)}) collective-permute-start(bf16[432,128]{1,0:T(8,128)(2,1)S(1)} %shard_map.77.refs_5_.refs_0_), channel_id=1, source_target_pairs={{0,8},{8,0},{16,24},{24,16},{1,9},{9,1},{17,25},{25,17},{2,10},{10... | collective-permute-start | bytes 331784 | tf_op jit(solution)/shard_map/ppermute | solution.py:47
  35.9 1.0 %collective-permute-start.13 = (bf16[432,128]{1,0:T(8,128)(2,1)S(1)}, bf16[432,128]{1,0:T(8,128)(2,1)S(1)}, u32[]{:S(2)}, u32[]{:S(2)}) collective-permute-start(bf16[432,128]{1,0:T(8,128)(2,1)S(1)} %shard_map.77.refs_5_.refs_0_), channel_id=1, source_target_pairs={{0,16},{8,24},{16,0},{24,8},{1,17},{9,25},{17,1},{25,9},{2,18},{10... | collective-permute-start | bytes 331784 | tf_op jit(solution)/shard_map/ppermute | solution.py:47
  36.9 1.4 %collective-permute-start.14 = (bf16[432,128]{1,0:T(8,128)(2,1)S(1)}, bf16[432,128]{1,0:T(8,128)(2,1)S(1)}, u32[]{:S(2)}, u32[]{:S(2)}) collective-permute-start(bf16[432,128]{1,0:T(8,128)(2,1)S(1)} %shard_map.77.refs_5_.refs_0_), channel_id=1, source_target_pairs={{0,24},{8,16},{16,8},{24,0},{1,25},{9,17},{17,9},{25,1},{2,26},{10... | collective-permute-start | bytes 331784 | tf_op jit(solution)/shard_map/ppermute | solution.py:47
  38.3 2.8 %shard_map.78 = bf16[512,256]{1,0:T(8,128)(2,1)} custom-call(s32[1]{0:T(128)S(6)} %copy.13.refs_0_, bf16[512,256]{1,0:T(8,128)(2,1)S(1)} %get-tuple-element.25.refs_1_, bf16[512,256]{1,0:T(8,128)(2,1)S(1)} %bitcast.8, bf16[512,256]{1,0:T(8,128)(2,1)S(1)} %collective-permute-done.7.refs_3_, bf16[9,768,256]{2,1,0:T(8,128)(2,1)S(1)} %get-tuple-element.41.refs_4_, ...), custom_call_target="tpu_custom_call" | custom-call | flops 1811939328 | bytes 4325380 | tf_op jit(solution)/shard_map/pallas_call | solution.py:28
  41.1 1.4 %collective-permute-done.14.refs_3_ = bf16[432,128]{1,0:T(8,128)(2,1)S(1)} collective-permute-done((bf16[432,128]{1,0:T(8,128)(2,1)S(1)}, bf16[432,128]{1,0:T(8,128)(2,1)S(1)}, u32[]{:S(2)}, u32[]{:S(2)}) %collective-permute-start.14) | collective-permute-done | bytes 110624 | tf_op jit(solution)/shard_map/ppermute | solution.py:47
  42.6 1.1 %shard_map.79 = f32[27,32,256]{2,1,0:T(8,128)} custom-call(bf16[432,128]{1,0:T(8,128)(2,1)S(1)} %shard_map.77.refs_5_.refs_0_, bf16[432,128]{1,0:T(8,128)(2,1)S(1)} %collective-permute-done.12.refs_1_, bf16[432,128]{1,0:T(8,128)(2,1)S(1)} %collective-permute-done.13.refs_2_, bf16[432,128]{1,0:T(8,128)(2,1)S(1)} %collective-permute-done.14.refs_3_), custom_call_target="tpu_custom_call" | custom-call | bytes 442368 | tf_op jit(solution)/shard_map/pallas_call | solution.py:28
  (15 shorter events, 0.1 us)
Async XLA Ops:
  0.6 10.3 %collective-permute-start = (bf16[512,256]{1,0:T(8,128)(2,1)}, bf16[512,256]{1,0:T(8,128)(2,1)S(1)}, u32[]{:S(2)}, u32[]{:S(2)}) collective-permute-start(bf16[512,256]{1,0:T(8,128)(2,1)} %bitcast.11), channel_id=1, source_target_pairs={{0,8},{1,17},{2,10},{3,19},{4,12},{5,21},{6,14},{7,23},{8,0},{9,25... | collective-permute-start | bytes 786440 | tf_op jit(solution)/shard_map/ppermute | solution.py:61
  3.7 9.5 %collective-permute-start.1 = (bf16[512,256]{1,0:T(8,128)(2,1)}, bf16[512,256]{1,0:T(8,128)(2,1)S(1)}, u32[]{:S(2)}, u32[]{:S(2)}) collective-permute-start(bf16[512,256]{1,0:T(8,128)(2,1)} %bitcast.12), channel_id=1, source_target_pairs={{0,16},{1,9},{2,18},{3,11},{4,20},{5,13},{6,22},{7,15},{8,24},{9,1... | collective-permute-start | bytes 786440 | tf_op jit(solution)/shard_map/ppermute | solution.py:61
  6.4 8.4 %collective-permute-start.6 = (bf16[256,128]{1,0:T(8,128)(2,1)S(1)}, bf16[256,128]{1,0:T(8,128)(2,1)S(1)}, u32[]{:S(2)}, u32[]{:S(2)}) collective-permute-start(bf16[256,128]{1,0:T(8,128)(2,1)S(1)} %get-tuple-element.28), channel_id=1, source_target_pairs={{0,8},{1,17},{2,10},{3,19},{4,12},{5,21},{6,14},{7,23},{8,0},{9,25... | collective-permute-start | bytes 196616 | tf_op jit(solution)/shard_map/ppermute | solution.py:61
  7.0 8.2 %collective-permute-start.4 = (bf16[256,128]{1,0:T(8,128)(2,1)S(1)}, bf16[256,128]{1,0:T(8,128)(2,1)S(1)}, u32[]{:S(2)}, u32[]{:S(2)}) collective-permute-start(bf16[256,128]{1,0:T(8,128)(2,1)S(1)} %get-tuple-element.26), channel_id=1, source_target_pairs={{0,16},{1,9},{2,18},{3,11},{4,20},{5,13},{6,22},{7,15},{8,24},{9,1... | collective-permute-start | bytes 196616 | tf_op jit(solution)/shard_map/ppermute | solution.py:61
  7.0 8.3 %collective-permute-start.5 = (bf16[256,128]{1,0:T(8,128)(2,1)S(1)}, bf16[256,128]{1,0:T(8,128)(2,1)S(1)}, u32[]{:S(2)}, u32[]{:S(2)}) collective-permute-start(bf16[256,128]{1,0:T(8,128)(2,1)S(1)} %get-tuple-element.27), channel_id=1, source_target_pairs={{0,24},{8,16},{16,8},{24,0},{1,25},{9,17},{17,9},{25,1},{2,26},{10... | collective-permute-start | bytes 196616 | tf_op jit(solution)/shard_map/ppermute | solution.py:47
  10.9 6.8 %collective-permute-start.2 = (bf16[256,256]{1,0:T(8,128)(2,1)S(1)}, bf16[256,256]{1,0:T(8,128)(2,1)S(1)}, u32[]{:S(2)}, u32[]{:S(2)}) collective-permute-start(bf16[256,256]{1,0:T(8,128)(2,1)S(1)} %shard_map.68), channel_id=1, source_target_pairs={{0,16},{1,9},{2,18},{3,11},{4,20},{5,13},{6,22},{7,15},{8,24},{9,1... | collective-permute-start | bytes 393224 | tf_op jit(solution)/shard_map/ppermute | solution.py:61
  13.2 5.0 %collective-permute-start.3 = (bf16[256,256]{1,0:T(8,128)(2,1)S(1)}, bf16[256,256]{1,0:T(8,128)(2,1)S(1)}, u32[]{:S(2)}, u32[]{:S(2)}) collective-permute-start(bf16[256,256]{1,0:T(8,128)(2,1)S(1)} %shard_map.69), channel_id=1, source_target_pairs={{0,8},{1,17},{2,10},{3,19},{4,12},{5,21},{6,14},{7,23},{8,0},{9,25... | collective-permute-start | bytes 393224 | tf_op jit(solution)/shard_map/ppermute | solution.py:61
  17.7 1.1 %copy-start = (bf16[1,2,16,16,256]{4,3,2,1,0:T(8,128)(2,1)S(1)}, bf16[1,2,16,16,256]{4,3,2,1,0:T(8,128)(2,1)}, u32[]{:S(2)}) copy-start(bf16[1,2,16,16,256]{4,3,2,1,0:T(8,128)(2,1)} %param.5) | copy-start | bytes 786436
  18.8 1.9 %collective-permute-start.8 = (bf16[4,432,128]{2,1,0:T(8,128)(2,1)S(1)}, bf16[4,432,128]{2,1,0:T(8,128)(2,1)S(1)}, u32[]{:S(2)}, u32[]{:S(2)}) collective-permute-start(bf16[4,432,128]{2,1,0:T(8,128)(2,1)S(1)} %get-tuple-element.39.refs_5_), channel_id=1, source_target_pairs={{0,1},{1,0},{2,3},{3,2},{4,5},{5,4},{6,7},{7,6},{8,9},{9,8},{10,11... | collective-permute-start | bytes 1327112 | tf_op jit(solution)/shard_map/ppermute | solution.py:47
  18.9 19.4 %collective-permute-start.7 = (bf16[512,256]{1,0:T(8,128)(2,1)S(1)}, bf16[512,256]{1,0:T(8,128)(2,1)S(1)}, u32[]{:S(2)}, u32[]{:S(2)}) collective-permute-start(bf16[512,256]{1,0:T(8,128)(2,1)S(1)} %bitcast.7), channel_id=1, source_target_pairs={{8,0},{16,8},{24,16},{9,1},{17,9},{25,17},{10,2},{18,10},{26,18},{... | collective-permute-start | bytes 786440 | tf_op jit(solution)/shard_map/ppermute | solution.py:438
  20.2 5.0 %copy-start.1 = (bf16[3,3,3,256,256]{4,3,2,1,0:T(8,128)(2,1)S(1)}, bf16[3,3,3,256,256]{4,3,2,1,0:T(8,128)(2,1)}, u32[]{:S(2)}) copy-start(bf16[3,3,3,256,256]{4,3,2,1,0:T(8,128)(2,1)} %param.6) | copy-start | bytes 10616836
  20.9 11.7 %collective-permute-start.10 = (bf16[1,432,128]{2,1,0:T(8,128)(2,1)S(1)}, bf16[1,432,128]{2,1,0:T(8,128)(2,1)S(1)}, u32[]{:S(2)}, u32[]{:S(2)}) collective-permute-start(bf16[1,432,128]{2,1,0:T(8,128)(2,1)S(1)} %get-tuple-element.44), channel_id=1, source_target_pairs={{0,4},{1,5},{2,6},{3,7},{4,0},{5,1},{6,2},{7,3},{8,12},{9,13},{10,... | collective-permute-start | bytes 331784 | tf_op jit(solution)/shard_map/ppermute | solution.py:47
  23.6 9.0 %collective-permute-start.11 = (bf16[1,432,128]{2,1,0:T(8,128)(2,1)S(1)}, bf16[1,432,128]{2,1,0:T(8,128)(2,1)S(1)}, u32[]{:S(2)}, u32[]{:S(2)}) collective-permute-start(bf16[1,432,128]{2,1,0:T(8,128)(2,1)S(1)} %get-tuple-element.45), channel_id=1, source_target_pairs={{0,6},{1,7},{2,4},{3,5},{4,2},{5,3},{6,0},{7,1},{8,14},{9,15},{10,... | collective-permute-start | bytes 331784 | tf_op jit(solution)/shard_map/ppermute | solution.py:47
  24.9 8.5 %collective-permute-start.9 = (bf16[1,432,128]{2,1,0:T(8,128)(2,1)S(1)}, bf16[1,432,128]{2,1,0:T(8,128)(2,1)S(1)}, u32[]{:S(2)}, u32[]{:S(2)}) collective-permute-start(bf16[1,432,128]{2,1,0:T(8,128)(2,1)S(1)} %get-tuple-element.43), channel_id=1, source_target_pairs={{0,2},{1,3},{2,0},{3,1},{4,6},{5,7},{6,4},{7,5},{8,10},{9,11},{10,... | collective-permute-start | bytes 331784 | tf_op jit(solution)/shard_map/ppermute | solution.py:47
  33.5 7.7 %collective-permute-start.12 = (bf16[432,128]{1,0:T(8,128)(2,1)S(1)}, bf16[432,128]{1,0:T(8,128)(2,1)S(1)}, u32[]{:S(2)}, u32[]{:S(2)}) collective-permute-start(bf16[432,128]{1,0:T(8,128)(2,1)S(1)} %shard_map.77.refs_5_.refs_0_), channel_id=1, source_target_pairs={{0,8},{8,0},{16,24},{24,16},{1,9},{9,1},{17,25},{25,17},{2,10},{10... | collective-permute-start | bytes 331784 | tf_op jit(solution)/shard_map/ppermute | solution.py:47
  35.9 5.2 %collective-permute-start.13 = (bf16[432,128]{1,0:T(8,128)(2,1)S(1)}, bf16[432,128]{1,0:T(8,128)(2,1)S(1)}, u32[]{:S(2)}, u32[]{:S(2)}) collective-permute-start(bf16[432,128]{1,0:T(8,128)(2,1)S(1)} %shard_map.77.refs_5_.refs_0_), channel_id=1, source_target_pairs={{0,16},{8,24},{16,0},{24,8},{1,17},{9,25},{17,1},{25,9},{2,18},{10... | collective-permute-start | bytes 331784 | tf_op jit(solution)/shard_map/ppermute | solution.py:47
  36.9 5.6 %collective-permute-start.14 = (bf16[432,128]{1,0:T(8,128)(2,1)S(1)}, bf16[432,128]{1,0:T(8,128)(2,1)S(1)}, u32[]{:S(2)}, u32[]{:S(2)}) collective-permute-start(bf16[432,128]{1,0:T(8,128)(2,1)S(1)} %shard_map.77.refs_5_.refs_0_), channel_id=1, source_target_pairs={{0,24},{8,16},{16,8},{24,0},{1,25},{9,17},{17,9},{25,1},{2,26},{10... | collective-permute-start | bytes 331784 | tf_op jit(solution)/shard_map/ppermute | solution.py:47

commit v4 on v3

--- a/solution.py
+++ b/solution.py
@@ -216,7 +216,7 @@
         return ref[part, :, tile * LANES : (tile + 1) * LANES]
     if tile < 13:
         return ref[part, tile * count : (tile + 1) * count, :]
-    value = ref[part, tile * count :, :]
+    value = ref[part, tile * count :, :].astype(F32)
     return jnp.concatenate([value, half_turn(value)], axis=0)
 
 
@@ -253,10 +253,15 @@
             put_tile(out_ref, part, at, value.astype(out_ref.dtype))
 
 
-def send_body(count, area, grads, first, second, *refs):
+def first_rows_body(first, turned):
+    rows = first.shape[0]
+    turned[:, :rows] = jax.nn.silu(first[...].astype(F32)).astype(BF16).T
+
+
+def send_body(count, area, grads, second, held, *refs):
     products, (send_ref, turned) = refs[:3], refs[3:]
-    values = jnp.concatenate([first[...], second[...]], axis=0).astype(F32)
-    turned[...] = jax.nn.silu(values).astype(BF16).T
+    rows = second.shape[0]
+    turned[:, 2 * area - rows :] = jax.nn.silu(second[...].astype(F32)).astype(BF16).T
     other = 1 - lax.axis_index("dp") % 2
     core_sums(count, area, other, grads, turned, products, send_ref)
 
@@ -266,18 +271,17 @@
 
 
 def sum_body(arrived, radix, step, *refs):
-    keep_ref, in_refs = refs[0], refs[1 : 1 + arrived]
-    total = keep_ref[...]
-    for ref in in_refs:
-        total = total + ref[...].astype(F32)
+    terms, out_refs = refs[: 1 + arrived], refs[1 + arrived :]
+
+    def total(part):
+        return sum((ref[part].astype(F32) for ref in terms[1:]), terms[0][part])
+
     if radix == 1:
-        refs[1 + arrived][...] = total[0].astype(BF16)
+        out_refs[0][...] = total(0).astype(BF16)
         return
-    out_refs, held = refs[1 + arrived : -1], refs[-1]
-    held[...] = total
     digit = (lax.axis_index("dp") // 2) // step % radix
     for mask, out in enumerate(out_refs):
-        out[...] = held[pl.ds((digit ^ mask) * step, step)].astype(out.dtype)
+        out[...] = total(pl.ds((digit ^ mask) * step, step)).astype(out.dtype)
 
 
 def sum_over_clips(keep, send, after):
@@ -297,36 +301,36 @@
         outs = [pltpu.VMEM((step, count, lanes), F32)]
         outs += [pltpu.VMEM((step, count, lanes), BF16)] * (radix - 1)
         keep, *sends = call(
-            functools.partial(sum_body, len(arrived), radix, step),
-            outs,
-            (keep, *arrived),
-            scratch=[pltpu.VMEM((parts, count, lanes), F32)],
+            functools.partial(sum_body, len(arrived), radix, step), outs, (keep, *arrived)
         )
         arrived = swaps(sends, "dp", 2 * step)
 
 
 def place_body(peers, scale, *refs):
     pieces, out_hbm, held, placed, sems = refs[:peers], *refs[peers:]
-    for turn, piece in enumerate(pieces):
-        held[lax.axis_index("tm") ^ turn] = piece[...].astype(F32) * scale
+    for mask, piece in enumerate(pieces):
+        held[lax.axis_index("tm") ^ mask] = piece[...]
     count = placed.shape[1]
     low = low_half((count, LANES))
     copies = []
-    for time_tap in range(3):
-        for tap in range(9):
-            tile = 4 * time_tap + tap // 2 if tap < 8 else 12 + time_tap // 2
-            half = tap % 2 if tap < 8 else time_tap % 2
-            for pair in range(peers // 2):
-                left = get_tile(held, 2 * pair, tile, count)
-                right = get_tile(held, 2 * pair + 1, tile, count)
-                if half == 0:
-                    value = jnp.where(low, left, half_turn(right))
-                else:
-                    value = jnp.where(low, half_turn(left), right)
-                placed[9 * time_tap + tap, :, pair * LANES : (pair + 1) * LANES] = value
-        taps = pl.ds(9 * time_tap, 9)
-        copies.append(pltpu.make_async_copy(placed.at[taps], out_hbm.at[taps], sems.at[time_tap]))
-        copies[-1].start()
+    for tap in range(27):
+        time_tap, at = tap // 9, tap % 9
+        tile = 4 * time_tap + at // 2 if at < 8 else 12 + time_tap // 2
+        half = at % 2 if at < 8 else time_tap % 2
+        for pair in range(peers // 2):
+            left = get_tile(held, 2 * pair, tile, count).astype(F32)
+            right = get_tile(held, 2 * pair + 1, tile, count).astype(F32)
+            if half == 0:
+                value = jnp.where(low, left, half_turn(right))
+            else:
+                value = jnp.where(low, half_turn(left), right)
+            placed[tap, :, pair * LANES : (pair + 1) * LANES] = value * scale
+        if tap % 3 == 2:
+            taps = pl.ds(tap - 2, 3)
+            copies.append(
+                pltpu.make_async_copy(placed.at[taps], out_hbm.at[taps], sems.at[tap // 3])
+            )
+            copies[-1].start()
     for copy in copies:
         copy.wait()
 
@@ -457,10 +461,13 @@
         flops=2 * 27 * 2 * peers * area * channels * LANES // 2,
     )
     half = 27 * 2 * area * channels * LANES // 2
+    last = pltpu.VMEM((channels, 2 * area), BF16)
+    (last_turned,) = call(first_rows_body, [last], (first,))
     send, last_turned = call(
         functools.partial(send_body, count, area),
-        [pltpu.VMEM(sums_shape(parts, count), BF16), pltpu.VMEM((channels, 2 * area), BF16)],
-        (grads, first, second, *products),
+        [pltpu.VMEM(sums_shape(parts, count), BF16), last],
+        (grads, second, last_turned, *products),
+        aliases={2: 1},
         flops=half,
     )
     (keep,) = call(
@@ -497,9 +504,9 @@
         [sds((27, count, channels), F32)],
         pieces,
         scratch=[
-            pltpu.VMEM((peers, *piece.shape), F32),
+            pltpu.VMEM((peers, *piece.shape), BF16),
             pltpu.VMEM((27, count, channels), F32),
-            pltpu.SemaphoreType.DMA((3,)),
+            pltpu.SemaphoreType.DMA((9,)),
         ],
         out_space=pl.ANY,
     )

time: 44.5 us -> 44.4 us (level)
    pallas_call x13 -> x14, Pallas kernels: 12.5 us -> 12.5 us  [call(): pl.pallas_call(with_after, out_shape=tuple(outs), in_specs=[pl.BlockSpec(...]
where the time goes in v4:
time: 44.4 us; the launch traced here: 43.6 us
  starting transfers between devices  22.3 us (50%)
  Pallas kernels  12.5 us (28%)
  waiting for transfers between devices  7.42 us (17%)
  between operations  1.41 us (3%)
    pallas_call x14, Pallas kernels, call(): pl.pallas_call(with_after, out_shape=tuple(outs), in_specs=[pl.BlockSpec(...  12.5 us
    ppermute x8, starting transfers between devices, swap(): return lax.ppermute(value, axis, [(s, s ^ mask) for s in range(count)])  12 us
    ppermute x6, starting transfers between devices, cross(): return lax.ppermute(value, ('tm', 'dp'), pairs)  9 us
    ppermute x8, waiting for transfers between devices, swap(): return lax.ppermute(value, axis, [(s, s ^ mask) for s in range(count)])  7.05 us
    ppermute x1, starting transfers between devices, local(): later = lax.ppermute(cot, 'tm', [(s, s - 1) for s in range(1, peers)])  1.29 us
  transfers between devices with their start and end apart: 15, of which 5 were waited for; matrix products, arithmetic and copies ran while one was open for 0% of the time, Pallas kernels for 25%

profile of v4, /device:TPU:0, one launch (start us, length us, event | category | flops | bytes accessed | tf_op | source)
XLA Modules:
  0.0 43.6 jit_solution(8280580469260230005)
XLA Ops:
  0.6 3.0 %collective-permute-start = (bf16[512,256]{1,0:T(8,128)(2,1)}, bf16[512,256]{1,0:T(8,128)(2,1)S(1)}, u32[]{:S(2)}, u32[]{:S(2)}) collective-permute-start(bf16[512,256]{1,0:T(8,128)(2,1)} %bitcast.11), channel_id=1, source_target_pairs={{0,8},{1,17},{2,10},{3,19},{4,12},{5,21},{6,14},{7,23},{8,0},{9,25... | collective-permute-start | bytes 786440 | tf_op jit(solution)/shard_map/ppermute | solution.py:61
  3.7 1.5 %collective-permute-start.1 = (bf16[512,256]{1,0:T(8,128)(2,1)}, bf16[512,256]{1,0:T(8,128)(2,1)S(1)}, u32[]{:S(2)}, u32[]{:S(2)}) collective-permute-start(bf16[512,256]{1,0:T(8,128)(2,1)} %bitcast.12), channel_id=1, source_target_pairs={{0,16},{1,9},{2,18},{3,11},{4,20},{5,13},{6,22},{7,15},{8,24},{9,1... | collective-permute-start | bytes 786440 | tf_op jit(solution)/shard_map/ppermute | solution.py:61
  5.2 1.2 %shard_map.67 = (bf16[256,128]{1,0:T(8,128)(2,1)S(1)}, bf16[256,128]{1,0:T(8,128)(2,1)S(1)}, bf16[256,128]{1,0:T(8,128)(2,1)S(1)}, bf16[256,128]{1,0:T(8,128)(2,1)S(1)}, bf16[512,256]{1,0:T(8,128)(2,1)S(1)}) custom-call(bf16[512,256]{1,0:T(8,128)(2,1)} %bitcast.6, bf16[512,256]{1,0:T(8,128)(2,1)} %bitcast.13), custom_call_target="tpu_custom_call" | custom-call | bytes 524288 | tf_op jit(solution)/shard_map/pallas_call | solution.py:28
  6.4 0.6 %collective-permute-start.6 = (bf16[256,128]{1,0:T(8,128)(2,1)S(1)}, bf16[256,128]{1,0:T(8,128)(2,1)S(1)}, u32[]{:S(2)}, u32[]{:S(2)}) collective-permute-start(bf16[256,128]{1,0:T(8,128)(2,1)S(1)} %get-tuple-element.28), channel_id=1, source_target_pairs={{0,8},{1,17},{2,10},{3,19},{4,12},{5,21},{6,14},{7,23},{8,0},{9,25... | collective-permute-start | bytes 196616 | tf_op jit(solution)/shard_map/ppermute | solution.py:61
  7.0 0.1 collective-permute-start.4
  7.0 2.9 %collective-permute-start.5 = (bf16[256,128]{1,0:T(8,128)(2,1)S(1)}, bf16[256,128]{1,0:T(8,128)(2,1)S(1)}, u32[]{:S(2)}, u32[]{:S(2)}) collective-permute-start(bf16[256,128]{1,0:T(8,128)(2,1)S(1)} %get-tuple-element.27), channel_id=1, source_target_pairs={{0,24},{8,16},{16,8},{24,0},{1,25},{9,17},{17,9},{25,1},{2,26},{10... | collective-permute-start | bytes 196616 | tf_op jit(solution)/shard_map/ppermute | solution.py:47
  10.6 0.3 shard_map.70
  10.9 2.2 %collective-permute-start.2 = (bf16[256,256]{1,0:T(8,128)(2,1)S(1)}, bf16[256,256]{1,0:T(8,128)(2,1)S(1)}, u32[]{:S(2)}, u32[]{:S(2)}) collective-permute-start(bf16[256,256]{1,0:T(8,128)(2,1)S(1)} %shard_map.68), channel_id=1, source_target_pairs={{0,16},{1,9},{2,18},{3,11},{4,20},{5,13},{6,22},{7,15},{8,24},{9,1... | collective-permute-start | bytes 393224 | tf_op jit(solution)/shard_map/ppermute | solution.py:61
  13.2 1.6 %collective-permute-start.3 = (bf16[256,256]{1,0:T(8,128)(2,1)S(1)}, bf16[256,256]{1,0:T(8,128)(2,1)S(1)}, u32[]{:S(2)}, u32[]{:S(2)}) collective-permute-start(bf16[256,256]{1,0:T(8,128)(2,1)S(1)} %shard_map.69), channel_id=1, source_target_pairs={{0,8},{1,17},{2,10},{3,19},{4,12},{5,21},{6,14},{7,23},{8,0},{9,25... | collective-permute-start | bytes 393224 | tf_op jit(solution)/shard_map/ppermute | solution.py:61
  14.7 0.4 shard_map.71
  15.2 0.2 collective-permute-done.5.refs_2_
  15.3 2.4 %shard_map.72 = (bf16[2560,640]{1,0:T(8,128)(2,1)S(1)}, f32[256,640]{1,0:T(8,128)S(1)}, f32[256,640]{1,0:T(8,128)S(1)}, f32[256,640]{1,0:T(8,128)S(1)}) custom-call(s32[1]{0:T(128)S(6)} %copy.15.refs_0_, bf16[256,128]{1,0:T(8,128)(2,1)S(1)} %collective-permute-done.4.refs_1_, ...), custom_call_target="tpu_custom_call", output_to_operand_aliasing={{0}: (4, {})} | custom-call | flops 1811939328 | bytes 4194308 | tf_op jit(solution)/shard_map/pallas_call | solution.py:28
  17.7 0.1 shard_map.73.refs_2_
  17.9 0.4 collective-permute-done.3.refs_1_.refs_5_
  18.2 0.6 %shard_map.74 = (bf16[4,432,128]{2,1,0:T(8,128)(2,1)S(1)}, bf16[256,512]{1,0:T(8,128)(2,1)S(1)}) custom-call(bf16[2560,640]{1,0:T(8,128)(2,1)S(1)} %get-tuple-element.34.refs_0_, bf16[256,256]{1,0:T(8,128)(2,1)S(1)} %collective-permute-done.3.refs_1_.refs_5_, bf16[256,512]{1,0:T(8,128)(2,1)S(1)} %shard_map.73.refs_2_, ...), custom_call_target="tpu_custom_call", output_to_operand_aliasing={{1}: (2, {})} | custom-call | flops 226492416 | bytes 5636096 | tf_op jit(solution)/shard_map/pallas_call | solution.py:28
  18.8 0.0 collective-permute-start.8
  18.9 1.3 %collective-permute-start.7 = (bf16[512,256]{1,0:T(8,128)(2,1)S(1)}, bf16[512,256]{1,0:T(8,128)(2,1)S(1)}, u32[]{:S(2)}, u32[]{:S(2)}) collective-permute-start(bf16[512,256]{1,0:T(8,128)(2,1)S(1)} %bitcast.7), channel_id=1, source_target_pairs={{8,0},{16,8},{24,16},{9,1},{17,9},{25,17},{10,2},{18,10},{26,18},{... | collective-permute-start | bytes 786440 | tf_op jit(solution)/shard_map/ppermute | solution.py:442
  20.2 0.6 %shard_map.75.refs_7_.refs_0_ = f32[4,432,128]{2,1,0:T(8,128)S(1)} custom-call(bf16[2560,640]{1,0:T(8,128)(2,1)S(1)} %get-tuple-element.34.refs_0_, bf16[256,512]{1,0:T(8,128)(2,1)S(1)} %get-tuple-element.38.refs_1_, f32[256,640]{1,0:T(8,128)S(1)} %get-tuple-element.35.refs_3_.refs_2_, f32[256,640]{1,0:T(8,128)S(1)} %get-tuple-element.36.refs_4_.refs_3_, ...), custom_call_target="tpu_custom_call" | custom-call | flops 226492416 | bytes 5505024 | tf_op jit(solution)/shard_map/pallas_call | solution.py:28
  20.7 0.1 shard_map.77
  20.9 2.7 %collective-permute-start.10 = (bf16[1,432,128]{2,1,0:T(8,128)(2,1)S(1)}, bf16[1,432,128]{2,1,0:T(8,128)(2,1)S(1)}, u32[]{:S(2)}, u32[]{:S(2)}) collective-permute-start(bf16[1,432,128]{2,1,0:T(8,128)(2,1)S(1)} %get-tuple-element.44), channel_id=1, source_target_pairs={{0,4},{1,5},{2,6},{3,7},{4,0},{5,1},{6,2},{7,3},{8,12},{9,13},{10,... | collective-permute-start | bytes 331784 | tf_op jit(solution)/shard_map/ppermute | solution.py:47
  23.5 1.4 %collective-permute-start.11 = (bf16[1,432,128]{2,1,0:T(8,128)(2,1)S(1)}, bf16[1,432,128]{2,1,0:T(8,128)(2,1)S(1)}, u32[]{:S(2)}, u32[]{:S(2)}) collective-permute-start(bf16[1,432,128]{2,1,0:T(8,128)(2,1)S(1)} %get-tuple-element.45), channel_id=1, source_target_pairs={{0,6},{1,7},{2,4},{3,5},{4,2},{5,3},{6,0},{7,1},{8,14},{9,15},{10,... | collective-permute-start | bytes 331784 | tf_op jit(solution)/shard_map/ppermute | solution.py:47
  24.9 0.2 collective-permute-start.9
  25.1 2.8 %shard_map.76 = (bf16[512,256]{1,0:T(8,128)(2,1)}, f32[8,128]{1,0:T(8,128)S(1)}, bf16[9,768,256]{2,1,0:T(8,128)(2,1)S(1)}) custom-call(s32[1]{0:T(128)S(6)} %copy.15.refs_0_, bf16[512,256]{1,0:T(8,128)(2,1)S(1)} %get-tuple-element.25.refs_1_, bf16[512,256]{1,0:T(8,128)(2,1)S(1)} %collective-permute-done.refs_0_.refs_2_, ...), custom_call_target="tpu_custom_call" | custom-call | flops 1811939328 | bytes 4587524 | tf_op jit(solution)/shard_map/pallas_call | solution.py:28
  27.9 4.6 %collective-permute-done.10.refs_2_ = bf16[1,432,128]{2,1,0:T(8,128)(2,1)S(1)} collective-permute-done((bf16[1,432,128]{2,1,0:T(8,128)(2,1)S(1)}, bf16[1,432,128]{2,1,0:T(8,128)(2,1)S(1)}, u32[]{:S(2)}, u32[]{:S(2)}) %collective-permute-start.10) | collective-permute-done | bytes 110624 | tf_op jit(solution)/shard_map/ppermute | solution.py:47
  32.5 0.8 %collective-permute-done.9.refs_1_ = bf16[1,432,128]{2,1,0:T(8,128)(2,1)S(1)} collective-permute-done((bf16[1,432,128]{2,1,0:T(8,128)(2,1)S(1)}, bf16[1,432,128]{2,1,0:T(8,128)(2,1)S(1)}, u32[]{:S(2)}, u32[]{:S(2)}) %collective-permute-start.9) | collective-permute-done | bytes 110624 | tf_op jit(solution)/shard_map/ppermute | solution.py:47
  33.4 0.1 shard_map.78.refs_5_.refs_0_
  33.5 2.4 %collective-permute-start.12 = (bf16[432,128]{1,0:T(8,128)(2,1)S(1)}, bf16[432,128]{1,0:T(8,128)(2,1)S(1)}, u32[]{:S(2)}, u32[]{:S(2)}) collective-permute-start(bf16[432,128]{1,0:T(8,128)(2,1)S(1)} %shard_map.78.refs_5_.refs_0_), channel_id=1, source_target_pairs={{0,8},{8,0},{16,24},{24,16},{1,9},{9,1},{17,25},{25,17},{2,10},{10... | collective-permute-start | bytes 331784 | tf_op jit(solution)/shard_map/ppermute | solution.py:47
  35.9 1.0 %collective-permute-start.13 = (bf16[432,128]{1,0:T(8,128)(2,1)S(1)}, bf16[432,128]{1,0:T(8,128)(2,1)S(1)}, u32[]{:S(2)}, u32[]{:S(2)}) collective-permute-start(bf16[432,128]{1,0:T(8,128)(2,1)S(1)} %shard_map.78.refs_5_.refs_0_), channel_id=1, source_target_pairs={{0,16},{8,24},{16,0},{24,8},{1,17},{9,25},{17,1},{25,9},{2,18},{10... | collective-permute-start | bytes 331784 | tf_op jit(solution)/shard_map/ppermute | solution.py:47
  36.9 1.4 %collective-permute-start.14 = (bf16[432,128]{1,0:T(8,128)(2,1)S(1)}, bf16[432,128]{1,0:T(8,128)(2,1)S(1)}, u32[]{:S(2)}, u32[]{:S(2)}) collective-permute-start(bf16[432,128]{1,0:T(8,128)(2,1)S(1)} %shard_map.78.refs_5_.refs_0_), channel_id=1, source_target_pairs={{0,24},{8,16},{16,8},{24,0},{1,25},{9,17},{17,9},{25,1},{2,26},{10... | collective-permute-start | bytes 331784 | tf_op jit(solution)/shard_map/ppermute | solution.py:47
  38.3 2.8 %shard_map.79 = bf16[512,256]{1,0:T(8,128)(2,1)} custom-call(s32[1]{0:T(128)S(6)} %copy.15.refs_0_, bf16[512,256]{1,0:T(8,128)(2,1)S(1)} %get-tuple-element.25.refs_1_, bf16[512,256]{1,0:T(8,128)(2,1)S(1)} %bitcast.8, bf16[512,256]{1,0:T(8,128)(2,1)S(1)} %collective-permute-done.7.refs_3_, bf16[9,768,256]{2,1,0:T(8,128)(2,1)S(1)} %get-tuple-element.41.refs_4_, ...), custom_call_target="tpu_custom_call" | custom-call | flops 1811939328 | bytes 4325380 | tf_op jit(solution)/shard_map/pallas_call | solution.py:28
  41.1 1.4 %collective-permute-done.14.refs_3_ = bf16[432,128]{1,0:T(8,128)(2,1)S(1)} collective-permute-done((bf16[432,128]{1,0:T(8,128)(2,1)S(1)}, bf16[432,128]{1,0:T(8,128)(2,1)S(1)}, u32[]{:S(2)}, u32[]{:S(2)}) %collective-permute-start.14) | collective-permute-done | bytes 110624 | tf_op jit(solution)/shard_map/ppermute | solution.py:47
  42.5 1.1 %shard_map.80 = f32[27,32,256]{2,1,0:T(8,128)} custom-call(bf16[432,128]{1,0:T(8,128)(2,1)S(1)} %shard_map.78.refs_5_.refs_0_, bf16[432,128]{1,0:T(8,128)(2,1)S(1)} %collective-permute-done.12.refs_1_, bf16[432,128]{1,0:T(8,128)(2,1)S(1)} %collective-permute-done.13.refs_2_, bf16[432,128]{1,0:T(8,128)(2,1)S(1)} %collective-permute-done.14.refs_3_), custom_call_target="tpu_custom_call" | custom-call | bytes 442368 | tf_op jit(solution)/shard_map/pallas_call | solution.py:28
  (16 shorter events, 0.1 us)
Async XLA Ops:
  0.6 10.3 %collective-permute-start = (bf16[512,256]{1,0:T(8,128)(2,1)}, bf16[512,256]{1,0:T(8,128)(2,1)S(1)}, u32[]{:S(2)}, u32[]{:S(2)}) collective-permute-start(bf16[512,256]{1,0:T(8,128)(2,1)} %bitcast.11), channel_id=1, source_target_pairs={{0,8},{1,17},{2,10},{3,19},{4,12},{5,21},{6,14},{7,23},{8,0},{9,25... | collective-permute-start | bytes 786440 | tf_op jit(solution)/shard_map/ppermute | solution.py:61
  3.7 9.5 %collective-permute-start.1 = (bf16[512,256]{1,0:T(8,128)(2,1)}, bf16[512,256]{1,0:T(8,128)(2,1)S(1)}, u32[]{:S(2)}, u32[]{:S(2)}) collective-permute-start(bf16[512,256]{1,0:T(8,128)(2,1)} %bitcast.12), channel_id=1, source_target_pairs={{0,16},{1,9},{2,18},{3,11},{4,20},{5,13},{6,22},{7,15},{8,24},{9,1... | collective-permute-start | bytes 786440 | tf_op jit(solution)/shard_map/ppermute | solution.py:61
  6.4 8.4 %collective-permute-start.6 = (bf16[256,128]{1,0:T(8,128)(2,1)S(1)}, bf16[256,128]{1,0:T(8,128)(2,1)S(1)}, u32[]{:S(2)}, u32[]{:S(2)}) collective-permute-start(bf16[256,128]{1,0:T(8,128)(2,1)S(1)} %get-tuple-element.28), channel_id=1, source_target_pairs={{0,8},{1,17},{2,10},{3,19},{4,12},{5,21},{6,14},{7,23},{8,0},{9,25... | collective-permute-start | bytes 196616 | tf_op jit(solution)/shard_map/ppermute | solution.py:61
  7.0 8.2 %collective-permute-start.4 = (bf16[256,128]{1,0:T(8,128)(2,1)S(1)}, bf16[256,128]{1,0:T(8,128)(2,1)S(1)}, u32[]{:S(2)}, u32[]{:S(2)}) collective-permute-start(bf16[256,128]{1,0:T(8,128)(2,1)S(1)} %get-tuple-element.26), channel_id=1, source_target_pairs={{0,16},{1,9},{2,18},{3,11},{4,20},{5,13},{6,22},{7,15},{8,24},{9,1... | collective-permute-start | bytes 196616 | tf_op jit(solution)/shard_map/ppermute | solution.py:61
  7.0 8.3 %collective-permute-start.5 = (bf16[256,128]{1,0:T(8,128)(2,1)S(1)}, bf16[256,128]{1,0:T(8,128)(2,1)S(1)}, u32[]{:S(2)}, u32[]{:S(2)}) collective-permute-start(bf16[256,128]{1,0:T(8,128)(2,1)S(1)} %get-tuple-element.27), channel_id=1, source_target_pairs={{0,24},{8,16},{16,8},{24,0},{1,25},{9,17},{17,9},{25,1},{2,26},{10... | collective-permute-start | bytes 196616 | tf_op jit(solution)/shard_map/ppermute | solution.py:47
  10.9 6.8 %collective-permute-start.2 = (bf16[256,256]{1,0:T(8,128)(2,1)S(1)}, bf16[256,256]{1,0:T(8,128)(2,1)S(1)}, u32[]{:S(2)}, u32[]{:S(2)}) collective-permute-start(bf16[256,256]{1,0:T(8,128)(2,1)S(1)} %shard_map.68), channel_id=1, source_target_pairs={{0,16},{1,9},{2,18},{3,11},{4,20},{5,13},{6,22},{7,15},{8,24},{9,1... | collective-permute-start | bytes 393224 | tf_op jit(solution)/shard_map/ppermute | solution.py:61
  13.2 5.0 %collective-permute-start.3 = (bf16[256,256]{1,0:T(8,128)(2,1)S(1)}, bf16[256,256]{1,0:T(8,128)(2,1)S(1)}, u32[]{:S(2)}, u32[]{:S(2)}) collective-permute-start(bf16[256,256]{1,0:T(8,128)(2,1)S(1)} %shard_map.69), channel_id=1, source_target_pairs={{0,8},{1,17},{2,10},{3,19},{4,12},{5,21},{6,14},{7,23},{8,0},{9,25... | collective-permute-start | bytes 393224 | tf_op jit(solution)/shard_map/ppermute | solution.py:61
  17.7 1.1 %copy-start = (bf16[1,2,16,16,256]{4,3,2,1,0:T(8,128)(2,1)S(1)}, bf16[1,2,16,16,256]{4,3,2,1,0:T(8,128)(2,1)}, u32[]{:S(2)}) copy-start(bf16[1,2,16,16,256]{4,3,2,1,0:T(8,128)(2,1)} %param.5) | copy-start | bytes 786436
  18.8 1.9 %collective-permute-start.8 = (bf16[4,432,128]{2,1,0:T(8,128)(2,1)S(1)}, bf16[4,432,128]{2,1,0:T(8,128)(2,1)S(1)}, u32[]{:S(2)}, u32[]{:S(2)}) collective-permute-start(bf16[4,432,128]{2,1,0:T(8,128)(2,1)S(1)} %get-tuple-element.39.refs_5_), channel_id=1, source_target_pairs={{0,1},{1,0},{2,3},{3,2},{4,5},{5,4},{6,7},{7,6},{8,9},{9,8},{10,11... | collective-permute-start | bytes 1327112 | tf_op jit(solution)/shard_map/ppermute | solution.py:47
  18.9 19.4 %collective-permute-start.7 = (bf16[512,256]{1,0:T(8,128)(2,1)S(1)}, bf16[512,256]{1,0:T(8,128)(2,1)S(1)}, u32[]{:S(2)}, u32[]{:S(2)}) collective-permute-start(bf16[512,256]{1,0:T(8,128)(2,1)S(1)} %bitcast.7), channel_id=1, source_target_pairs={{8,0},{16,8},{24,16},{9,1},{17,9},{25,17},{10,2},{18,10},{26,18},{... | collective-permute-start | bytes 786440 | tf_op jit(solution)/shard_map/ppermute | solution.py:442
  20.2 4.9 %copy-start.1 = (bf16[3,3,3,256,256]{4,3,2,1,0:T(8,128)(2,1)S(1)}, bf16[3,3,3,256,256]{4,3,2,1,0:T(8,128)(2,1)}, u32[]{:S(2)}) copy-start(bf16[3,3,3,256,256]{4,3,2,1,0:T(8,128)(2,1)} %param.6) | copy-start | bytes 10616836
  20.9 11.7 %collective-permute-start.10 = (bf16[1,432,128]{2,1,0:T(8,128)(2,1)S(1)}, bf16[1,432,128]{2,1,0:T(8,128)(2,1)S(1)}, u32[]{:S(2)}, u32[]{:S(2)}) collective-permute-start(bf16[1,432,128]{2,1,0:T(8,128)(2,1)S(1)} %get-tuple-element.44), channel_id=1, source_target_pairs={{0,4},{1,5},{2,6},{3,7},{4,0},{5,1},{6,2},{7,3},{8,12},{9,13},{10,... | collective-permute-start | bytes 331784 | tf_op jit(solution)/shard_map/ppermute | solution.py:47
  23.5 9.0 %collective-permute-start.11 = (bf16[1,432,128]{2,1,0:T(8,128)(2,1)S(1)}, bf16[1,432,128]{2,1,0:T(8,128)(2,1)S(1)}, u32[]{:S(2)}, u32[]{:S(2)}) collective-permute-start(bf16[1,432,128]{2,1,0:T(8,128)(2,1)S(1)} %get-tuple-element.45), channel_id=1, source_target_pairs={{0,6},{1,7},{2,4},{3,5},{4,2},{5,3},{6,0},{7,1},{8,14},{9,15},{10,... | collective-permute-start | bytes 331784 | tf_op jit(solution)/shard_map/ppermute | solution.py:47
  24.9 8.5 %collective-permute-start.9 = (bf16[1,432,128]{2,1,0:T(8,128)(2,1)S(1)}, bf16[1,432,128]{2,1,0:T(8,128)(2,1)S(1)}, u32[]{:S(2)}, u32[]{:S(2)}) collective-permute-start(bf16[1,432,128]{2,1,0:T(8,128)(2,1)S(1)} %get-tuple-element.43), channel_id=1, source_target_pairs={{0,2},{1,3},{2,0},{3,1},{4,6},{5,7},{6,4},{7,5},{8,10},{9,11},{10,... | collective-permute-start | bytes 331784 | tf_op jit(solution)/shard_map/ppermute | solution.py:47
  33.5 7.7 %collective-permute-start.12 = (bf16[432,128]{1,0:T(8,128)(2,1)S(1)}, bf16[432,128]{1,0:T(8,128)(2,1)S(1)}, u32[]{:S(2)}, u32[]{:S(2)}) collective-permute-start(bf16[432,128]{1,0:T(8,128)(2,1)S(1)} %shard_map.78.refs_5_.refs_0_), channel_id=1, source_target_pairs={{0,8},{8,0},{16,24},{24,16},{1,9},{9,1},{17,25},{25,17},{2,10},{10... | collective-permute-start | bytes 331784 | tf_op jit(solution)/shard_map/ppermute | solution.py:47
  35.9 5.2 %collective-permute-start.13 = (bf16[432,128]{1,0:T(8,128)(2,1)S(1)}, bf16[432,128]{1,0:T(8,128)(2,1)S(1)}, u32[]{:S(2)}, u32[]{:S(2)}) collective-permute-start(bf16[432,128]{1,0:T(8,128)(2,1)S(1)} %shard_map.78.refs_5_.refs_0_), channel_id=1, source_target_pairs={{0,16},{8,24},{16,0},{24,8},{1,17},{9,25},{17,1},{25,9},{2,18},{10... | collective-permute-start | bytes 331784 | tf_op jit(solution)/shard_map/ppermute | solution.py:47
  36.9 5.6 %collective-permute-start.14 = (bf16[432,128]{1,0:T(8,128)(2,1)S(1)}, bf16[432,128]{1,0:T(8,128)(2,1)S(1)}, u32[]{:S(2)}, u32[]{:S(2)}) collective-permute-start(bf16[432,128]{1,0:T(8,128)(2,1)S(1)} %shard_map.78.refs_5_.refs_0_), channel_id=1, source_target_pairs={{0,24},{8,16},{16,8},{24,0},{1,25},{9,17},{17,9},{25,1},{2,26},{10... | collective-permute-start | bytes 331784 | tf_op jit(solution)/shard_map/ppermute | solution.py:47

commit v5 on v4

--- a/solution.py
+++ b/solution.py
@@ -253,15 +253,10 @@
             put_tile(out_ref, part, at, value.astype(out_ref.dtype))
 
 
-def first_rows_body(first, turned):
-    rows = first.shape[0]
-    turned[:, :rows] = jax.nn.silu(first[...].astype(F32)).astype(BF16).T
-
-
-def send_body(count, area, grads, second, held, *refs):
+def send_body(count, area, grads, first, second, *refs):
     products, (send_ref, turned) = refs[:3], refs[3:]
-    rows = second.shape[0]
-    turned[:, 2 * area - rows :] = jax.nn.silu(second[...].astype(F32)).astype(BF16).T
+    values = jnp.concatenate([first[...], second[...]], axis=0).astype(F32)
+    turned[...] = jax.nn.silu(values).astype(BF16).T
     other = 1 - lax.axis_index("dp") % 2
     core_sums(count, area, other, grads, turned, products, send_ref)
 
@@ -271,17 +266,18 @@
 
 
 def sum_body(arrived, radix, step, *refs):
-    terms, out_refs = refs[: 1 + arrived], refs[1 + arrived :]
-
-    def total(part):
-        return sum((ref[part].astype(F32) for ref in terms[1:]), terms[0][part])
-
+    keep_ref, in_refs = refs[0], refs[1 : 1 + arrived]
+    total = keep_ref[...]
+    for ref in in_refs:
+        total = total + ref[...].astype(F32)
     if radix == 1:
-        out_refs[0][...] = total(0).astype(BF16)
+        refs[1 + arrived][...] = total[0].astype(BF16)
         return
+    out_refs, held = refs[1 + arrived : -1], refs[-1]
+    held[...] = total
     digit = (lax.axis_index("dp") // 2) // step % radix
     for mask, out in enumerate(out_refs):
-        out[...] = total(pl.ds((digit ^ mask) * step, step)).astype(out.dtype)
+        out[...] = held[pl.ds((digit ^ mask) * step, step)].astype(out.dtype)
 
 
 def sum_over_clips(keep, send, after):
@@ -301,7 +297,10 @@
         outs = [pltpu.VMEM((step, count, lanes), F32)]
         outs += [pltpu.VMEM((step, count, lanes), BF16)] * (radix - 1)
         keep, *sends = call(
-            functools.partial(sum_body, len(arrived), radix, step), outs, (keep, *arrived)
+            functools.partial(sum_body, len(arrived), radix, step),
+            outs,
+            (keep, *arrived),
+            scratch=[pltpu.VMEM((parts, count, lanes), F32)],
         )
         arrived = swaps(sends, "dp", 2 * step)
 
@@ -432,7 +431,7 @@
     slices[1] = cross(slices[1], True)
     slices[2] = cross(slices[2], False)
     slices[3] = swap(slices[3], "tm", 3)
-    split = area
+    split = area + area // 8
     relayed = [
         call(functools.partial(cut_body, start), [pltpu.VMEM((size, channels), BF16)], (near,))[0]
         for start, size, near in ((0, split, near_a), (split, 2 * area - split, near_b))
@@ -461,13 +460,10 @@
         flops=2 * 27 * 2 * peers * area * channels * LANES // 2,
     )
     half = 27 * 2 * area * channels * LANES // 2
-    last = pltpu.VMEM((channels, 2 * area), BF16)
-    (last_turned,) = call(first_rows_body, [last], (first,))
     send, last_turned = call(
         functools.partial(send_body, count, area),
-        [pltpu.VMEM(sums_shape(parts, count), BF16), last],
-        (grads, second, last_turned, *products),
-        aliases={2: 1},
+        [pltpu.VMEM(sums_shape(parts, count), BF16), pltpu.VMEM((channels, 2 * area), BF16)],
+        (grads, first, second, *products),
         flops=half,
     )
     (keep,) = call(

time: 44.4 us -> 44.3 us (level)
    pallas_call x14 -> x13, Pallas kernels: 12.5 us -> 12.4 us  [call(): pl.pallas_call(with_after, out_shape=tuple(outs), in_specs=[pl.BlockSpec(...]
where the time goes in v5:
time: 44.3 us; the launch traced here: 43.5 us
  starting transfers between devices  22.3 us (50%)
  Pallas kernels  12.4 us (28%)
  waiting for transfers between devices  7.37 us (17%)
  between operations  1.4 us (3%)
    pallas_call x13, Pallas kernels, call(): pl.pallas_call(with_after, out_shape=tuple(outs), in_specs=[pl.BlockSpec(...  12.4 us
    ppermute x8, starting transfers between devices, swap(): return lax.ppermute(value, axis, [(s, s ^ mask) for s in range(count)])  12 us
    ppermute x6, starting transfers between devices, cross(): return lax.ppermute(value, ('tm', 'dp'), pairs)  9 us
    ppermute x8, waiting for transfers between devices, swap(): return lax.ppermute(value, axis, [(s, s ^ mask) for s in range(count)])  7.06 us
    ppermute x1, starting transfers between devices, local(): later = lax.ppermute(cot, 'tm', [(s, s - 1) for s in range(1, peers)])  1.29 us
  transfers between devices with their start and end apart: 15, of which 5 were waited for; matrix products, arithmetic and copies ran while one was open for 0% of the time, Pallas kernels for 25%

profile of v5, /device:TPU:0, one launch (start us, length us, event | category | flops | bytes accessed | tf_op | source)
XLA Modules:
  0.0 43.5 jit_solution(3495391093034114336)
XLA Ops:
  0.6 3.0 %collective-permute-start = (bf16[512,256]{1,0:T(8,128)(2,1)}, bf16[512,256]{1,0:T(8,128)(2,1)S(1)}, u32[]{:S(2)}, u32[]{:S(2)}) collective-permute-start(bf16[512,256]{1,0:T(8,128)(2,1)} %bitcast.11), channel_id=1, source_target_pairs={{0,8},{1,17},{2,10},{3,19},{4,12},{5,21},{6,14},{7,23},{8,0},{9,25... | collective-permute-start | bytes 786440 | tf_op jit(solution)/shard_map/ppermute | solution.py:61
  3.7 1.5 %collective-permute-start.1 = (bf16[512,256]{1,0:T(8,128)(2,1)}, bf16[512,256]{1,0:T(8,128)(2,1)S(1)}, u32[]{:S(2)}, u32[]{:S(2)}) collective-permute-start(bf16[512,256]{1,0:T(8,128)(2,1)} %bitcast.12), channel_id=1, source_target_pairs={{0,16},{1,9},{2,18},{3,11},{4,20},{5,13},{6,22},{7,15},{8,24},{9,1... | collective-permute-start | bytes 786440 | tf_op jit(solution)/shard_map/ppermute | solution.py:61
  5.2 1.2 %shard_map.67 = (bf16[256,128]{1,0:T(8,128)(2,1)S(1)}, bf16[256,128]{1,0:T(8,128)(2,1)S(1)}, bf16[256,128]{1,0:T(8,128)(2,1)S(1)}, bf16[256,128]{1,0:T(8,128)(2,1)S(1)}, bf16[512,256]{1,0:T(8,128)(2,1)S(1)}) custom-call(bf16[512,256]{1,0:T(8,128)(2,1)} %bitcast.6, bf16[512,256]{1,0:T(8,128)(2,1)} %bitcast.13), custom_call_target="tpu_custom_call" | custom-call | bytes 524288 | tf_op jit(solution)/shard_map/pallas_call | solution.py:28
  6.4 0.6 %collective-permute-start.6 = (bf16[256,128]{1,0:T(8,128)(2,1)S(1)}, bf16[256,128]{1,0:T(8,128)(2,1)S(1)}, u32[]{:S(2)}, u32[]{:S(2)}) collective-permute-start(bf16[256,128]{1,0:T(8,128)(2,1)S(1)} %get-tuple-element.28), channel_id=1, source_target_pairs={{0,8},{1,17},{2,10},{3,19},{4,12},{5,21},{6,14},{7,23},{8,0},{9,25... | collective-permute-start | bytes 196616 | tf_op jit(solution)/shard_map/ppermute | solution.py:61
  7.0 0.1 collective-permute-start.4
  7.0 2.9 %collective-permute-start.5 = (bf16[256,128]{1,0:T(8,128)(2,1)S(1)}, bf16[256,128]{1,0:T(8,128)(2,1)S(1)}, u32[]{:S(2)}, u32[]{:S(2)}) collective-permute-start(bf16[256,128]{1,0:T(8,128)(2,1)S(1)} %get-tuple-element.27), channel_id=1, source_target_pairs={{0,24},{8,16},{16,8},{24,0},{1,25},{9,17},{17,9},{25,1},{2,26},{10... | collective-permute-start | bytes 196616 | tf_op jit(solution)/shard_map/ppermute | solution.py:47
  10.6 0.3 shard_map.70
  10.9 2.2 %collective-permute-start.2 = (bf16[288,256]{1,0:T(8,128)(2,1)S(1)}, bf16[288,256]{1,0:T(8,128)(2,1)S(1)}, u32[]{:S(2)}, u32[]{:S(2)}) collective-permute-start(bf16[288,256]{1,0:T(8,128)(2,1)S(1)} %shard_map.68), channel_id=1, source_target_pairs={{0,16},{1,9},{2,18},{3,11},{4,20},{5,13},{6,22},{7,15},{8,24},{9,1... | collective-permute-start | bytes 442376 | tf_op jit(solution)/shard_map/ppermute | solution.py:61
  13.2 1.6 %collective-permute-start.3 = (bf16[224,256]{1,0:T(8,128)(2,1)S(1)}, bf16[224,256]{1,0:T(8,128)(2,1)S(1)}, u32[]{:S(2)}, u32[]{:S(2)}) collective-permute-start(bf16[224,256]{1,0:T(8,128)(2,1)S(1)} %shard_map.69), channel_id=1, source_target_pairs={{0,8},{1,17},{2,10},{3,19},{4,12},{5,21},{6,14},{7,23},{8,0},{9,25... | collective-permute-start | bytes 344072 | tf_op jit(solution)/shard_map/ppermute | solution.py:61
  14.7 0.4 shard_map.71
  15.2 0.2 collective-permute-done.5.refs_2_
  15.3 2.4 %shard_map.72 = (bf16[2560,640]{1,0:T(8,128)(2,1)S(1)}, f32[256,640]{1,0:T(8,128)S(1)}, f32[256,640]{1,0:T(8,128)S(1)}, f32[256,640]{1,0:T(8,128)S(1)}) custom-call(s32[1]{0:T(128)S(6)} %copy.13.refs_0_, bf16[256,128]{1,0:T(8,128)(2,1)S(1)} %collective-permute-done.4.refs_1_, ...), custom_call_target="tpu_custom_call", output_to_operand_aliasing={{0}: (4, {})} | custom-call | flops 1811939328 | bytes 4194308 | tf_op jit(solution)/shard_map/pallas_call | solution.py:28
  17.7 0.0 copy-start
  17.7 0.3 collective-permute-done.3.refs_2_.refs_5_
  18.0 0.6 %shard_map.73 = (bf16[4,432,128]{2,1,0:T(8,128)(2,1)S(1)}, bf16[256,512]{1,0:T(8,128)(2,1)S(1)}) custom-call(bf16[2560,640]{1,0:T(8,128)(2,1)S(1)} %get-tuple-element.34.refs_0_, bf16[288,256]{1,0:T(8,128)(2,1)S(1)} %collective-permute-done.2.refs_1_.refs_4_, bf16[224,256]{1,0:T(8,128)(2,1)S(1)} %collective-permute-done.3.refs_2_.refs_5_, ...), custom_call_target="tpu_custom_call" | custom-call | flops 226492416 | bytes 5505024 | tf_op jit(solution)/shard_map/pallas_call | solution.py:28
  18.7 0.0 collective-permute-start.8
  18.7 1.3 %collective-permute-start.7 = (bf16[512,256]{1,0:T(8,128)(2,1)S(1)}, bf16[512,256]{1,0:T(8,128)(2,1)S(1)}, u32[]{:S(2)}, u32[]{:S(2)}) collective-permute-start(bf16[512,256]{1,0:T(8,128)(2,1)S(1)} %bitcast.7), channel_id=1, source_target_pairs={{8,0},{16,8},{24,16},{9,1},{17,9},{25,17},{10,2},{18,10},{26,18},{... | collective-permute-start | bytes 786440 | tf_op jit(solution)/shard_map/ppermute | solution.py:441
  20.0 0.6 %shard_map.74.refs_7_.refs_0_ = f32[4,432,128]{2,1,0:T(8,128)S(1)} custom-call(bf16[2560,640]{1,0:T(8,128)(2,1)S(1)} %get-tuple-element.34.refs_0_, bf16[256,512]{1,0:T(8,128)(2,1)S(1)} %get-tuple-element.38.refs_1_, f32[256,640]{1,0:T(8,128)S(1)} %get-tuple-element.35.refs_3_.refs_2_, f32[256,640]{1,0:T(8,128)S(1)} %get-tuple-element.36.refs_4_.refs_3_, ...), custom_call_target="tpu_custom_call" | custom-call | flops 226492416 | bytes 5505024 | tf_op jit(solution)/shard_map/pallas_call | solution.py:28
  20.6 0.1 shard_map.76
  20.7 2.7 %collective-permute-start.10 = (bf16[1,432,128]{2,1,0:T(8,128)(2,1)S(1)}, bf16[1,432,128]{2,1,0:T(8,128)(2,1)S(1)}, u32[]{:S(2)}, u32[]{:S(2)}) collective-permute-start(bf16[1,432,128]{2,1,0:T(8,128)(2,1)S(1)} %get-tuple-element.44), channel_id=1, source_target_pairs={{0,4},{1,5},{2,6},{3,7},{4,0},{5,1},{6,2},{7,3},{8,12},{9,13},{10,... | collective-permute-start | bytes 331784 | tf_op jit(solution)/shard_map/ppermute | solution.py:47
  23.4 1.3 %collective-permute-start.11 = (bf16[1,432,128]{2,1,0:T(8,128)(2,1)S(1)}, bf16[1,432,128]{2,1,0:T(8,128)(2,1)S(1)}, u32[]{:S(2)}, u32[]{:S(2)}) collective-permute-start(bf16[1,432,128]{2,1,0:T(8,128)(2,1)S(1)} %get-tuple-element.45), channel_id=1, source_target_pairs={{0,6},{1,7},{2,4},{3,5},{4,2},{5,3},{6,0},{7,1},{8,14},{9,15},{10,... | collective-permute-start | bytes 331784 | tf_op jit(solution)/shard_map/ppermute | solution.py:47
  24.7 0.2 collective-permute-start.9
  25.0 2.8 %shard_map.75 = (bf16[512,256]{1,0:T(8,128)(2,1)}, f32[8,128]{1,0:T(8,128)S(1)}, bf16[9,768,256]{2,1,0:T(8,128)(2,1)S(1)}) custom-call(s32[1]{0:T(128)S(6)} %copy.13.refs_0_, bf16[512,256]{1,0:T(8,128)(2,1)S(1)} %get-tuple-element.25.refs_1_, bf16[512,256]{1,0:T(8,128)(2,1)S(1)} %collective-permute-done.refs_0_.refs_2_, ...), custom_call_target="tpu_custom_call" | custom-call | flops 1811939328 | bytes 4587524 | tf_op jit(solution)/shard_map/pallas_call | solution.py:28
  27.8 4.6 %collective-permute-done.10.refs_2_ = bf16[1,432,128]{2,1,0:T(8,128)(2,1)S(1)} collective-permute-done((bf16[1,432,128]{2,1,0:T(8,128)(2,1)S(1)}, bf16[1,432,128]{2,1,0:T(8,128)(2,1)S(1)}, u32[]{:S(2)}, u32[]{:S(2)}) %collective-permute-start.10) | collective-permute-done | bytes 110624 | tf_op jit(solution)/shard_map/ppermute | solution.py:47
  32.4 0.9 %collective-permute-done.9.refs_1_ = bf16[1,432,128]{2,1,0:T(8,128)(2,1)S(1)} collective-permute-done((bf16[1,432,128]{2,1,0:T(8,128)(2,1)S(1)}, bf16[1,432,128]{2,1,0:T(8,128)(2,1)S(1)}, u32[]{:S(2)}, u32[]{:S(2)}) %collective-permute-start.9) | collective-permute-done | bytes 110624 | tf_op jit(solution)/shard_map/ppermute | solution.py:47
  33.3 0.1 shard_map.77.refs_5_.refs_0_
  33.3 2.4 %collective-permute-start.12 = (bf16[432,128]{1,0:T(8,128)(2,1)S(1)}, bf16[432,128]{1,0:T(8,128)(2,1)S(1)}, u32[]{:S(2)}, u32[]{:S(2)}) collective-permute-start(bf16[432,128]{1,0:T(8,128)(2,1)S(1)} %shard_map.77.refs_5_.refs_0_), channel_id=1, source_target_pairs={{0,8},{8,0},{16,24},{24,16},{1,9},{9,1},{17,25},{25,17},{2,10},{10... | collective-permute-start | bytes 331784 | tf_op jit(solution)/shard_map/ppermute | solution.py:47
  35.7 1.0 %collective-permute-start.13 = (bf16[432,128]{1,0:T(8,128)(2,1)S(1)}, bf16[432,128]{1,0:T(8,128)(2,1)S(1)}, u32[]{:S(2)}, u32[]{:S(2)}) collective-permute-start(bf16[432,128]{1,0:T(8,128)(2,1)S(1)} %shard_map.77.refs_5_.refs_0_), channel_id=1, source_target_pairs={{0,16},{8,24},{16,0},{24,8},{1,17},{9,25},{17,1},{25,9},{2,18},{10... | collective-permute-start | bytes 331784 | tf_op jit(solution)/shard_map/ppermute | solution.py:47
  36.8 1.4 %collective-permute-start.14 = (bf16[432,128]{1,0:T(8,128)(2,1)S(1)}, bf16[432,128]{1,0:T(8,128)(2,1)S(1)}, u32[]{:S(2)}, u32[]{:S(2)}) collective-permute-start(bf16[432,128]{1,0:T(8,128)(2,1)S(1)} %shard_map.77.refs_5_.refs_0_), channel_id=1, source_target_pairs={{0,24},{8,16},{16,8},{24,0},{1,25},{9,17},{17,9},{25,1},{2,26},{10... | collective-permute-start | bytes 331784 | tf_op jit(solution)/shard_map/ppermute | solution.py:47
  38.1 2.8 %shard_map.78 = bf16[512,256]{1,0:T(8,128)(2,1)} custom-call(s32[1]{0:T(128)S(6)} %copy.13.refs_0_, bf16[512,256]{1,0:T(8,128)(2,1)S(1)} %get-tuple-element.25.refs_1_, bf16[512,256]{1,0:T(8,128)(2,1)S(1)} %bitcast.8, bf16[512,256]{1,0:T(8,128)(2,1)S(1)} %collective-permute-done.7.refs_3_, bf16[9,768,256]{2,1,0:T(8,128)(2,1)S(1)} %get-tuple-element.41.refs_4_, ...), custom_call_target="tpu_custom_call" | custom-call | flops 1811939328 | bytes 4325380 | tf_op jit(solution)/shard_map/pallas_call | solution.py:28
  41.0 1.4 %collective-permute-done.14.refs_3_ = bf16[432,128]{1,0:T(8,128)(2,1)S(1)} collective-permute-done((bf16[432,128]{1,0:T(8,128)(2,1)S(1)}, bf16[432,128]{1,0:T(8,128)(2,1)S(1)}, u32[]{:S(2)}, u32[]{:S(2)}) %collective-permute-start.14) | collective-permute-done | bytes 110624 | tf_op jit(solution)/shard_map/ppermute | solution.py:47
  42.4 1.1 %shard_map.79 = f32[27,32,256]{2,1,0:T(8,128)} custom-call(bf16[432,128]{1,0:T(8,128)(2,1)S(1)} %shard_map.77.refs_5_.refs_0_, bf16[432,128]{1,0:T(8,128)(2,1)S(1)} %collective-permute-done.12.refs_1_, bf16[432,128]{1,0:T(8,128)(2,1)S(1)} %collective-permute-done.13.refs_2_, bf16[432,128]{1,0:T(8,128)(2,1)S(1)} %collective-permute-done.14.refs_3_), custom_call_target="tpu_custom_call" | custom-call | bytes 442368 | tf_op jit(solution)/shard_map/pallas_call | solution.py:28
  (15 shorter events, 0.1 us)
Async XLA Ops:
  0.6 10.3 %collective-permute-start = (bf16[512,256]{1,0:T(8,128)(2,1)}, bf16[512,256]{1,0:T(8,128)(2,1)S(1)}, u32[]{:S(2)}, u32[]{:S(2)}) collective-permute-start(bf16[512,256]{1,0:T(8,128)(2,1)} %bitcast.11), channel_id=1, source_target_pairs={{0,8},{1,17},{2,10},{3,19},{4,12},{5,21},{6,14},{7,23},{8,0},{9,25... | collective-permute-start | bytes 786440 | tf_op jit(solution)/shard_map/ppermute | solution.py:61
  3.7 9.5 %collective-permute-start.1 = (bf16[512,256]{1,0:T(8,128)(2,1)}, bf16[512,256]{1,0:T(8,128)(2,1)S(1)}, u32[]{:S(2)}, u32[]{:S(2)}) collective-permute-start(bf16[512,256]{1,0:T(8,128)(2,1)} %bitcast.12), channel_id=1, source_target_pairs={{0,16},{1,9},{2,18},{3,11},{4,20},{5,13},{6,22},{7,15},{8,24},{9,1... | collective-permute-start | bytes 786440 | tf_op jit(solution)/shard_map/ppermute | solution.py:61
  6.4 8.4 %collective-permute-start.6 = (bf16[256,128]{1,0:T(8,128)(2,1)S(1)}, bf16[256,128]{1,0:T(8,128)(2,1)S(1)}, u32[]{:S(2)}, u32[]{:S(2)}) collective-permute-start(bf16[256,128]{1,0:T(8,128)(2,1)S(1)} %get-tuple-element.28), channel_id=1, source_target_pairs={{0,8},{1,17},{2,10},{3,19},{4,12},{5,21},{6,14},{7,23},{8,0},{9,25... | collective-permute-start | bytes 196616 | tf_op jit(solution)/shard_map/ppermute | solution.py:61
  7.0 8.2 %collective-permute-start.4 = (bf16[256,128]{1,0:T(8,128)(2,1)S(1)}, bf16[256,128]{1,0:T(8,128)(2,1)S(1)}, u32[]{:S(2)}, u32[]{:S(2)}) collective-permute-start(bf16[256,128]{1,0:T(8,128)(2,1)S(1)} %get-tuple-element.26), channel_id=1, source_target_pairs={{0,16},{1,9},{2,18},{3,11},{4,20},{5,13},{6,22},{7,15},{8,24},{9,1... | collective-permute-start | bytes 196616 | tf_op jit(solution)/shard_map/ppermute | solution.py:61
  7.0 8.3 %collective-permute-start.5 = (bf16[256,128]{1,0:T(8,128)(2,1)S(1)}, bf16[256,128]{1,0:T(8,128)(2,1)S(1)}, u32[]{:S(2)}, u32[]{:S(2)}) collective-permute-start(bf16[256,128]{1,0:T(8,128)(2,1)S(1)} %get-tuple-element.27), channel_id=1, source_target_pairs={{0,24},{8,16},{16,8},{24,0},{1,25},{9,17},{17,9},{25,1},{2,26},{10... | collective-permute-start | bytes 196616 | tf_op jit(solution)/shard_map/ppermute | solution.py:47
  10.9 7.1 %collective-permute-start.2 = (bf16[288,256]{1,0:T(8,128)(2,1)S(1)}, bf16[288,256]{1,0:T(8,128)(2,1)S(1)}, u32[]{:S(2)}, u32[]{:S(2)}) collective-permute-start(bf16[288,256]{1,0:T(8,128)(2,1)S(1)} %shard_map.68), channel_id=1, source_target_pairs={{0,16},{1,9},{2,18},{3,11},{4,20},{5,13},{6,22},{7,15},{8,24},{9,1... | collective-permute-start | bytes 442376 | tf_op jit(solution)/shard_map/ppermute | solution.py:61
  13.2 4.9 %collective-permute-start.3 = (bf16[224,256]{1,0:T(8,128)(2,1)S(1)}, bf16[224,256]{1,0:T(8,128)(2,1)S(1)}, u32[]{:S(2)}, u32[]{:S(2)}) collective-permute-start(bf16[224,256]{1,0:T(8,128)(2,1)S(1)} %shard_map.69), channel_id=1, source_target_pairs={{0,8},{1,17},{2,10},{3,19},{4,12},{5,21},{6,14},{7,23},{8,0},{9,25... | collective-permute-start | bytes 344072 | tf_op jit(solution)/shard_map/ppermute | solution.py:61
  17.7 1.0 %copy-start = (bf16[1,2,16,16,256]{4,3,2,1,0:T(8,128)(2,1)S(1)}, bf16[1,2,16,16,256]{4,3,2,1,0:T(8,128)(2,1)}, u32[]{:S(2)}) copy-start(bf16[1,2,16,16,256]{4,3,2,1,0:T(8,128)(2,1)} %param.5) | copy-start | bytes 786436
  18.7 1.9 %collective-permute-start.8 = (bf16[4,432,128]{2,1,0:T(8,128)(2,1)S(1)}, bf16[4,432,128]{2,1,0:T(8,128)(2,1)S(1)}, u32[]{:S(2)}, u32[]{:S(2)}) collective-permute-start(bf16[4,432,128]{2,1,0:T(8,128)(2,1)S(1)} %get-tuple-element.39.refs_5_), channel_id=1, source_target_pairs={{0,1},{1,0},{2,3},{3,2},{4,5},{5,4},{6,7},{7,6},{8,9},{9,8},{10,11... | collective-permute-start | bytes 1327112 | tf_op jit(solution)/shard_map/ppermute | solution.py:47
  18.7 19.4 %collective-permute-start.7 = (bf16[512,256]{1,0:T(8,128)(2,1)S(1)}, bf16[512,256]{1,0:T(8,128)(2,1)S(1)}, u32[]{:S(2)}, u32[]{:S(2)}) collective-permute-start(bf16[512,256]{1,0:T(8,128)(2,1)S(1)} %bitcast.7), channel_id=1, source_target_pairs={{8,0},{16,8},{24,16},{9,1},{17,9},{25,17},{10,2},{18,10},{26,18},{... | collective-permute-start | bytes 786440 | tf_op jit(solution)/shard_map/ppermute | solution.py:441
  20.0 5.0 %copy-start.1 = (bf16[3,3,3,256,256]{4,3,2,1,0:T(8,128)(2,1)S(1)}, bf16[3,3,3,256,256]{4,3,2,1,0:T(8,128)(2,1)}, u32[]{:S(2)}) copy-start(bf16[3,3,3,256,256]{4,3,2,1,0:T(8,128)(2,1)} %param.6) | copy-start | bytes 10616836
  20.7 11.7 %collective-permute-start.10 = (bf16[1,432,128]{2,1,0:T(8,128)(2,1)S(1)}, bf16[1,432,128]{2,1,0:T(8,128)(2,1)S(1)}, u32[]{:S(2)}, u32[]{:S(2)}) collective-permute-start(bf16[1,432,128]{2,1,0:T(8,128)(2,1)S(1)} %get-tuple-element.44), channel_id=1, source_target_pairs={{0,4},{1,5},{2,6},{3,7},{4,0},{5,1},{6,2},{7,3},{8,12},{9,13},{10,... | collective-permute-start | bytes 331784 | tf_op jit(solution)/shard_map/ppermute | solution.py:47
  23.4 9.0 %collective-permute-start.11 = (bf16[1,432,128]{2,1,0:T(8,128)(2,1)S(1)}, bf16[1,432,128]{2,1,0:T(8,128)(2,1)S(1)}, u32[]{:S(2)}, u32[]{:S(2)}) collective-permute-start(bf16[1,432,128]{2,1,0:T(8,128)(2,1)S(1)} %get-tuple-element.45), channel_id=1, source_target_pairs={{0,6},{1,7},{2,4},{3,5},{4,2},{5,3},{6,0},{7,1},{8,14},{9,15},{10,... | collective-permute-start | bytes 331784 | tf_op jit(solution)/shard_map/ppermute | solution.py:47
  24.7 8.5 %collective-permute-start.9 = (bf16[1,432,128]{2,1,0:T(8,128)(2,1)S(1)}, bf16[1,432,128]{2,1,0:T(8,128)(2,1)S(1)}, u32[]{:S(2)}, u32[]{:S(2)}) collective-permute-start(bf16[1,432,128]{2,1,0:T(8,128)(2,1)S(1)} %get-tuple-element.43), channel_id=1, source_target_pairs={{0,2},{1,3},{2,0},{3,1},{4,6},{5,7},{6,4},{7,5},{8,10},{9,11},{10,... | collective-permute-start | bytes 331784 | tf_op jit(solution)/shard_map/ppermute | solution.py:47
  33.3 7.7 %collective-permute-start.12 = (bf16[432,128]{1,0:T(8,128)(2,1)S(1)}, bf16[432,128]{1,0:T(8,128)(2,1)S(1)}, u32[]{:S(2)}, u32[]{:S(2)}) collective-permute-start(bf16[432,128]{1,0:T(8,128)(2,1)S(1)} %shard_map.77.refs_5_.refs_0_), channel_id=1, source_target_pairs={{0,8},{8,0},{16,24},{24,16},{1,9},{9,1},{17,25},{25,17},{2,10},{10... | collective-permute-start | bytes 331784 | tf_op jit(solution)/shard_map/ppermute | solution.py:47
  35.7 5.2 %collective-permute-start.13 = (bf16[432,128]{1,0:T(8,128)(2,1)S(1)}, bf16[432,128]{1,0:T(8,128)(2,1)S(1)}, u32[]{:S(2)}, u32[]{:S(2)}) collective-permute-start(bf16[432,128]{1,0:T(8,128)(2,1)S(1)} %shard_map.77.refs_5_.refs_0_), channel_id=1, source_target_pairs={{0,16},{8,24},{16,0},{24,8},{1,17},{9,25},{17,1},{25,9},{2,18},{10... | collective-permute-start | bytes 331784 | tf_op jit(solution)/shard_map/ppermute | solution.py:47
  36.8 5.6 %collective-permute-start.14 = (bf16[432,128]{1,0:T(8,128)(2,1)S(1)}, bf16[432,128]{1,0:T(8,128)(2,1)S(1)}, u32[]{:S(2)}, u32[]{:S(2)}) collective-permute-start(bf16[432,128]{1,0:T(8,128)(2,1)S(1)} %shard_map.77.refs_5_.refs_0_), channel_id=1, source_target_pairs={{0,24},{8,16},{16,8},{24,0},{1,25},{9,17},{17,9},{25,1},{2,26},{10... | collective-permute-start | bytes 331784 | tf_op jit(solution)/shard_map/ppermute | solution.py:47
